TPU v7x, 512 devices: a whole 4x4x16 slice. The times are simulated.
512 devices in a mesh: row: 16 (over y, z_hi), col: 32 (over z_lo, x, core).
Axes of the slice: x: 4, y: 4, z: 16 (z_hi: 4, z_lo: 4; z = z_hi * 4 + z_lo), core: 2. Of those that a mesh axis runs over, the one named last changes fastest.
Arguments:
- object_field: float32 [2, 6144, 8192], P(None, 'row', 'col'), may hold values from -5 to 5
- probe_modes: float32 [2, 2, 256, 256], replicated, may hold values from -4 to 4
- scan_positions: int32 [16, 32, 2, 2], P('row', 'col'), may hold values from 0 to 256, as said below
- amplitudes: bfloat16 [16, 32, 2, 256, 256], P('row', 'col'), may hold values from 0.5 to 1.5
Outputs:
- object_out: float32 [2, 6144, 8192], P(None, 'row', 'col')
- probe_out: float32 [2, 2, 256, 256], replicated
Inputs may be any that keep to these rules, and one draw needn't show every extreme that they name: `scan_positions`: in even batches the row offset is at most 128; in odd batches it is at least 192. The column offset lies in 32 to 128 in every batch. Every window lies inside its tile extended by 128 rows below and 128 columns to the right.
All inputs are finite; a program needn't handle non-finite values.
Results may differ from a plain program's by a relative error of at most 0.0003.
Values sent between devices are 32-bit elements; how exact they have to be, the bound alone decides.
No kernel may reach another device: no remote copies, remote signals or barrier semaphores. Data moves between devices by JAX's collectives and lax.ppermute only.
A program may use at most 64 MiB of HBM per device.

v0:
```python
import math

import jax
import jax.numpy as jnp
import numpy as np
from jax import lax
from jax.experimental import pallas as pl
from jax.experimental.pallas import tpu as pltpu
from jax.sharding import Mesh
from jax.sharding import PartitionSpec as P


HALO = 128
BATCHES = 2
WIN = 256
HALF = 128
INTERPRET = False
ROW = ("row_0", "row_1")
COL = ("col_0", "col_1", "col_2")
PLANE = ("row_0", "col_1")
DEPTH = ("row_1", "col_0")
CORE = "col_2"


def halves(x):
    high = x.astype(jnp.bfloat16)
    low = (x - high.astype(np.float64)).astype(jnp.bfloat16)
    return high, low


def dft_constants():
    index = np.arange(HALF)
    angle = 2.0 * np.pi * (np.outer(index, index) % HALF) / HALF
    cosine = np.cos(angle) / 16.0
    sine = -np.sin(angle) / 16.0
    forward = np.block([[cosine, -sine], [sine, cosine]])
    high, low = halves(forward)
    left = np.concatenate([high, high, low], axis=1)
    left_t = np.concatenate([high.T, high.T, low.T], axis=1)
    right = np.concatenate([high, high, low], axis=0)
    right_t = np.concatenate([high.T, high.T, low.T], axis=0)
    turn = 2.0 * np.pi * index / WIN
    twiddle = np.stack([np.cos(turn), -np.sin(turn)]).astype(np.float32)
    rows = np.ascontiguousarray(np.broadcast_to(twiddle[:, :, None], (2, HALF, HALF)))
    cols = np.ascontiguousarray(np.broadcast_to(twiddle[:, None, :], (2, 8, HALF)))
    return left, left_t, right, right_t, rows, cols


def split3(x, axis):
    high = x.astype(jnp.bfloat16)
    low = (x - high.astype(jnp.float32)).astype(jnp.bfloat16)
    return jnp.concatenate([high, low, high], axis=axis)


def left_dft(matrix, x):
    return jnp.dot(matrix, split3(x, 0), preferred_element_type=jnp.float32)


def right_dft(x, matrix):
    return jnp.dot(split3(x, 1), matrix, preferred_element_type=jnp.float32)


def forward_dft(real, imag, left, right_t, twr, twc):
    t_r, t_i = twr
    c_r, c_i = twc
    a_r, b_r, a_i, b_i = real[:HALF], real[HALF:], imag[:HALF], imag[HALF:]
    d_r, d_i = a_r - b_r, a_i - b_i
    even = left_dft(left, jnp.concatenate([a_r + b_r, a_i + b_i], axis=0))
    odd = left_dft(left, jnp.concatenate([d_r * t_r - d_i * t_i, d_r * t_i + d_i * t_r], axis=0))
    real = jnp.concatenate([even[:HALF], odd[:HALF]], axis=0)
    imag = jnp.concatenate([even[HALF:], odd[HALF:]], axis=0)
    a_r, b_r, a_i, b_i = real[:, :HALF], real[:, HALF:], imag[:, :HALF], imag[:, HALF:]
    d_r, d_i = a_r - b_r, a_i - b_i
    even = right_dft(jnp.concatenate([a_r + b_r, a_i + b_i], axis=1), right_t)
    odd = right_dft(jnp.concatenate([d_r * c_r - d_i * c_i, d_r * c_i + d_i * c_r], axis=1), right_t)
    real = jnp.concatenate([even[:, :HALF], odd[:, :HALF]], axis=1)
    imag = jnp.concatenate([even[:, HALF:], odd[:, HALF:]], axis=1)
    return real, imag


def inverse_dft(real, imag, left_t, right, twr, twc):
    t_r, t_i = twr
    c_r, c_i = twc
    even = right_dft(jnp.concatenate([real[:, :HALF], imag[:, :HALF]], axis=1), right)
    odd = right_dft(jnp.concatenate([real[:, HALF:], imag[:, HALF:]], axis=1), right)
    o_r, o_i = odd[:, :HALF], odd[:, HALF:]
    o_r, o_i = o_r * c_r + o_i * c_i, o_i * c_r - o_r * c_i
    e_r, e_i = even[:, :HALF], even[:, HALF:]
    real = jnp.concatenate([e_r + o_r, e_r - o_r], axis=1)
    imag = jnp.concatenate([e_i + o_i, e_i - o_i], axis=1)
    even = left_dft(left_t, jnp.concatenate([real[:HALF], imag[:HALF]], axis=0))
    odd = left_dft(left_t, jnp.concatenate([real[HALF:], imag[HALF:]], axis=0))
    o_r, o_i = odd[:HALF], odd[HALF:]
    o_r, o_i = o_r * t_r + o_i * t_i, o_i * t_r - o_r * t_i
    e_r, e_i = even[:HALF], even[HALF:]
    real = jnp.concatenate([e_r + o_r, e_r - o_r], axis=0)
    imag = jnp.concatenate([e_i + o_i, e_i - o_i], axis=0)
    return real, imag


def window_fit(window, probe, amplitude, tables, far, window_ref, gradient, add_probe):
    left, left_t, right, right_t, rows, cols = tables
    window_ref[0] = window[0]
    window_ref[1] = window[1]

    def twiddles():
        twr = tuple(jnp.concatenate([rows[k], rows[k]], axis=1) for k in range(2))
        twc = tuple(cols[k][:1] for k in range(2))
        return twr, twc

    def outward(m, carry):
        twr, twc = twiddles()
        w_r, w_i = window_ref[0], window_ref[1]
        p_r, p_i = probe[m, 0], probe[m, 1]
        f_r, f_i = forward_dft(p_r * w_r - p_i * w_i, p_r * w_i + p_i * w_r, left[...], right_t[...], twr, twc)
        far[m, 0] = f_r
        far[m, 1] = f_i
        return carry

    lax.fori_loop(0, 2, outward, 0)
    intensity = far[0, 0] * far[0, 0] + far[0, 1] * far[0, 1]
    intensity = intensity + (far[1, 0] * far[1, 0] + far[1, 1] * far[1, 1])
    factor = amplitude / jnp.sqrt(jnp.maximum(intensity, 0.1)) - 1.0
    for m in range(2):
        far[m, 0] = far[m, 0] * factor
        far[m, 1] = far[m, 1] * factor
    gradient[...] = jnp.zeros(gradient.shape, jnp.float32)

    def inward(m, carry):
        twr, twc = twiddles()
        x_r, x_i = inverse_dft(far[m, 0], far[m, 1], left_t[...], right[...], twr, twc)
        w_r, w_i = window_ref[0], window_ref[1]
        p_r, p_i = probe[m, 0], probe[m, 1]
        gradient[0] += p_r * x_r + p_i * x_i
        gradient[1] += p_r * x_i - p_i * x_r
        add_probe(m, w_r * x_r + w_i * x_i, w_r * x_i - w_i * x_r)
        return carry

    lax.fori_loop(0, 2, inward, 0)


def before_kernel(probe, amp, amp_out, step_out):
    out_at = lax.broadcasted_iota(jnp.int32, (WIN, WIN), 0)
    in_at = lax.broadcasted_iota(jnp.int32, (WIN, WIN), 1)
    wanted = jnp.where(out_at < HALF, 2 * out_at, 2 * (out_at - HALF) + 1)
    pick = jnp.where(in_at == wanted, 1.0, 0.0).astype(jnp.bfloat16)
    for b in range(BATCHES):
        rows = jnp.dot(pick, amp[b], preferred_element_type=jnp.float32).astype(jnp.bfloat16)
        amp_out[b] = lax.dot_general(rows, pick, (((1,), (1,)), ((), ())), preferred_element_type=jnp.float32)
    total = jnp.zeros((8, HALF), jnp.float32)
    for m in range(2):
        for k in range(2):
            square = probe[m, k] * probe[m, k]
            square = jnp.sum(square.reshape(WIN // 8, 8, WIN), axis=0)
            total = total + square[:, :HALF] + square[:, HALF:]
    power = jnp.sum(total) / (WIN * WIN)
    step_out[...] = jnp.full((8, HALF), 1.0, jnp.float32) / (power + 1e-06)


TILE_R = 384
LAST = TILE_R - WIN
WIDE = WIN + HALO


def first_kernel(pos, above, obj, halo, probe, amp, step, left, left_t, right, right_t, rows, cols,
                 new_obj, spill, edge, middle, probe_sum, far, win, grad):
    row, col = pos[0, 0], pos[0, 1]

    def cut(k):
        wide = jnp.concatenate([obj[k], halo[k]], axis=1)
        wide = pltpu.roll(wide, WIDE - col, 1)[:, :WIN]
        return pltpu.roll(wide, lax.rem(TILE_R - row, TILE_R), 0)[:WIN]

    def add_probe(m, real, imag):
        probe_sum[m, 0] = real
        probe_sum[m, 1] = imag

    window_fit((cut(0), cut(1)), probe, amp[0], (left, left_t, right, right_t, rows, cols), far, win, grad, add_probe)
    scale = step[:1, :1]
    for k in range(2):
        g = jnp.concatenate([grad[k] * scale, jnp.zeros((TILE_R - WIN, WIN), jnp.float32)], axis=0)
        g = pltpu.roll(g, row, 0)
        g = jnp.concatenate([g, jnp.zeros((TILE_R, HALO), jnp.float32)], axis=1)
        g = pltpu.roll(g, col, 1)
        updated = obj[k] + g[:, :WIN]
        new_obj[k] = updated
        edge[k] = updated[:, :HALO]
        middle[k] = updated[:HALO, HALO:]
        spill[k] = g[:, WIN:]


def lanes():
    return lax.broadcasted_iota(jnp.int32, (HALO, HALO), 1)


def upward_kernel(info, edge, from_left, from_right, spill, upward):
    keep = info[1].astype(jnp.float32)
    for k in range(2):
        own = edge[k, :HALO] + from_left[k, :HALO]
        upward[k] = jnp.where(lanes() >= info[0], own, from_right[k, :HALO] + spill[k, :HALO] * keep)


def second_kernel(pos, info, obj, from_left, from_right, spill, below_mid, below_rest, probe, amp, step, probe_in,
                  left, left_t, right, right_t, rows, cols,
                  new_obj, new_spill, downward, keep_sum, send_sum, far, win, grad):
    row, col = pos[1, 0] - LAST, pos[1, 1]
    keep, core = info[1].astype(jnp.float32), info[2]

    def cut(k):
        upper = jnp.concatenate(
            [obj[k, LAST:, :HALO] + from_left[k, LAST:], obj[k, LAST:, HALO:], from_right[k, LAST:] + spill[k, LAST:] * keep],
            axis=1)
        lower = jnp.concatenate([below_rest[k], below_mid[k], below_rest[k]], axis=1)
        tall = pltpu.roll(jnp.concatenate([upper, lower], axis=0), WIDE - col, 1)[:, :WIN]
        return pltpu.roll(tall, lax.rem(TILE_R - row, TILE_R), 0)[:WIN]

    def add_probe(m, real, imag):
        @pl.when(m == core)
        def _():
            keep_sum[0] = probe_in[m, 0] + real
            keep_sum[1] = probe_in[m, 1] + imag

        @pl.when(m != core)
        def _():
            send_sum[0] = probe_in[m, 0] + real
            send_sum[1] = probe_in[m, 1] + imag

    window_fit((cut(0), cut(1)), probe, amp[1], (left, left_t, right, right_t, rows, cols), far, win, grad, add_probe)
    scale = step[:1, :1]
    for k in range(2):
        g = jnp.concatenate([grad[k] * scale, jnp.zeros((TILE_R - WIN, WIN), jnp.float32)], axis=0)
        g = pltpu.roll(g, row, 0)
        g = jnp.concatenate([g, jnp.zeros((TILE_R, HALO), jnp.float32)], axis=1)
        g = pltpu.roll(g, col, 1)
        downward[k, :, :HALO] = g[WIN:, :HALO] + g[WIN:, WIN:]
        downward[k, :, HALO:] = g[WIN:, HALO:WIN]
        new_obj[k, :LAST, :HALO] = obj[k, :LAST, :HALO] + from_left[k, :LAST]
        new_obj[k, :LAST, HALO:] = obj[k, :LAST, HALO:]
        new_obj[k, LAST:, :HALO] = obj[k, LAST:, :HALO] + from_left[k, LAST:] + g[:WIN, :HALO]
        new_obj[k, LAST:, HALO:] = obj[k, LAST:, HALO:] + g[:WIN, HALO:WIN]
        new_spill[k] = g[:WIN, WIN:]


def spill_kernel(info, spill, from_above, new_spill):
    for k in range(2):
        new_spill[k, :HALO] = jnp.where(lanes() < info[0], from_above[k, :, :HALO], 0.0)
        new_spill[k, HALO:] = spill[k]


def object_kernel(info, obj, from_above, from_left, out):
    for k in range(2):
        fell = jnp.where(lanes() >= info[0], from_above[k, :, :HALO], 0.0)
        out[k, :HALO, :HALO] = obj[k, :HALO, :HALO] + fell + from_left[k, :HALO]
        out[k, HALO:, :HALO] = obj[k, HALO:, :HALO] + from_left[k, HALO:]
        out[k, :HALO, HALO:] = obj[k, :HALO, HALO:] + from_above[k, :, HALO:]
        out[k, HALO:, HALO:] = obj[k, HALO:, HALO:]


def probe_kernel(info, probe, own, other, out):
    core = info[2]
    out[core] = probe[core] + own[...]
    out[1 - core] = probe[1 - core] + other[...]


def call(kernel, outs, scratch, scalars, *arrays, last=False):
    vmem = pl.BlockSpec(memory_space=pltpu.VMEM)
    smem = pl.BlockSpec(memory_space=pltpu.SMEM)
    if INTERPRET or last:
        shapes = [jax.ShapeDtypeStruct(s, jnp.float32) for s in outs]
    else:
        shapes = [pltpu.VMEM(s, jnp.float32) for s in outs]
    if not INTERPRET:
        arrays = [pltpu.with_memory_space_constraint(x, pltpu.VMEM) for x in arrays]
    return pl.pallas_call(
        kernel,
        out_shape=shapes,
        in_specs=[smem] * len(scalars) + [vmem] * len(arrays),
        out_specs=[vmem] * len(outs),
        scratch_shapes=[pltpu.VMEM(s, jnp.float32) for s in scratch],
        compiler_params=pltpu.CompilerParams(vmem_limit_bytes=24 * 1024 * 1024),
        interpret=INTERPRET,
    )(*scalars, *arrays)


def passed_along(block, axis, distance):
    devices = range(lax.axis_size(axis))
    route = [(i - distance, i) for i in devices if i - distance in devices]
    return lax.ppermute(block, axis, route)


def exchanged(parts, axes):
    return lax.all_to_all(parts, axes, 0, 0, tiled=False)


def swapped(block):
    return lax.ppermute(block, CORE, [(0, 1), (1, 0)])


def summed_everywhere(keep, send, divisor):
    plane, depth = lax.axis_size(PLANE), lax.axis_size(DEPTH)
    mode = keep + swapped(send)
    parts = exchanged(mode.reshape(plane, -1, WIN), PLANE)
    share = jnp.sum(parts, axis=0)
    parts = exchanged(jnp.broadcast_to(share, (depth, *share.shape)), DEPTH)
    share = jnp.sum(parts, axis=0) / divisor
    mode = exchanged(jnp.broadcast_to(share, (plane, *share.shape)), PLANE).reshape(2, WIN, WIN)
    return mode, swapped(mode)


def step_once(object_field, probe_modes, scan_positions, amplitudes):
    tables = [jnp.asarray(t) for t in dft_constants()]
    positions = scan_positions[0, 0]
    device_count = lax.axis_size(ROW) * lax.axis_size(COL)
    divisor = math.sqrt(device_count * BATCHES)
    has_right = (lax.axis_index(COL) < lax.axis_size(COL) - 1).astype(jnp.int32)
    tile, side, probe_shape = (2, TILE_R, WIN), (2, TILE_R, HALO), (2, 2, WIN, WIN)
    block = (2, HALO, HALO)
    fit_scratch = [probe_shape, (2, WIN, WIN), (2, WIN, WIN)]

    halo = passed_along(object_field[:, :, :HALO], COL, -1)
    above = passed_along(positions, ROW, 1)
    info = jnp.stack([above[1, 1], has_right, lax.axis_index(CORE)])
    amp, step = call(before_kernel, [(BATCHES, WIN, WIN), (8, HALF)], [], [], probe_modes, amplitudes[0, 0])
    obj, spill, edge, middle, probe_sum = call(
        first_kernel, [tile, side, side, block, probe_shape], fit_scratch, [positions, info],
        object_field, halo, probe_modes, amp, step, *tables)
    from_left = passed_along(spill, COL, 1)
    from_right = passed_along(edge, COL, -1)
    below_mid = passed_along(middle, ROW, -1)
    (upward,) = call(upward_kernel, [block], [], [info], edge, from_left, from_right, spill)
    below_rest = passed_along(upward, ROW, -1)
    obj, spill, downward, keep, send = call(
        second_kernel, [tile, (2, WIN, HALO), (2, HALO, WIN), (2, WIN, WIN), (2, WIN, WIN)], fit_scratch, [positions, info],
        obj, from_left, from_right, spill, below_mid, below_rest, probe_modes, amp, step, probe_sum, *tables)
    from_above = passed_along(downward, ROW, 1)
    own, other = summed_everywhere(keep, send, divisor)
    (spill,) = call(spill_kernel, [side], [], [info], spill, from_above)
    from_left = passed_along(spill, COL, 1)
    (object_out,) = call(object_kernel, [tile], [], [info], obj, from_above, from_left, last=True)
    (probe_out,) = call(probe_kernel, [probe_shape], [], [info], probe_modes, own, other, last=True)
    return (object_out, probe_out)


def solution(mesh):
    torus = Mesh(mesh.devices.reshape(4, 4, 4, 4, 2), ("row_0", "row_1", "col_0", "col_1", "col_2"))
    in_specs = (P(None, ROW, COL), P(), P(ROW, COL, None, None), P(ROW, COL, None, None, None))
    out_specs = (P(None, ROW, COL), P())
    return jax.shard_map(step_once, mesh=torus, in_specs=in_specs, out_specs=out_specs, check_vma=False)
```

profile of v0, /device:TPU:120, one launch (start us, length us, event | category | flops | bytes accessed | tf_op | source)
XLA Modules:
  0.0 171.1 jit_solution(16464680608004348758)
XLA Ops:
  0.6 0.0 copy-start.2
  0.6 1.1 slice.7
  1.7 0.0 copy-start.11
  1.7 3.7 %collective-permute-start.1 = (f32[2,384,128]{2,1,0:T(8,128)S(1)}, f32[2,384,128]{2,1,0:T(8,128)S(1)}, u32[]{:S(2)}, u32[]{:S(2)}) collective-permute-start(f32[2,384,128]{2,1,0:T(8,128)S(1)} %slice.7), channel_id=1, source_target_pairs={{1,0},{2,1},{3,2},{4,3},{5,4},{6,5},{7,6},{8,7},{9,8},{10,9},{11,1... | collective-permute-start | bytes 1179656 | tf_op jit(solution)/shard_map/ppermute | solution.py:288
  5.4 0.0 copy-done.11
  5.4 9.1 %collective-permute-start = (s32[2,2]{1,0:T(2,128)S(1)}, s32[2,2]{1,0:T(2,128)S(1)}, u32[]{:S(2)}, u32[]{:S(2)}) collective-permute-start(s32[2,2]{1,0:T(2,128)S(1)} %bitcast.10), channel_id=1, source_target_pairs={{0,32},{32,64},{64,96},{96,128},{128,160},{160,192},{192,224},{224... | collective-permute-start | bytes 56 | tf_op jit(solution)/shard_map/ppermute | solution.py:288
  14.5 0.0 copy-start
  14.5 1.2 copy-done
  15.8 0.0 copy-start.9
  15.8 0.9 copy-done.9
  16.7 0.0 copy-start.3
  16.7 0.0 copy-start.4
  16.7 0.0 copy-start.5
  16.7 0.0 copy-start.8
  16.7 0.4 shard_map.113
  17.1 0.0 copy-start.10
  17.1 0.9 collective-permute-done
  18.1 0.6 slice.6
  18.7 0.7 pad_add_fusion.above.info
  19.4 0.0 collective-permute-done.1.halo
  19.4 0.0 copy-done.2
  19.4 0.0 copy-done.3
  19.4 0.0 copy-done.4
  19.4 0.0 copy-done.5
  19.4 0.0 copy-done.8
  19.4 0.0 copy-done.10
  19.4 0.0 copy-start.6
  19.4 1.0 copy-done.6
  20.4 5.2 %shard_map.114 = (f32[2,384,256]{2,1,0:T(8,128)S(1)}, f32[2,384,128]{2,1,0:T(8,128)S(1)}, f32[2,384,128]{2,1,0:T(8,128)S(1)}, f32[2,128,128]{2,1,0:T(8,128)S(1)}, f32[2,2,256,256]{3,2,1,0:T(8,128)S(1)}) custom-call(s32[2,2]{1,0:T(2,128)S(1)} %bitcast.11, s32[3]{0:T(128)S(1)} %pad_add_fusion.above.info, f32[2,384,256]{2,1,0:T(8,128)S(1)} %copy-done.2, ...), custom_call_target="tpu_custom_call" | custom-call | tf_op jit(solution)/shard_map/pallas_call | solution.py:274
  25.7 0.0 copy-start.1
  25.7 2.1 %collective-permute-start.3 = (f32[2,384,128]{2,1,0:T(8,128)S(1)}, f32[2,384,128]{2,1,0:T(8,128)S(1)}, u32[]{:S(2)}, u32[]{:S(2)}) collective-permute-start(f32[2,384,128]{2,1,0:T(8,128)S(1)} %get-tuple-element.18.edge), channel_id=1, source_target_pairs={{1,0},{2,1},{3,2},{4,3},{5,4},{6,5},{7,6},{8,7},{9,8},{10,9},{11,1... | collective-permute-start | bytes 1179656 | tf_op jit(solution)/shard_map/ppermute | solution.py:288
  27.7 2.4 %collective-permute-start.2 = (f32[2,384,128]{2,1,0:T(8,128)S(1)}, f32[2,384,128]{2,1,0:T(8,128)S(1)}, u32[]{:S(2)}, u32[]{:S(2)}) collective-permute-start(f32[2,384,128]{2,1,0:T(8,128)S(1)} %get-tuple-element.17.spill), channel_id=1, source_target_pairs={{0,1},{1,2},{2,3},{3,4},{4,5},{5,6},{6,7},{7,8},{8,9},{9,10},{10,1... | collective-permute-start | bytes 1179656 | tf_op jit(solution)/shard_map/ppermute | solution.py:288
  30.2 0.0 copy-start.7
  30.2 8.0 %collective-permute-start.4 = (f32[2,128,128]{2,1,0:T(8,128)S(1)}, f32[2,128,128]{2,1,0:T(8,128)S(1)}, u32[]{:S(2)}, u32[]{:S(2)}) collective-permute-start(f32[2,128,128]{2,1,0:T(8,128)S(1)} %get-tuple-element.19), channel_id=1, source_target_pairs={{32,0},{64,32},{96,64},{128,96},{160,128},{192,160},{224,192},{256... | collective-permute-start | bytes 393224 | tf_op jit(solution)/shard_map/ppermute | solution.py:288
  38.1 0.0 collective-permute-done.3.from_right
  38.2 0.8 collective-permute-done.2.from_left
  39.0 0.6 shard_map.115
  39.5 7.8 %collective-permute-start.5 = (f32[2,128,128]{2,1,0:T(8,128)S(1)}, f32[2,128,128]{2,1,0:T(8,128)S(1)}, u32[]{:S(2)}, u32[]{:S(2)}) collective-permute-start(f32[2,128,128]{2,1,0:T(8,128)S(1)} %shard_map.115), channel_id=1, source_target_pairs={{32,0},{64,32},{96,64},{128,96},{160,128},{192,160},{224,192},{256... | collective-permute-start | bytes 393224 | tf_op jit(solution)/shard_map/ppermute | solution.py:288
  47.4 3.3 %collective-permute-done.4.below_mid = f32[2,128,128]{2,1,0:T(8,128)S(1)} collective-permute-done((f32[2,128,128]{2,1,0:T(8,128)S(1)}, f32[2,128,128]{2,1,0:T(8,128)S(1)}, u32[]{:S(2)}, u32[]{:S(2)}) %collective-permute-start.4) | collective-permute-done | bytes 131104 | tf_op jit(solution)/shard_map/ppermute | solution.py:288
  50.6 3.8 %collective-permute-done.5.below_rest = f32[2,128,128]{2,1,0:T(8,128)S(1)} collective-permute-done((f32[2,128,128]{2,1,0:T(8,128)S(1)}, f32[2,128,128]{2,1,0:T(8,128)S(1)}, u32[]{:S(2)}, u32[]{:S(2)}) %collective-permute-start.5) | collective-permute-done | bytes 131104 | tf_op jit(solution)/shard_map/ppermute | solution.py:288
  54.4 0.0 copy-done.1
  54.4 0.0 copy-done.7
  54.4 5.5 %shard_map.116 = (f32[2,384,256]{2,1,0:T(8,128)S(1)}, f32[2,256,128]{2,1,0:T(8,128)S(1)}, f32[2,128,256]{2,1,0:T(8,128)S(1)}, f32[2,256,256]{2,1,0:T(8,128)S(1)}, f32[2,256,256]{2,1,0:T(8,128)S(1)}) custom-call(s32[2,2]{1,0:T(2,128)S(1)} %bitcast.12, s32[3]{0:T(128)S(1)} %pad_add_fusion.above.info, f32[2,384,256]{2,1,0:T(8,128)S(1)} %get-tuple-element.16.obj, ...), custom_call_target="tpu_custom_call" | custom-call | tf_op jit(solution)/shard_map/pallas_call | solution.py:274
  59.9 1.9 %collective-permute-start.8 = (f32[2,256,256]{2,1,0:T(8,128)S(1)}, f32[2,256,256]{2,1,0:T(8,128)S(1)}, u32[]{:S(2)}, u32[]{:S(2)}) collective-permute-start(f32[2,256,256]{2,1,0:T(8,128)S(1)} %get-tuple-element.25), channel_id=1, source_target_pairs={{0,1},{1,0},{2,3},{3,2},{4,5},{5,4},{6,7},{7,6},{8,9},{9,8},{10,11... | collective-permute-start | bytes 1572872 | tf_op jit(solution)/shard_map/ppermute | solution.py:296
  61.8 1.9 %collective-permute-done.8 = f32[2,256,256]{2,1,0:T(8,128)S(1)} collective-permute-done((f32[2,256,256]{2,1,0:T(8,128)S(1)}, f32[2,256,256]{2,1,0:T(8,128)S(1)}, u32[]{:S(2)}, u32[]{:S(2)}) %collective-permute-start.8) | collective-permute-done | bytes 524320 | tf_op jit(solution)/shard_map/ppermute | solution.py:296
  63.7 0.1 add.11
  63.8 24.3 %all_to_all.15 = f32[16,32,256]{2,1,0:T(8,128)S(1)} all-to-all(f32[16,32,256]{2,1,0:T(8,128)S(1)} %bitcast.13), channel_id=1, replica_groups=mesh['row_0'=4,'row_1'=4,'col_0'=4,'col_1'=4,'col_2'=2] {'row_0','col_1'}, dimensions={0} | all-to-all | bytes 1048576 | tf_op jit(solution)/shard_map/all_to_all | solution.py:292
  88.2 36.3 %all_to_all.16 = f32[16,32,256]{2,1,0:T(8,128)S(1)} all-to-all(f32[16,32,256]{2,1,0:T(8,128)S(1)} %broadcast_in_dim.6), channel_id=1, replica_groups=mesh['row_0'=4,'row_1'=4,'col_0'=4,'col_1'=4,'col_2'=2] {'row_1','col_0'}, dimensions={0} | all-to-all | bytes 1048576 | tf_op jit(solution)/shard_map/all_to_all | solution.py:292
  124.5 0.8 broadcast_in_dim.7
  125.3 5.8 %all-to-all-start.2 = ((f32[16,32,256]{2,1,0:T(8,128)}), f32[16,32,256]{2,1,0:T(8,128)S(1)}, u32[]{:S(2)}, u32[]{:S(2)}) async-start(f32[16,32,256]{2,1,0:T(8,128)} %broadcast_in_dim.7), calls=%async_computation.2 | async-start | bytes 1048576 | tf_op jit(solution)/shard_map/all_to_all | solution.py:292
  131.2 4.3 %collective-permute-start.6 = (f32[2,128,256]{2,1,0:T(8,128)S(1)}, f32[2,128,256]{2,1,0:T(8,128)S(1)}, u32[]{:S(2)}, u32[]{:S(2)}) collective-permute-start(f32[2,128,256]{2,1,0:T(8,128)S(1)} %get-tuple-element.22), channel_id=1, source_target_pairs={{0,32},{32,64},{64,96},{96,128},{128,160},{160,192},{192,224},{224... | collective-permute-start | bytes 786440 | tf_op jit(solution)/shard_map/ppermute | solution.py:288
  135.5 3.5 %all-to-all-done.2 = f32[16,32,256]{2,1,0:T(8,128)S(1)} async-done(((f32[16,32,256]{2,1,0:T(8,128)}), f32[16,32,256]{2,1,0:T(8,128)S(1)}, u32[]{:S(2)}, u32[]{:S(2)}) %all-to-all-start.2) | async-done | bytes 524320 | tf_op jit(solution)/shard_map/all_to_all | solution.py:292
  139.0 1.9 %collective-permute-start.9 = (f32[2,256,256]{2,1,0:T(8,128)S(1)}, f32[2,256,256]{2,1,0:T(8,128)S(1)}, u32[]{:S(2)}, u32[]{:S(2)}) collective-permute-start(f32[2,256,256]{2,1,0:T(8,128)S(1)} %bitcast.7), channel_id=1, source_target_pairs={{0,1},{1,0},{2,3},{3,2},{4,5},{5,4},{6,7},{7,6},{8,9},{9,8},{10,11... | collective-permute-start | bytes 1572872 | tf_op jit(solution)/shard_map/ppermute | solution.py:296
  140.9 15.3 %collective-permute-done.6.from_above = f32[2,128,256]{2,1,0:T(8,128)S(1)} collective-permute-done((f32[2,128,256]{2,1,0:T(8,128)S(1)}, f32[2,128,256]{2,1,0:T(8,128)S(1)}, u32[]{:S(2)}, u32[]{:S(2)}) %collective-permute-start.6) | collective-permute-done | bytes 262176 | tf_op jit(solution)/shard_map/ppermute | solution.py:288
  156.2 0.6 shard_map.117
  156.8 1.9 %collective-permute-start.7 = (f32[2,384,128]{2,1,0:T(8,128)S(1)}, f32[2,384,128]{2,1,0:T(8,128)S(1)}, u32[]{:S(2)}, u32[]{:S(2)}) collective-permute-start(f32[2,384,128]{2,1,0:T(8,128)S(1)} %shard_map.117), channel_id=1, source_target_pairs={{0,1},{1,2},{2,3},{3,4},{4,5},{5,6},{6,7},{7,8},{8,9},{9,10},{10,1... | collective-permute-start | bytes 1179656 | tf_op jit(solution)/shard_map/ppermute | solution.py:288
  158.7 9.3 %collective-permute-done.7.from_left = f32[2,384,128]{2,1,0:T(8,128)S(1)} collective-permute-done((f32[2,384,128]{2,1,0:T(8,128)S(1)}, f32[2,384,128]{2,1,0:T(8,128)S(1)}, u32[]{:S(2)}, u32[]{:S(2)}) %collective-permute-start.7) | collective-permute-done | bytes 393248 | tf_op jit(solution)/shard_map/ppermute | solution.py:288
  168.0 1.5 shard_map.118
  169.5 0.0 collective-permute-done.9.other
  169.5 1.6 shard_map.119
  (4 shorter events, 0.1 us)
Async XLA Ops:
  0.6 18.8 %copy-start.2 = (f32[2,384,256]{2,1,0:T(8,128)S(1)}, f32[2,384,256]{2,1,0:T(8,128)}, u32[]{:S(2)}) copy-start(f32[2,384,256]{2,1,0:T(8,128)} %obj.1) | copy-start | bytes 2359300
  1.7 3.7 %copy-start.11 = (s32[1,1,2,2]{3,2,1,0:T(2,128)S(1)}, s32[1,1,2,2]{3,2,1,0:T(2,128)}, u32[]{:S(2)}) copy-start(s32[1,1,2,2]{3,2,1,0:T(2,128)} %param.12) | copy-start | bytes 52
  1.7 17.6 %collective-permute-start.1 = (f32[2,384,128]{2,1,0:T(8,128)S(1)}, f32[2,384,128]{2,1,0:T(8,128)S(1)}, u32[]{:S(2)}, u32[]{:S(2)}) collective-permute-start(f32[2,384,128]{2,1,0:T(8,128)S(1)} %slice.7), channel_id=1, source_target_pairs={{1,0},{2,1},{3,2},{4,3},{5,4},{6,5},{7,6},{8,7},{9,8},{10,9},{11,1... | collective-permute-start | bytes 1179656 | tf_op jit(solution)/shard_map/ppermute | solution.py:288
  5.4 12.7 %collective-permute-start = (s32[2,2]{1,0:T(2,128)S(1)}, s32[2,2]{1,0:T(2,128)S(1)}, u32[]{:S(2)}, u32[]{:S(2)}) collective-permute-start(s32[2,2]{1,0:T(2,128)S(1)} %bitcast.10), channel_id=1, source_target_pairs={{0,32},{32,64},{64,96},{96,128},{128,160},{160,192},{192,224},{224... | collective-permute-start | bytes 56 | tf_op jit(solution)/shard_map/ppermute | solution.py:288
  14.5 1.2 copy-start
  15.8 0.9 copy-start.9
  16.7 2.7 %copy-start.3 = (bf16[768,256]{1,0:T(8,128)(2,1)S(1)}, bf16[768,256]{1,0:T(8,128)(2,1)}, u32[]{:S(2)}) copy-start(bf16[768,256]{1,0:T(8,128)(2,1)} %constant.37.clone.right_t) | copy-start | bytes 1179652
  16.7 2.7 %copy-start.4 = (bf16[768,256]{1,0:T(8,128)(2,1)S(1)}, bf16[768,256]{1,0:T(8,128)(2,1)}, u32[]{:S(2)}) copy-start(bf16[768,256]{1,0:T(8,128)(2,1)} %constant.36.clone.right) | copy-start | bytes 1179652
  16.7 2.7 %copy-start.5 = (bf16[256,768]{1,0:T(8,128)(2,1)S(1)}, bf16[256,768]{1,0:T(8,128)(2,1)}, u32[]{:S(2)}) copy-start(bf16[256,768]{1,0:T(8,128)(2,1)} %constant.35.clone.left_t) | copy-start | bytes 1179652
  16.7 2.7 %copy-start.8 = (f32[2,128,128]{2,1,0:T(8,128)S(1)}, f32[2,128,128]{2,1,0:T(8,128)}, u32[]{:S(2)}) copy-start(f32[2,128,128]{2,1,0:T(8,128)} %constant.38.clone.rows) | copy-start | bytes 393220
  17.1 2.3 %copy-start.10 = (f32[2,8,128]{2,1,0:T(8,128)S(1)}, f32[2,8,128]{2,1,0:T(8,128)}, u32[]{:S(2)}) copy-start(f32[2,8,128]{2,1,0:T(8,128)} %constant.39.clone.cols) | copy-start | bytes 24580
  19.4 1.0 copy-start.6
  25.7 28.8 %copy-start.1 = (f32[2,2,256,256]{3,2,1,0:T(8,128)S(1)}, f32[2,2,256,256]{3,2,1,0:T(8,128)}, u32[]{:S(2)}) copy-start(f32[2,2,256,256]{3,2,1,0:T(8,128)} %probe.7) | copy-start | bytes 3145732
  25.7 12.5 %collective-permute-start.3 = (f32[2,384,128]{2,1,0:T(8,128)S(1)}, f32[2,384,128]{2,1,0:T(8,128)S(1)}, u32[]{:S(2)}, u32[]{:S(2)}) collective-permute-start(f32[2,384,128]{2,1,0:T(8,128)S(1)} %get-tuple-element.18.edge), channel_id=1, source_target_pairs={{1,0},{2,1},{3,2},{4,3},{5,4},{6,5},{7,6},{8,7},{9,8},{10,9},{11,1... | collective-permute-start | bytes 1179656 | tf_op jit(solution)/shard_map/ppermute | solution.py:288
  27.7 11.2 %collective-permute-start.2 = (f32[2,384,128]{2,1,0:T(8,128)S(1)}, f32[2,384,128]{2,1,0:T(8,128)S(1)}, u32[]{:S(2)}, u32[]{:S(2)}) collective-permute-start(f32[2,384,128]{2,1,0:T(8,128)S(1)} %get-tuple-element.17.spill), channel_id=1, source_target_pairs={{0,1},{1,2},{2,3},{3,4},{4,5},{5,6},{6,7},{7,8},{8,9},{9,10},{10,1... | collective-permute-start | bytes 1179656 | tf_op jit(solution)/shard_map/ppermute | solution.py:288
  30.2 24.3 %copy-start.7 = (bf16[256,768]{1,0:T(8,128)(2,1)S(1)}, bf16[256,768]{1,0:T(8,128)(2,1)}, u32[]{:S(2)}) copy-start(bf16[256,768]{1,0:T(8,128)(2,1)} %constant.34.clone.left) | copy-start | bytes 1179652
  30.2 20.5 %collective-permute-start.4 = (f32[2,128,128]{2,1,0:T(8,128)S(1)}, f32[2,128,128]{2,1,0:T(8,128)S(1)}, u32[]{:S(2)}, u32[]{:S(2)}) collective-permute-start(f32[2,128,128]{2,1,0:T(8,128)S(1)} %get-tuple-element.19), channel_id=1, source_target_pairs={{32,0},{64,32},{96,64},{128,96},{160,128},{192,160},{224,192},{256... | collective-permute-start | bytes 393224 | tf_op jit(solution)/shard_map/ppermute | solution.py:288
  39.5 14.9 %collective-permute-start.5 = (f32[2,128,128]{2,1,0:T(8,128)S(1)}, f32[2,128,128]{2,1,0:T(8,128)S(1)}, u32[]{:S(2)}, u32[]{:S(2)}) collective-permute-start(f32[2,128,128]{2,1,0:T(8,128)S(1)} %shard_map.115), channel_id=1, source_target_pairs={{32,0},{64,32},{96,64},{128,96},{160,128},{192,160},{224,192},{256... | collective-permute-start | bytes 393224 | tf_op jit(solution)/shard_map/ppermute | solution.py:288
  59.9 3.8 %collective-permute-start.8 = (f32[2,256,256]{2,1,0:T(8,128)S(1)}, f32[2,256,256]{2,1,0:T(8,128)S(1)}, u32[]{:S(2)}, u32[]{:S(2)}) collective-permute-start(f32[2,256,256]{2,1,0:T(8,128)S(1)} %get-tuple-element.25), channel_id=1, source_target_pairs={{0,1},{1,0},{2,3},{3,2},{4,5},{5,4},{6,7},{7,6},{8,9},{9,8},{10,11... | collective-permute-start | bytes 1572872 | tf_op jit(solution)/shard_map/ppermute | solution.py:296
  125.3 13.7 %all-to-all-start.2 = ((f32[16,32,256]{2,1,0:T(8,128)}), f32[16,32,256]{2,1,0:T(8,128)S(1)}, u32[]{:S(2)}, u32[]{:S(2)}) async-start(f32[16,32,256]{2,1,0:T(8,128)} %broadcast_in_dim.7), calls=%async_computation.2 | async-start | bytes 1048576 | tf_op jit(solution)/shard_map/all_to_all | solution.py:292
  131.2 25.0 %collective-permute-start.6 = (f32[2,128,256]{2,1,0:T(8,128)S(1)}, f32[2,128,256]{2,1,0:T(8,128)S(1)}, u32[]{:S(2)}, u32[]{:S(2)}) collective-permute-start(f32[2,128,256]{2,1,0:T(8,128)S(1)} %get-tuple-element.22), channel_id=1, source_target_pairs={{0,32},{32,64},{64,96},{96,128},{128,160},{160,192},{192,224},{224... | collective-permute-start | bytes 786440 | tf_op jit(solution)/shard_map/ppermute | solution.py:288
  139.0 30.5 %collective-permute-start.9 = (f32[2,256,256]{2,1,0:T(8,128)S(1)}, f32[2,256,256]{2,1,0:T(8,128)S(1)}, u32[]{:S(2)}, u32[]{:S(2)}) collective-permute-start(f32[2,256,256]{2,1,0:T(8,128)S(1)} %bitcast.7), channel_id=1, source_target_pairs={{0,1},{1,0},{2,3},{3,2},{4,5},{5,4},{6,7},{7,6},{8,9},{9,8},{10,11... | collective-permute-start | bytes 1572872 | tf_op jit(solution)/shard_map/ppermute | solution.py:296
  156.8 11.2 %collective-permute-start.7 = (f32[2,384,128]{2,1,0:T(8,128)S(1)}, f32[2,384,128]{2,1,0:T(8,128)S(1)}, u32[]{:S(2)}, u32[]{:S(2)}) collective-permute-start(f32[2,384,128]{2,1,0:T(8,128)S(1)} %shard_map.117), channel_id=1, source_target_pairs={{0,1},{1,2},{2,3},{3,4},{4,5},{5,6},{6,7},{7,8},{8,9},{9,10},{10,1... | collective-permute-start | bytes 1179656 | tf_op jit(solution)/shard_map/ppermute | solution.py:288
where the time goes:
time: 172 us; the launch traced here: 171 us
  blocking collectives  60.5 us (35%)
  starting transfers between devices  48.9 us (28%)
  waiting for transfers between devices  38.7 us (23%)
  Pallas kernels  15.4 us (9%)
  local copies, waits for them, and re-layouts  5.79 us (3%)
    all_to_all x2, blocking collectives, exchanged(): return lax.all_to_all(parts, axes, 0, 0, tiled=False)  60.5 us
    ppermute x8, starting transfers between devices, passed_along(): return lax.ppermute(block, axis, route)  39.3 us
    ppermute x8, waiting for transfers between devices, passed_along(): return lax.ppermute(block, axis, route)  33.3 us
    pallas_call x7, Pallas kernels, call(): pl.pallas_call(kernel, out_shape=shapes, in_specs=[smem] * len(scalars) +...  15.4 us
    all_to_all x1, starting transfers between devices, exchanged(): return lax.all_to_all(parts, axes, 0, 0, tiled=False)  5.85 us
    ppermute x2, starting transfers between devices, swapped(): return lax.ppermute(block, CORE, [(0, 1), (1, 0)])  3.83 us
    all_to_all x1, waiting for transfers between devices, exchanged(): return lax.all_to_all(parts, axes, 0, 0, tiled=False)  3.5 us
  transfers between devices with their start and end apart: 11, of which 8 were waited for; matrix products, arithmetic and copies ran while one was open for 1% of the time, Pallas kernels for 2%

commit v1 on v0

--- a/solution.py
+++ b/solution.py
@@ -18,7 +18,6 @@
 ROW = ("row_0", "row_1")
 COL = ("col_0", "col_1", "col_2")
 PLANE = ("row_0", "col_1")
-DEPTH = ("row_1", "col_0")
 CORE = "col_2"
 
 
@@ -35,15 +34,11 @@
     sine = -np.sin(angle) / 16.0
     forward = np.block([[cosine, -sine], [sine, cosine]])
     high, low = halves(forward)
-    left = np.concatenate([high, high, low], axis=1)
-    left_t = np.concatenate([high.T, high.T, low.T], axis=1)
-    right = np.concatenate([high, high, low], axis=0)
-    right_t = np.concatenate([high.T, high.T, low.T], axis=0)
     turn = 2.0 * np.pi * index / WIN
     twiddle = np.stack([np.cos(turn), -np.sin(turn)]).astype(np.float32)
     rows = np.ascontiguousarray(np.broadcast_to(twiddle[:, :, None], (2, HALF, HALF)))
     cols = np.ascontiguousarray(np.broadcast_to(twiddle[:, None, :], (2, 8, HALF)))
-    return left, left_t, right, right_t, rows, cols
+    return high, low, np.ascontiguousarray(high.T), np.ascontiguousarray(low.T), rows, cols
 
 
 def split3(x, axis):
@@ -98,8 +93,16 @@
     return real, imag
 
 
+def left_of(high, low):
+    return jnp.concatenate([high[...], high[...], low[...]], axis=1)
+
+
+def right_of(high, low):
+    return jnp.concatenate([high[...], high[...], low[...]], axis=0)
+
+
 def window_fit(window, probe, amplitude, tables, far, window_ref, gradient, add_probe):
-    left, left_t, right, right_t, rows, cols = tables
+    high, low, high_t, low_t, rows, cols = tables
     window_ref[0] = window[0]
     window_ref[1] = window[1]
 
@@ -112,7 +115,8 @@
         twr, twc = twiddles()
         w_r, w_i = window_ref[0], window_ref[1]
         p_r, p_i = probe[m, 0], probe[m, 1]
-        f_r, f_i = forward_dft(p_r * w_r - p_i * w_i, p_r * w_i + p_i * w_r, left[...], right_t[...], twr, twc)
+        f_r, f_i = forward_dft(p_r * w_r - p_i * w_i, p_r * w_i + p_i * w_r,
+                               left_of(high, low), right_of(high_t, low_t), twr, twc)
         far[m, 0] = f_r
         far[m, 1] = f_i
         return carry
@@ -128,7 +132,7 @@
 
     def inward(m, carry):
         twr, twc = twiddles()
-        x_r, x_i = inverse_dft(far[m, 0], far[m, 1], left_t[...], right[...], twr, twc)
+        x_r, x_i = inverse_dft(far[m, 0], far[m, 1], left_of(high_t, low_t), right_of(high, low), twr, twc)
         w_r, w_i = window_ref[0], window_ref[1]
         p_r, p_i = probe[m, 0], probe[m, 1]
         gradient[0] += p_r * x_r + p_i * x_i
@@ -162,7 +166,7 @@
 WIDE = WIN + HALO
 
 
-def first_kernel(pos, above, obj, halo, probe, amp, step, left, left_t, right, right_t, rows, cols,
+def first_kernel(pos, obj, halo, probe, amp, step, high, low, high_t, low_t, rows, cols,
                  new_obj, spill, edge, middle, probe_sum, far, win, grad):
     row, col = pos[0, 0], pos[0, 1]
 
@@ -175,7 +179,7 @@
         probe_sum[m, 0] = real
         probe_sum[m, 1] = imag
 
-    window_fit((cut(0), cut(1)), probe, amp[0], (left, left_t, right, right_t, rows, cols), far, win, grad, add_probe)
+    window_fit((cut(0), cut(1)), probe, amp[0], (high, low, high_t, low_t, rows, cols), far, win, grad, add_probe)
     scale = step[:1, :1]
     for k in range(2):
         g = jnp.concatenate([grad[k] * scale, jnp.zeros((TILE_R - WIN, WIN), jnp.float32)], axis=0)
@@ -193,18 +197,18 @@
     return lax.broadcasted_iota(jnp.int32, (HALO, HALO), 1)
 
 
-def upward_kernel(info, edge, from_left, from_right, spill, upward):
-    keep = info[1].astype(jnp.float32)
+def upward_kernel(above, info, edge, from_left, from_right, spill, upward):
+    keep = info[0].astype(jnp.float32)
     for k in range(2):
         own = edge[k, :HALO] + from_left[k, :HALO]
-        upward[k] = jnp.where(lanes() >= info[0], own, from_right[k, :HALO] + spill[k, :HALO] * keep)
+        upward[k] = jnp.where(lanes() >= above[1, 1], own, from_right[k, :HALO] + spill[k, :HALO] * keep)
 
 
 def second_kernel(pos, info, obj, from_left, from_right, spill, below_mid, below_rest, probe, amp, step, probe_in,
-                  left, left_t, right, right_t, rows, cols,
+                  high, low, high_t, low_t, rows, cols,
                   new_obj, new_spill, downward, keep_sum, send_sum, far, win, grad):
     row, col = pos[1, 0] - LAST, pos[1, 1]
-    keep, core = info[1].astype(jnp.float32), info[2]
+    keep, core = info[0].astype(jnp.float32), info[1]
 
     def cut(k):
         upper = jnp.concatenate(
@@ -225,39 +229,36 @@
             send_sum[0] = probe_in[m, 0] + real
             send_sum[1] = probe_in[m, 1] + imag
 
-    window_fit((cut(0), cut(1)), probe, amp[1], (left, left_t, right, right_t, rows, cols), far, win, grad, add_probe)
+    window_fit((cut(0), cut(1)), probe, amp[1], (high, low, high_t, low_t, rows, cols), far, win, grad, add_probe)
     scale = step[:1, :1]
     for k in range(2):
         g = jnp.concatenate([grad[k] * scale, jnp.zeros((TILE_R - WIN, WIN), jnp.float32)], axis=0)
         g = pltpu.roll(g, row, 0)
         g = jnp.concatenate([g, jnp.zeros((TILE_R, HALO), jnp.float32)], axis=1)
         g = pltpu.roll(g, col, 1)
-        downward[k, :, :HALO] = g[WIN:, :HALO] + g[WIN:, WIN:]
-        downward[k, :, HALO:] = g[WIN:, HALO:WIN]
+        downward[k] = g[WIN:, :WIN]
         new_obj[k, :LAST, :HALO] = obj[k, :LAST, :HALO] + from_left[k, :LAST]
         new_obj[k, :LAST, HALO:] = obj[k, :LAST, HALO:]
         new_obj[k, LAST:, :HALO] = obj[k, LAST:, :HALO] + from_left[k, LAST:] + g[:WIN, :HALO]
         new_obj[k, LAST:, HALO:] = obj[k, LAST:, HALO:] + g[:WIN, HALO:WIN]
-        new_spill[k] = g[:WIN, WIN:]
-
-
-def spill_kernel(info, spill, from_above, new_spill):
-    for k in range(2):
-        new_spill[k, :HALO] = jnp.where(lanes() < info[0], from_above[k, :, :HALO], 0.0)
-        new_spill[k, HALO:] = spill[k]
-
-
-def object_kernel(info, obj, from_above, from_left, out):
-    for k in range(2):
-        fell = jnp.where(lanes() >= info[0], from_above[k, :, :HALO], 0.0)
-        out[k, :HALO, :HALO] = obj[k, :HALO, :HALO] + fell + from_left[k, :HALO]
-        out[k, HALO:, :HALO] = obj[k, HALO:, :HALO] + from_left[k, HALO:]
-        out[k, :HALO, HALO:] = obj[k, :HALO, HALO:] + from_above[k, :, HALO:]
-        out[k, HALO:, HALO:] = obj[k, HALO:, HALO:]
+        new_spill[k] = g[:, WIN:]
+
+
+def down_kernel(downward, from_left, out):
+    for k in range(2):
+        out[k, :, :HALO] = downward[k, :, :HALO] + from_left[k, WIN:]
+        out[k, :, HALO:] = downward[k, :, HALO:]
+
+
+def object_kernel(obj, from_left, from_above, out):
+    for k in range(2):
+        out[k, :LAST] = obj[k, :LAST] + from_above[k]
+        out[k, LAST:, :HALO] = obj[k, LAST:, :HALO] + from_left[k, :WIN]
+        out[k, LAST:, HALO:] = obj[k, LAST:, HALO:]
 
 
 def probe_kernel(info, probe, own, other, out):
-    core = info[2]
+    core = info[1]
     out[core] = probe[core] + own[...]
     out[1 - core] = probe[1 - core] + other[...]
 
@@ -297,12 +298,14 @@
 
 
 def summed_everywhere(keep, send, divisor):
-    plane, depth = lax.axis_size(PLANE), lax.axis_size(DEPTH)
+    plane = lax.axis_size(PLANE)
     mode = keep + swapped(send)
     parts = exchanged(mode.reshape(plane, -1, WIN), PLANE)
     share = jnp.sum(parts, axis=0)
-    parts = exchanged(jnp.broadcast_to(share, (depth, *share.shape)), DEPTH)
-    share = jnp.sum(parts, axis=0) / divisor
+    for axis in ("col_0", "row_1"):
+        parts = exchanged(jnp.broadcast_to(share, (lax.axis_size(axis), *share.shape)), axis)
+        share = jnp.sum(parts, axis=0)
+    share = share / divisor
     mode = exchanged(jnp.broadcast_to(share, (plane, *share.shape)), PLANE).reshape(2, WIN, WIN)
     return mode, swapped(mode)
 
@@ -319,24 +322,24 @@
 
     halo = passed_along(object_field[:, :, :HALO], COL, -1)
     above = passed_along(positions, ROW, 1)
-    info = jnp.stack([above[1, 1], has_right, lax.axis_index(CORE)])
+    info = jnp.stack([has_right, lax.axis_index(CORE)])
     amp, step = call(before_kernel, [(BATCHES, WIN, WIN), (8, HALF)], [], [], probe_modes, amplitudes[0, 0])
     obj, spill, edge, middle, probe_sum = call(
-        first_kernel, [tile, side, side, block, probe_shape], fit_scratch, [positions, info],
+        first_kernel, [tile, side, side, block, probe_shape], fit_scratch, [positions],
         object_field, halo, probe_modes, amp, step, *tables)
     from_left = passed_along(spill, COL, 1)
     from_right = passed_along(edge, COL, -1)
     below_mid = passed_along(middle, ROW, -1)
-    (upward,) = call(upward_kernel, [block], [], [info], edge, from_left, from_right, spill)
+    (upward,) = call(upward_kernel, [block], [], [above, info], edge, from_left, from_right, spill)
     below_rest = passed_along(upward, ROW, -1)
     obj, spill, downward, keep, send = call(
-        second_kernel, [tile, (2, WIN, HALO), (2, HALO, WIN), (2, WIN, WIN), (2, WIN, WIN)], fit_scratch, [positions, info],
+        second_kernel, [tile, side, (2, HALO, WIN), (2, WIN, WIN), (2, WIN, WIN)], fit_scratch, [positions, info],
         obj, from_left, from_right, spill, below_mid, below_rest, probe_modes, amp, step, probe_sum, *tables)
+    own, other = summed_everywhere(keep, send, divisor)
+    from_left = passed_along(spill, COL, 1)
+    (downward,) = call(down_kernel, [(2, HALO, WIN)], [], [], downward, from_left)
     from_above = passed_along(downward, ROW, 1)
-    own, other = summed_everywhere(keep, send, divisor)
-    (spill,) = call(spill_kernel, [side], [], [info], spill, from_above)
-    from_left = passed_along(spill, COL, 1)
-    (object_out,) = call(object_kernel, [tile], [], [info], obj, from_above, from_left, last=True)
+    (object_out,) = call(object_kernel, [tile], [], [], obj, from_left, from_above, last=True)
     (probe_out,) = call(probe_kernel, [probe_shape], [], [info], probe_modes, own, other, last=True)
     return (object_out, probe_out)
 

time: 172 us -> 177 us (1.029)
  the two profiles are of different devices: /device:TPU:120 before, /device:TPU:25 now
where the time goes in v1:
time: 177 us; the launch traced here: 176 us
  starting transfers between devices  56.3 us (32%)
  blocking collectives  47.3 us (27%)
  waiting for transfers between devices  46.7 us (26%)
  Pallas kernels  14.9 us (8%)
  local copies, waits for them, and re-layouts  9.66 us (5%)
    all_to_all x3, blocking collectives, exchanged(): return lax.all_to_all(parts, axes, 0, 0, tiled=False)  47.3 us
    ppermute x8, waiting for transfers between devices, passed_along(): return lax.ppermute(block, axis, route)  44.8 us
    ppermute x8, starting transfers between devices, passed_along(): return lax.ppermute(block, axis, route)  41.6 us
    pallas_call x7, Pallas kernels, call(): pl.pallas_call(kernel, out_shape=shapes, in_specs=[smem] * len(scalars) +...  14.9 us
    ppermute x2, starting transfers between devices, swapped(): return lax.ppermute(block, CORE, [(0, 1), (1, 0)])  9.02 us
    unnamed x46, local copies, waits for them, and re-layouts  7.7 us
    all_to_all x1, starting transfers between devices, exchanged(): return lax.all_to_all(parts, axes, 0, 0, tiled=False)  5.68 us
  transfers between devices with their start and end apart: 11, of which 5 were waited for; matrix products, arithmetic and copies ran while one was open for 0% of the time, Pallas kernels for 1%

profile of v1, /device:TPU:25, one launch (start us, length us, event | category | flops | bytes accessed | tf_op | source)
XLA Modules:
  0.0 176.1 jit_solution(3630463916611783110)
XLA Ops:
  0.6 0.0 copy-start.2
  0.6 1.1 slice.3
  1.7 2.6 %collective-permute-start = (f32[2,384,128]{2,1,0:T(8,128)S(1)}, f32[2,384,128]{2,1,0:T(8,128)S(1)}, u32[]{:S(2)}, u32[]{:S(2)}) collective-permute-start(f32[2,384,128]{2,1,0:T(8,128)S(1)} %slice.3), channel_id=1, source_target_pairs={{1,0},{2,1},{3,2},{4,3},{5,4},{6,5},{7,6},{8,7},{9,8},{10,9},{11,1... | collective-permute-start | bytes 1179656 | tf_op jit(solution)/shard_map/ppermute | solution.py:289
  4.3 0.0 copy-start
  4.3 1.2 copy-done
  5.6 0.9 copy-done.17
  6.5 0.0 copy-start.15
  6.5 0.0 copy-start.20
  6.5 0.4 shard_map.113
  7.0 3.9 %collective-permute-done.halo = f32[2,384,128]{2,1,0:T(8,128)S(1)} collective-permute-done((f32[2,384,128]{2,1,0:T(8,128)S(1)}, f32[2,384,128]{2,1,0:T(8,128)S(1)}, u32[]{:S(2)}, u32[]{:S(2)}) %collective-permute-start) | collective-permute-done | bytes 393248 | tf_op jit(solution)/shard_map/ppermute | solution.py:289
  10.9 0.0 copy-done.2
  10.9 0.0 copy-done.7
  10.9 0.0 copy-done.9
  10.9 0.0 copy-done.11
  10.9 0.0 copy-done.13
  10.9 0.0 copy-done.15
  10.9 0.0 copy-done.20
  10.9 0.6 copy-done.21
  11.6 5.2 %shard_map.114 = (f32[2,384,256]{2,1,0:T(8,128)S(1)}, f32[2,384,128]{2,1,0:T(8,128)S(1)}, f32[2,384,128]{2,1,0:T(8,128)S(1)}, f32[2,128,128]{2,1,0:T(8,128)S(1)}, f32[2,2,256,256]{3,2,1,0:T(8,128)S(1)}) custom-call(s32[2,2]{1,0:T(2,128)S(1)} %bitcast.9, f32[2,384,256]{2,1,0:T(8,128)S(1)} %copy-done.2, f32[2,384,128]{2,1,0:T(8,128)S(1)} %collective-permute-done.halo, ...), custom_call_target="tpu_custom_call" | custom-call | tf_op jit(solution)/shard_map/pallas_call | solution.py:275
  16.8 0.0 copy-start.3
  16.8 1.0 copy-done.3
  17.8 0.9 copy-done.5
  18.7 2.0 %collective-permute-start.2 = (f32[2,384,128]{2,1,0:T(8,128)S(1)}, f32[2,384,128]{2,1,0:T(8,128)S(1)}, u32[]{:S(2)}, u32[]{:S(2)}) collective-permute-start(f32[2,384,128]{2,1,0:T(8,128)S(1)} %get-tuple-element.18.edge), channel_id=1, source_target_pairs={{1,0},{2,1},{3,2},{4,3},{5,4},{6,5},{7,6},{8,7},{9,8},{10,9},{11,1... | collective-permute-start | bytes 1179656 | tf_op jit(solution)/shard_map/ppermute | solution.py:289
  20.7 3.6 %collective-permute-start.1 = (f32[2,384,128]{2,1,0:T(8,128)S(1)}, f32[2,384,128]{2,1,0:T(8,128)S(1)}, u32[]{:S(2)}, u32[]{:S(2)}) collective-permute-start(f32[2,384,128]{2,1,0:T(8,128)S(1)} %get-tuple-element.17.spill), channel_id=1, source_target_pairs={{0,1},{1,2},{2,3},{3,4},{4,5},{5,6},{6,7},{7,8},{8,9},{9,10},{10,1... | collective-permute-start | bytes 1179656 | tf_op jit(solution)/shard_map/ppermute | solution.py:289
  24.4 8.8 %collective-permute-start.4 = (s32[2,2]{1,0:T(2,128)S(1)}, s32[2,2]{1,0:T(2,128)S(1)}, u32[]{:S(2)}, u32[]{:S(2)}) collective-permute-start(s32[2,2]{1,0:T(2,128)S(1)} %bitcast.10), channel_id=1, source_target_pairs={{0,32},{32,64},{64,96},{96,128},{128,160},{160,192},{192,224},{224... | collective-permute-start | bytes 56 | tf_op jit(solution)/shard_map/ppermute | solution.py:289
  33.2 0.1 pad_add_fusion.info
  33.3 0.0 copy-start.16
  33.3 5.9 %collective-permute-start.3 = (f32[2,128,128]{2,1,0:T(8,128)S(1)}, f32[2,128,128]{2,1,0:T(8,128)S(1)}, u32[]{:S(2)}, u32[]{:S(2)}) collective-permute-start(f32[2,128,128]{2,1,0:T(8,128)S(1)} %get-tuple-element.19), channel_id=1, source_target_pairs={{32,0},{64,32},{96,64},{128,96},{160,128},{192,160},{224,192},{256... | collective-permute-start | bytes 393224 | tf_op jit(solution)/shard_map/ppermute | solution.py:289
  39.2 0.0 collective-permute-done.4.above
  39.2 0.0 collective-permute-done.2.from_right
  39.2 0.0 collective-permute-done.1.from_left
  39.2 0.6 shard_map.115
  39.8 7.3 %collective-permute-start.5 = (f32[2,128,128]{2,1,0:T(8,128)S(1)}, f32[2,128,128]{2,1,0:T(8,128)S(1)}, u32[]{:S(2)}, u32[]{:S(2)}) collective-permute-start(f32[2,128,128]{2,1,0:T(8,128)S(1)} %shard_map.115), channel_id=1, source_target_pairs={{32,0},{64,32},{96,64},{128,96},{160,128},{192,160},{224,192},{256... | collective-permute-start | bytes 393224 | tf_op jit(solution)/shard_map/ppermute | solution.py:289
  47.1 6.6 %collective-permute-done.3.below_mid = f32[2,128,128]{2,1,0:T(8,128)S(1)} collective-permute-done((f32[2,128,128]{2,1,0:T(8,128)S(1)}, f32[2,128,128]{2,1,0:T(8,128)S(1)}, u32[]{:S(2)}, u32[]{:S(2)}) %collective-permute-start.3) | collective-permute-done | bytes 131104 | tf_op jit(solution)/shard_map/ppermute | solution.py:289
  53.6 6.9 %collective-permute-done.5.below_rest = f32[2,128,128]{2,1,0:T(8,128)S(1)} collective-permute-done((f32[2,128,128]{2,1,0:T(8,128)S(1)}, f32[2,128,128]{2,1,0:T(8,128)S(1)}, u32[]{:S(2)}, u32[]{:S(2)}) %collective-permute-start.5) | collective-permute-done | bytes 131104 | tf_op jit(solution)/shard_map/ppermute | solution.py:289
  60.5 0.0 copy-done.1
  60.5 0.0 copy-done.8
  60.5 0.0 copy-done.10
  60.5 0.0 copy-done.12
  60.5 0.0 copy-done.14
  60.5 0.0 copy-done.16
  60.6 0.6 copy-done.22
  61.2 1.2 copy-done.4
  62.4 1.1 copy-done.6
  63.6 6.1 %shard_map.116 = (f32[2,384,256]{2,1,0:T(8,128)S(1)}, f32[2,384,128]{2,1,0:T(8,128)}, f32[2,128,256]{2,1,0:T(8,128)S(1)}, f32[2,256,256]{2,1,0:T(8,128)S(1)}, f32[2,256,256]{2,1,0:T(8,128)S(1)}) custom-call(s32[2,2]{1,0:T(2,128)S(1)} %bitcast.11, s32[2]{0:T(128)S(1)} %pad_add_fusion.info, f32[2,384,256]{2,1,0:T(8,128)S(1)} %copy-done.6, ...), custom_call_target="tpu_custom_call" | custom-call | tf_op jit(solution)/shard_map/pallas_call | solution.py:275
  69.7 1.9 %collective-permute-start.8 = (f32[2,256,256]{2,1,0:T(8,128)S(1)}, f32[2,256,256]{2,1,0:T(8,128)S(1)}, u32[]{:S(2)}, u32[]{:S(2)}) collective-permute-start(f32[2,256,256]{2,1,0:T(8,128)S(1)} %get-tuple-element.25), channel_id=1, source_target_pairs={{0,1},{1,0},{2,3},{3,2},{4,5},{5,4},{6,7},{7,6},{8,9},{9,8},{10,11... | collective-permute-start | bytes 1572872 | tf_op jit(solution)/shard_map/ppermute | solution.py:297
  71.6 1.9 %collective-permute-done.8 = f32[2,256,256]{2,1,0:T(8,128)S(1)} collective-permute-done((f32[2,256,256]{2,1,0:T(8,128)S(1)}, f32[2,256,256]{2,1,0:T(8,128)S(1)}, u32[]{:S(2)}, u32[]{:S(2)}) %collective-permute-start.8) | collective-permute-done | bytes 524320 | tf_op jit(solution)/shard_map/ppermute | solution.py:297
  73.5 0.1 add.11
  73.5 0.0 copy-done.18
  73.5 20.2 %all_to_all.20 = f32[16,32,256]{2,1,0:T(8,128)S(1)} all-to-all(f32[16,32,256]{2,1,0:T(8,128)S(1)} %bitcast.12), channel_id=1, replica_groups=mesh['row_0'=4,'row_1'=4,'col_0'=4,'col_1'=4,'col_2'=2] {'row_0','col_1'}, dimensions={0} | all-to-all | bytes 1048576 | tf_op jit(solution)/shard_map/all_to_all | solution.py:293
  93.8 7.2 %all_to_all.21 = f32[4,32,256]{2,1,0:T(8,128)S(1)} all-to-all(f32[4,32,256]{2,1,0:T(8,128)S(1)} %broadcast_in_dim.9), channel_id=1, replica_groups=mesh['row_0'=4,'row_1'=4,'col_0'=4,'col_1'=4,'col_2'=2] {'col_0'}, dimensions={0} | all-to-all | bytes 262144 | tf_op jit(solution)/shard_map/all_to_all | solution.py:293
  101.0 19.9 %all_to_all.22 = f32[4,32,256]{2,1,0:T(8,128)S(1)} all-to-all(f32[4,32,256]{2,1,0:T(8,128)S(1)} %broadcast_in_dim.10), channel_id=1, replica_groups=mesh['row_0'=4,'row_1'=4,'col_0'=4,'col_1'=4,'col_2'=2] {'row_1'}, dimensions={0} | all-to-all | bytes 262144 | tf_op jit(solution)/shard_map/all_to_all | solution.py:293
  120.9 0.8 broadcast_in_dim.11
  121.8 5.7 %all-to-all-start.3 = ((f32[16,32,256]{2,1,0:T(8,128)}), f32[16,32,256]{2,1,0:T(8,128)S(1)}, u32[]{:S(2)}, u32[]{:S(2)}) async-start(f32[16,32,256]{2,1,0:T(8,128)} %broadcast_in_dim.11), calls=%async_computation.3 | async-start | bytes 1048576 | tf_op jit(solution)/shard_map/all_to_all | solution.py:293
  127.4 7.7 %collective-permute-start.6 = (f32[2,384,128]{2,1,0:T(8,128)}, f32[2,384,128]{2,1,0:T(8,128)S(1)}, u32[]{:S(2)}, u32[]{:S(2)}) collective-permute-start(f32[2,384,128]{2,1,0:T(8,128)} %get-tuple-element.22), channel_id=1, source_target_pairs={{0,1},{1,2},{2,3},{3,4},{4,5},{5,6},{6,7},{7,8},{8,9},{9,10},{10,1... | collective-permute-start | bytes 1179656 | tf_op jit(solution)/shard_map/ppermute | solution.py:289
  135.1 0.0 all-to-all-done.3
  135.1 7.1 %collective-permute-start.9 = (f32[2,256,256]{2,1,0:T(8,128)S(1)}, f32[2,256,256]{2,1,0:T(8,128)S(1)}, u32[]{:S(2)}, u32[]{:S(2)}) collective-permute-start(f32[2,256,256]{2,1,0:T(8,128)S(1)} %bitcast.6), channel_id=1, source_target_pairs={{0,1},{1,0},{2,3},{3,2},{4,5},{5,4},{6,7},{7,6},{8,9},{9,8},{10,11... | collective-permute-start | bytes 1572872 | tf_op jit(solution)/shard_map/ppermute | solution.py:297
  142.2 0.0 collective-permute-done.6.from_left
  142.2 0.0 copy-done.19
  142.3 3.8 %collective-permute-start.7 = (f32[2,128,256]{2,1,0:T(8,128)S(1)}, f32[2,128,256]{2,1,0:T(8,128)S(1)}, u32[]{:S(2)}, u32[]{:S(2)}) collective-permute-start(f32[2,128,256]{2,1,0:T(8,128)S(1)} %shard_map.117), channel_id=1, source_target_pairs={{0,32},{32,64},{64,96},{96,128},{128,160},{160,192},{192,224},{224... | collective-permute-start | bytes 786440 | tf_op jit(solution)/shard_map/ppermute | solution.py:289
  146.0 27.4 %collective-permute-done.7.from_above = f32[2,128,256]{2,1,0:T(8,128)S(1)} collective-permute-done((f32[2,128,256]{2,1,0:T(8,128)S(1)}, f32[2,128,256]{2,1,0:T(8,128)S(1)}, u32[]{:S(2)}, u32[]{:S(2)}) %collective-permute-start.7) | collective-permute-done | bytes 262176 | tf_op jit(solution)/shard_map/ppermute | solution.py:289
  173.5 0.9 shard_map.118
  174.4 0.0 collective-permute-done.9.other
  174.4 1.6 shard_map.119
  (24 shorter events, 0.1 us)
Async XLA Ops:
  0.6 10.2 %copy-start.2 = (f32[2,384,256]{2,1,0:T(8,128)S(1)}, f32[2,384,256]{2,1,0:T(8,128)}, u32[]{:S(2)}) copy-start(f32[2,384,256]{2,1,0:T(8,128)} %obj.1) | copy-start | bytes 2359300
  1.7 9.1 %collective-permute-start = (f32[2,384,128]{2,1,0:T(8,128)S(1)}, f32[2,384,128]{2,1,0:T(8,128)S(1)}, u32[]{:S(2)}, u32[]{:S(2)}) collective-permute-start(f32[2,384,128]{2,1,0:T(8,128)S(1)} %slice.3), channel_id=1, source_target_pairs={{1,0},{2,1},{3,2},{4,3},{5,4},{6,5},{7,6},{8,7},{9,8},{10,9},{11,1... | collective-permute-start | bytes 1179656 | tf_op jit(solution)/shard_map/ppermute | solution.py:289
  4.3 1.2 copy-start
  5.6 0.9 copy-start.17
  6.5 4.4 %copy-start.7 = (f32[2,128,128]{2,1,0:T(8,128)S(1)}, f32[2,128,128]{2,1,0:T(8,128)}, u32[]{:S(2)}) copy-start(f32[2,128,128]{2,1,0:T(8,128)} %constant.38.clone.rows) | copy-start | bytes 393220
  6.5 4.4 %copy-start.9 = (bf16[256,256]{1,0:T(8,128)(2,1)S(1)}, bf16[256,256]{1,0:T(8,128)(2,1)}, u32[]{:S(2)}) copy-start(bf16[256,256]{1,0:T(8,128)(2,1)} %constant.37.clone.low_t) | copy-start | bytes 393220
  6.5 4.4 %copy-start.11 = (bf16[256,256]{1,0:T(8,128)(2,1)S(1)}, bf16[256,256]{1,0:T(8,128)(2,1)}, u32[]{:S(2)}) copy-start(bf16[256,256]{1,0:T(8,128)(2,1)} %constant.36.clone.high_t) | copy-start | bytes 393220
  6.5 4.4 %copy-start.13 = (bf16[256,256]{1,0:T(8,128)(2,1)S(1)}, bf16[256,256]{1,0:T(8,128)(2,1)}, u32[]{:S(2)}) copy-start(bf16[256,256]{1,0:T(8,128)(2,1)} %constant.35.clone.low) | copy-start | bytes 393220
  6.5 4.4 %copy-start.15 = (bf16[256,256]{1,0:T(8,128)(2,1)S(1)}, bf16[256,256]{1,0:T(8,128)(2,1)}, u32[]{:S(2)}) copy-start(bf16[256,256]{1,0:T(8,128)(2,1)} %constant.34.clone.high) | copy-start | bytes 393220
  6.5 4.4 %copy-start.20 = (f32[2,8,128]{2,1,0:T(8,128)S(1)}, f32[2,8,128]{2,1,0:T(8,128)}, u32[]{:S(2)}) copy-start(f32[2,8,128]{2,1,0:T(8,128)} %constant.39.clone.cols) | copy-start | bytes 24580
  10.9 0.7 copy-start.21
  16.8 1.0 copy-start.3
  17.8 0.9 copy-start.5
  18.7 41.9 %copy-start.1 = (f32[2,2,256,256]{3,2,1,0:T(8,128)S(1)}, f32[2,2,256,256]{3,2,1,0:T(8,128)}, u32[]{:S(2)}) copy-start(f32[2,2,256,256]{3,2,1,0:T(8,128)} %probe.7) | copy-start | bytes 3145732
  18.7 20.5 %collective-permute-start.2 = (f32[2,384,128]{2,1,0:T(8,128)S(1)}, f32[2,384,128]{2,1,0:T(8,128)S(1)}, u32[]{:S(2)}, u32[]{:S(2)}) collective-permute-start(f32[2,384,128]{2,1,0:T(8,128)S(1)} %get-tuple-element.18.edge), channel_id=1, source_target_pairs={{1,0},{2,1},{3,2},{4,3},{5,4},{6,5},{7,6},{8,7},{9,8},{10,9},{11,1... | collective-permute-start | bytes 1179656 | tf_op jit(solution)/shard_map/ppermute | solution.py:289
  20.7 18.5 %collective-permute-start.1 = (f32[2,384,128]{2,1,0:T(8,128)S(1)}, f32[2,384,128]{2,1,0:T(8,128)S(1)}, u32[]{:S(2)}, u32[]{:S(2)}) collective-permute-start(f32[2,384,128]{2,1,0:T(8,128)S(1)} %get-tuple-element.17.spill), channel_id=1, source_target_pairs={{0,1},{1,2},{2,3},{3,4},{4,5},{5,6},{6,7},{7,8},{8,9},{9,10},{10,1... | collective-permute-start | bytes 1179656 | tf_op jit(solution)/shard_map/ppermute | solution.py:289
  24.4 14.8 %collective-permute-start.4 = (s32[2,2]{1,0:T(2,128)S(1)}, s32[2,2]{1,0:T(2,128)S(1)}, u32[]{:S(2)}, u32[]{:S(2)}) collective-permute-start(s32[2,2]{1,0:T(2,128)S(1)} %bitcast.10), channel_id=1, source_target_pairs={{0,32},{32,64},{64,96},{96,128},{128,160},{160,192},{192,224},{224... | collective-permute-start | bytes 56 | tf_op jit(solution)/shard_map/ppermute | solution.py:289
  33.3 27.3 %copy-start.8 = (f32[2,128,128]{2,1,0:T(8,128)S(1)}, f32[2,128,128]{2,1,0:T(8,128)}, u32[]{:S(2)}) copy-start(f32[2,128,128]{2,1,0:T(8,128)} %constant.38.clone.rows) | copy-start | bytes 393220
  33.3 27.3 %copy-start.10 = (bf16[256,256]{1,0:T(8,128)(2,1)S(1)}, bf16[256,256]{1,0:T(8,128)(2,1)}, u32[]{:S(2)}) copy-start(bf16[256,256]{1,0:T(8,128)(2,1)} %constant.37.clone.low_t) | copy-start | bytes 393220
  33.3 27.3 %copy-start.12 = (bf16[256,256]{1,0:T(8,128)(2,1)S(1)}, bf16[256,256]{1,0:T(8,128)(2,1)}, u32[]{:S(2)}) copy-start(bf16[256,256]{1,0:T(8,128)(2,1)} %constant.36.clone.high_t) | copy-start | bytes 393220
  33.3 27.3 %copy-start.14 = (bf16[256,256]{1,0:T(8,128)(2,1)S(1)}, bf16[256,256]{1,0:T(8,128)(2,1)}, u32[]{:S(2)}) copy-start(bf16[256,256]{1,0:T(8,128)(2,1)} %constant.35.clone.low) | copy-start | bytes 393220
  33.3 27.3 %copy-start.16 = (bf16[256,256]{1,0:T(8,128)(2,1)S(1)}, bf16[256,256]{1,0:T(8,128)(2,1)}, u32[]{:S(2)}) copy-start(bf16[256,256]{1,0:T(8,128)(2,1)} %constant.34.clone.high) | copy-start | bytes 393220
  33.3 20.3 %collective-permute-start.3 = (f32[2,128,128]{2,1,0:T(8,128)S(1)}, f32[2,128,128]{2,1,0:T(8,128)S(1)}, u32[]{:S(2)}, u32[]{:S(2)}) collective-permute-start(f32[2,128,128]{2,1,0:T(8,128)S(1)} %get-tuple-element.19), channel_id=1, source_target_pairs={{32,0},{64,32},{96,64},{128,96},{160,128},{192,160},{224,192},{256... | collective-permute-start | bytes 393224 | tf_op jit(solution)/shard_map/ppermute | solution.py:289
  39.8 20.7 %collective-permute-start.5 = (f32[2,128,128]{2,1,0:T(8,128)S(1)}, f32[2,128,128]{2,1,0:T(8,128)S(1)}, u32[]{:S(2)}, u32[]{:S(2)}) collective-permute-start(f32[2,128,128]{2,1,0:T(8,128)S(1)} %shard_map.115), channel_id=1, source_target_pairs={{32,0},{64,32},{96,64},{128,96},{160,128},{192,160},{224,192},{256... | collective-permute-start | bytes 393224 | tf_op jit(solution)/shard_map/ppermute | solution.py:289
  60.5 0.7 copy-start.22
  61.2 1.2 copy-start.4
  62.4 1.1 copy-start.6
  69.7 3.9 %copy-start.18 = (f32[2,128,256]{2,1,0:T(8,128)}, f32[2,128,256]{2,1,0:T(8,128)S(1)}, u32[]{:S(2)}) copy-start(f32[2,128,256]{2,1,0:T(8,128)S(1)} %get-tuple-element.23.downward) | copy-start | bytes 786436
  69.7 3.8 %collective-permute-start.8 = (f32[2,256,256]{2,1,0:T(8,128)S(1)}, f32[2,256,256]{2,1,0:T(8,128)S(1)}, u32[]{:S(2)}, u32[]{:S(2)}) collective-permute-start(f32[2,256,256]{2,1,0:T(8,128)S(1)} %get-tuple-element.25), channel_id=1, source_target_pairs={{0,1},{1,0},{2,3},{3,2},{4,5},{5,4},{6,7},{7,6},{8,9},{9,8},{10,11... | collective-permute-start | bytes 1572872 | tf_op jit(solution)/shard_map/ppermute | solution.py:297
  121.7 20.5 %copy-start.19 = (f32[2,128,256]{2,1,0:T(8,128)S(1)}, f32[2,128,256]{2,1,0:T(8,128)}, u32[]{:S(2)}) copy-start(f32[2,128,256]{2,1,0:T(8,128)} %copy-done.18) | copy-start | bytes 786436
  121.8 13.3 %all-to-all-start.3 = ((f32[16,32,256]{2,1,0:T(8,128)}), f32[16,32,256]{2,1,0:T(8,128)S(1)}, u32[]{:S(2)}, u32[]{:S(2)}) async-start(f32[16,32,256]{2,1,0:T(8,128)} %broadcast_in_dim.11), calls=%async_computation.3 | async-start | bytes 1048576 | tf_op jit(solution)/shard_map/all_to_all | solution.py:293
  127.4 14.8 %collective-permute-start.6 = (f32[2,384,128]{2,1,0:T(8,128)}, f32[2,384,128]{2,1,0:T(8,128)S(1)}, u32[]{:S(2)}, u32[]{:S(2)}) collective-permute-start(f32[2,384,128]{2,1,0:T(8,128)} %get-tuple-element.22), channel_id=1, source_target_pairs={{0,1},{1,2},{2,3},{3,4},{4,5},{5,6},{6,7},{7,8},{8,9},{9,10},{10,1... | collective-permute-start | bytes 1179656 | tf_op jit(solution)/shard_map/ppermute | solution.py:289
  135.1 39.3 %collective-permute-start.9 = (f32[2,256,256]{2,1,0:T(8,128)S(1)}, f32[2,256,256]{2,1,0:T(8,128)S(1)}, u32[]{:S(2)}, u32[]{:S(2)}) collective-permute-start(f32[2,256,256]{2,1,0:T(8,128)S(1)} %bitcast.6), channel_id=1, source_target_pairs={{0,1},{1,0},{2,3},{3,2},{4,5},{5,4},{6,7},{7,6},{8,9},{9,8},{10,11... | collective-permute-start | bytes 1572872 | tf_op jit(solution)/shard_map/ppermute | solution.py:297
  142.3 31.2 %collective-permute-start.7 = (f32[2,128,256]{2,1,0:T(8,128)S(1)}, f32[2,128,256]{2,1,0:T(8,128)S(1)}, u32[]{:S(2)}, u32[]{:S(2)}) collective-permute-start(f32[2,128,256]{2,1,0:T(8,128)S(1)} %shard_map.117), channel_id=1, source_target_pairs={{0,32},{32,64},{64,96},{96,128},{128,160},{160,192},{192,224},{224... | collective-permute-start | bytes 786440 | tf_op jit(solution)/shard_map/ppermute | solution.py:289

commit v2 on v1

--- a/solution.py
+++ b/solution.py
@@ -101,7 +101,7 @@
     return jnp.concatenate([high[...], high[...], low[...]], axis=0)
 
 
-def window_fit(window, probe, amplitude, tables, far, window_ref, gradient, add_probe):
+def window_fit(window, probe, amplitude, tables, far, window_ref, gradient, add_probe, probe_copy, amp_copy):
     high, low, high_t, low_t, rows, cols = tables
     window_ref[0] = window[0]
     window_ref[1] = window[1]
@@ -112,6 +112,7 @@
         return twr, twc
 
     def outward(m, carry):
+        probe_copy(m).wait()
         twr, twc = twiddles()
         w_r, w_i = window_ref[0], window_ref[1]
         p_r, p_i = probe[m, 0], probe[m, 1]
@@ -124,7 +125,8 @@
     lax.fori_loop(0, 2, outward, 0)
     intensity = far[0, 0] * far[0, 0] + far[0, 1] * far[0, 1]
     intensity = intensity + (far[1, 0] * far[1, 0] + far[1, 1] * far[1, 1])
-    factor = amplitude / jnp.sqrt(jnp.maximum(intensity, 0.1)) - 1.0
+    amp_copy.wait()
+    factor = amplitude[...] / jnp.sqrt(jnp.maximum(intensity, 0.1)) - 1.0
     for m in range(2):
         far[m, 0] = far[m, 0] * factor
         far[m, 1] = far[m, 1] * factor
@@ -143,14 +145,22 @@
     lax.fori_loop(0, 2, inward, 0)
 
 
-def before_kernel(probe, amp, amp_out, step_out):
+def before_kernel(probe_hbm, amp_hbm, amp_out, step_out, probe, amp, ordered, sems):
+    amp_copy = pltpu.make_async_copy(amp_hbm, amp, sems.at[0])
+    probe_copy = pltpu.make_async_copy(probe_hbm, probe, sems.at[1])
+    out_copy = lambda b: pltpu.make_async_copy(ordered.at[b], amp_out.at[b], sems.at[2 + b])
+    amp_copy.start()
+    probe_copy.start()
     out_at = lax.broadcasted_iota(jnp.int32, (WIN, WIN), 0)
     in_at = lax.broadcasted_iota(jnp.int32, (WIN, WIN), 1)
     wanted = jnp.where(out_at < HALF, 2 * out_at, 2 * (out_at - HALF) + 1)
     pick = jnp.where(in_at == wanted, 1.0, 0.0).astype(jnp.bfloat16)
+    amp_copy.wait()
     for b in range(BATCHES):
         rows = jnp.dot(pick, amp[b], preferred_element_type=jnp.float32).astype(jnp.bfloat16)
-        amp_out[b] = lax.dot_general(rows, pick, (((1,), (1,)), ((), ())), preferred_element_type=jnp.float32)
+        ordered[b] = lax.dot_general(rows, pick, (((1,), (1,)), ((), ())), preferred_element_type=jnp.float32)
+        out_copy(b).start()
+    probe_copy.wait()
     total = jnp.zeros((8, HALF), jnp.float32)
     for m in range(2):
         for k in range(2):
@@ -159,6 +169,8 @@
             total = total + square[:, :HALF] + square[:, HALF:]
     power = jnp.sum(total) / (WIN * WIN)
     step_out[...] = jnp.full((8, HALF), 1.0, jnp.float32) / (power + 1e-06)
+    for b in range(BATCHES):
+        out_copy(b).wait()
 
 
 TILE_R = 384
@@ -166,9 +178,16 @@
 WIDE = WIN + HALO
 
 
-def first_kernel(pos, obj, halo, probe, amp, step, high, low, high_t, low_t, rows, cols,
-                 new_obj, spill, edge, middle, probe_sum, far, win, grad):
+def first_kernel(pos, obj, halo, probe_hbm, amp_hbm, step, high, low, high_t, low_t, rows, cols,
+                 obj_hbm, spill, edge, middle, sum_hbm, far, win, grad, probe, amp, new_obj, probe_sum, sems):
     row, col = pos[0, 0], pos[0, 1]
+    probe_copy = lambda m: pltpu.make_async_copy(probe_hbm.at[m], probe.at[m], sems.at[m])
+    sum_copy = lambda m: pltpu.make_async_copy(probe_sum.at[m], sum_hbm.at[m], sems.at[2 + m])
+    obj_copy = lambda k: pltpu.make_async_copy(new_obj.at[k], obj_hbm.at[k], sems.at[4 + k])
+    amp_copy = pltpu.make_async_copy(amp_hbm.at[0], amp, sems.at[6])
+    probe_copy(0).start()
+    probe_copy(1).start()
+    amp_copy.start()
 
     def cut(k):
         wide = jnp.concatenate([obj[k], halo[k]], axis=1)
@@ -178,8 +197,10 @@
     def add_probe(m, real, imag):
         probe_sum[m, 0] = real
         probe_sum[m, 1] = imag
-
-    window_fit((cut(0), cut(1)), probe, amp[0], (high, low, high_t, low_t, rows, cols), far, win, grad, add_probe)
+        sum_copy(m).start()
+
+    window_fit((cut(0), cut(1)), probe, amp, (high, low, high_t, low_t, rows, cols), far, win, grad, add_probe,
+               probe_copy, amp_copy)
     scale = step[:1, :1]
     for k in range(2):
         g = jnp.concatenate([grad[k] * scale, jnp.zeros((TILE_R - WIN, WIN), jnp.float32)], axis=0)
@@ -188,9 +209,13 @@
         g = pltpu.roll(g, col, 1)
         updated = obj[k] + g[:, :WIN]
         new_obj[k] = updated
+        obj_copy(k).start()
         edge[k] = updated[:, :HALO]
         middle[k] = updated[:HALO, HALO:]
         spill[k] = g[:, WIN:]
+    for k in range(2):
+        sum_copy(k).wait()
+        obj_copy(k).wait()
 
 
 def lanes():
@@ -204,57 +229,79 @@
         upward[k] = jnp.where(lanes() >= above[1, 1], own, from_right[k, :HALO] + spill[k, :HALO] * keep)
 
 
-def second_kernel(pos, info, obj, from_left, from_right, spill, below_mid, below_rest, probe, amp, step, probe_in,
+def merge_kernel(info, obj, from_left, from_right, spill, whole, source):
+    keep = info[0].astype(jnp.float32)
+    for k in range(2):
+        left = obj[k, :, :HALO] + from_left[k]
+        whole[k, :, :HALO] = left
+        whole[k, :, HALO:] = obj[k, :, HALO:]
+        source[k, :, :HALO] = left[LAST:]
+        source[k, :, HALO:WIN] = obj[k, LAST:, HALO:]
+        source[k, :, WIN:] = from_right[k, LAST:] + spill[k, LAST:] * keep
+
+
+def second_kernel(pos, info, source, below_mid, below_rest, probe_hbm, amp_hbm, step, before_hbm,
                   high, low, high_t, low_t, rows, cols,
-                  new_obj, new_spill, downward, keep_sum, send_sum, far, win, grad):
-    row, col = pos[1, 0] - LAST, pos[1, 1]
-    keep, core = info[0].astype(jnp.float32), info[1]
+                  grad_hbm, spill, downward, keep_sum, send_sum, far, win, grad, probe, amp, own_grad, before, sems):
+    row, col, core = pos[1, 0] - LAST, pos[1, 1], info[1]
+    probe_copy = lambda m: pltpu.make_async_copy(probe_hbm.at[m], probe.at[m], sems.at[m])
+    before_copy = lambda m: pltpu.make_async_copy(before_hbm.at[m], before.at[m], sems.at[2 + m])
+    grad_copy = lambda k: pltpu.make_async_copy(own_grad.at[k], grad_hbm.at[k], sems.at[4 + k])
+    amp_copy = pltpu.make_async_copy(amp_hbm.at[1], amp, sems.at[6])
+    probe_copy(0).start()
+    probe_copy(1).start()
+    amp_copy.start()
+    before_copy(0).start()
+    before_copy(1).start()
 
     def cut(k):
-        upper = jnp.concatenate(
-            [obj[k, LAST:, :HALO] + from_left[k, LAST:], obj[k, LAST:, HALO:], from_right[k, LAST:] + spill[k, LAST:] * keep],
-            axis=1)
         lower = jnp.concatenate([below_rest[k], below_mid[k], below_rest[k]], axis=1)
-        tall = pltpu.roll(jnp.concatenate([upper, lower], axis=0), WIDE - col, 1)[:, :WIN]
+        tall = pltpu.roll(jnp.concatenate([source[k], lower], axis=0), WIDE - col, 1)[:, :WIN]
         return pltpu.roll(tall, lax.rem(TILE_R - row, TILE_R), 0)[:WIN]
 
     def add_probe(m, real, imag):
+        before_copy(m).wait()
+
         @pl.when(m == core)
         def _():
-            keep_sum[0] = probe_in[m, 0] + real
-            keep_sum[1] = probe_in[m, 1] + imag
+            keep_sum[0] = before[m, 0] + real
+            keep_sum[1] = before[m, 1] + imag
 
         @pl.when(m != core)
         def _():
-            send_sum[0] = probe_in[m, 0] + real
-            send_sum[1] = probe_in[m, 1] + imag
-
-    window_fit((cut(0), cut(1)), probe, amp[1], (high, low, high_t, low_t, rows, cols), far, win, grad, add_probe)
+            send_sum[0] = before[m, 0] + real
+            send_sum[1] = before[m, 1] + imag
+
+    window_fit((cut(0), cut(1)), probe, amp, (high, low, high_t, low_t, rows, cols), far, win, grad, add_probe,
+               probe_copy, amp_copy)
     scale = step[:1, :1]
     for k in range(2):
         g = jnp.concatenate([grad[k] * scale, jnp.zeros((TILE_R - WIN, WIN), jnp.float32)], axis=0)
         g = pltpu.roll(g, row, 0)
         g = jnp.concatenate([g, jnp.zeros((TILE_R, HALO), jnp.float32)], axis=1)
         g = pltpu.roll(g, col, 1)
-        downward[k] = g[WIN:, :WIN]
-        new_obj[k, :LAST, :HALO] = obj[k, :LAST, :HALO] + from_left[k, :LAST]
-        new_obj[k, :LAST, HALO:] = obj[k, :LAST, HALO:]
-        new_obj[k, LAST:, :HALO] = obj[k, LAST:, :HALO] + from_left[k, LAST:] + g[:WIN, :HALO]
-        new_obj[k, LAST:, HALO:] = obj[k, LAST:, HALO:] + g[:WIN, HALO:WIN]
-        new_spill[k] = g[:, WIN:]
-
-
-def down_kernel(downward, from_left, out):
-    for k in range(2):
-        out[k, :, :HALO] = downward[k, :, :HALO] + from_left[k, WIN:]
-        out[k, :, HALO:] = downward[k, :, HALO:]
-
-
-def object_kernel(obj, from_left, from_above, out):
-    for k in range(2):
-        out[k, :LAST] = obj[k, :LAST] + from_above[k]
-        out[k, LAST:, :HALO] = obj[k, LAST:, :HALO] + from_left[k, :WIN]
-        out[k, LAST:, HALO:] = obj[k, LAST:, HALO:]
+        own_grad[k] = g[:WIN, :WIN]
+        grad_copy(k).start()
+        downward[k, :, :HALO] = g[WIN:, :HALO] + g[WIN:, WIN:]
+        downward[k, :, HALO:] = g[WIN:, HALO:WIN]
+        spill[k] = g[:WIN, WIN:]
+    for k in range(2):
+        grad_copy(k).wait()
+
+
+def spill_kernel(above, spill, from_above, new_spill):
+    for k in range(2):
+        new_spill[k, :HALO] = jnp.where(lanes() < above[1, 1], from_above[k, :, :HALO], 0.0)
+        new_spill[k, HALO:] = spill[k]
+
+
+def object_kernel(above, whole, grad, from_above, from_left, out):
+    for k in range(2):
+        fell = jnp.where(lanes() >= above[1, 1], from_above[k, :, :HALO], 0.0)
+        out[k, :LAST, :HALO] = whole[k, :LAST, :HALO] + fell + from_left[k, :LAST]
+        out[k, :LAST, HALO:] = whole[k, :LAST, HALO:] + from_above[k, :, HALO:]
+        out[k, LAST:, :HALO] = whole[k, LAST:, :HALO] + grad[k, :, :HALO] + from_left[k, LAST:]
+        out[k, LAST:, HALO:] = whole[k, LAST:, HALO:] + grad[k, :, HALO:]
 
 
 def probe_kernel(info, probe, own, other, out):
@@ -263,24 +310,34 @@
     out[1 - core] = probe[1 - core] + other[...]
 
 
-def call(kernel, outs, scratch, scalars, *arrays, last=False):
-    vmem = pl.BlockSpec(memory_space=pltpu.VMEM)
+HBM = object()
+AUTO = object()
+
+
+def call(kernel, outs, scratch, scalars, arrays, copies=0):
     smem = pl.BlockSpec(memory_space=pltpu.SMEM)
-    if INTERPRET or last:
-        shapes = [jax.ShapeDtypeStruct(s, jnp.float32) for s in outs]
-    else:
-        shapes = [pltpu.VMEM(s, jnp.float32) for s in outs]
-    if not INTERPRET:
-        arrays = [pltpu.with_memory_space_constraint(x, pltpu.VMEM) for x in arrays]
+    specs = {None: pl.BlockSpec(memory_space=pltpu.VMEM), HBM: pl.BlockSpec(memory_space=pltpu.HBM)}
+    specs[AUTO] = specs[None]
+    arrays = [x if isinstance(x, tuple) else (x, None) for x in arrays]
+    outs = [(o[0], o[1]) if isinstance(o[0], tuple) else (o, None) for o in outs]
+    spaces = {None: pltpu.VMEM, HBM: pltpu.HBM, AUTO: pltpu.HBM}
+    shapes = [
+        jax.ShapeDtypeStruct(shape, jnp.float32) if INTERPRET or where is AUTO else spaces[where](shape, jnp.float32)
+        for shape, where in outs
+    ]
+    operands = [
+        x if INTERPRET or where is AUTO else pltpu.with_memory_space_constraint(x, spaces[where]) for x, where in arrays
+    ]
     return pl.pallas_call(
         kernel,
         out_shape=shapes,
-        in_specs=[smem] * len(scalars) + [vmem] * len(arrays),
-        out_specs=[vmem] * len(outs),
-        scratch_shapes=[pltpu.VMEM(s, jnp.float32) for s in scratch],
+        in_specs=[smem] * len(scalars) + [specs[where] for _, where in arrays],
+        out_specs=[specs[where] for _, where in outs],
+        scratch_shapes=[pltpu.VMEM(s, jnp.float32) if isinstance(s, tuple) else s for s in scratch]
+        + ([pltpu.SemaphoreType.DMA((copies,))] if copies else []),
         compiler_params=pltpu.CompilerParams(vmem_limit_bytes=24 * 1024 * 1024),
         interpret=INTERPRET,
-    )(*scalars, *arrays)
+    )(*scalars, *operands)
 
 
 def passed_along(block, axis, distance):
@@ -317,30 +374,37 @@
     divisor = math.sqrt(device_count * BATCHES)
     has_right = (lax.axis_index(COL) < lax.axis_size(COL) - 1).astype(jnp.int32)
     tile, side, probe_shape = (2, TILE_R, WIN), (2, TILE_R, HALO), (2, 2, WIN, WIN)
-    block = (2, HALO, HALO)
-    fit_scratch = [probe_shape, (2, WIN, WIN), (2, WIN, WIN)]
+    block, window = (2, HALO, HALO), (2, WIN, WIN)
+    fit_scratch = [probe_shape, window, window, probe_shape, (WIN, WIN)]
 
     halo = passed_along(object_field[:, :, :HALO], COL, -1)
     above = passed_along(positions, ROW, 1)
     info = jnp.stack([has_right, lax.axis_index(CORE)])
-    amp, step = call(before_kernel, [(BATCHES, WIN, WIN), (8, HALF)], [], [], probe_modes, amplitudes[0, 0])
+    amp, step = call(
+        before_kernel, [((BATCHES, WIN, WIN), HBM), (8, HALF)],
+        [probe_shape, pltpu.VMEM((BATCHES, WIN, WIN), jnp.bfloat16), (BATCHES, WIN, WIN)],
+        [], [(probe_modes, HBM), (amplitudes[0, 0], HBM)], copies=4)
     obj, spill, edge, middle, probe_sum = call(
-        first_kernel, [tile, side, side, block, probe_shape], fit_scratch, [positions],
-        object_field, halo, probe_modes, amp, step, *tables)
+        first_kernel, [(tile, HBM), side, side, block, (probe_shape, HBM)], fit_scratch + [tile, probe_shape],
+        [positions], [object_field, halo, (probe_modes, HBM), (amp, HBM), step, *tables], copies=7)
+    below_mid = passed_along(middle, ROW, -1)
+    from_right = passed_along(edge, COL, -1)
     from_left = passed_along(spill, COL, 1)
-    from_right = passed_along(edge, COL, -1)
-    below_mid = passed_along(middle, ROW, -1)
-    (upward,) = call(upward_kernel, [block], [], [above, info], edge, from_left, from_right, spill)
+    (upward,) = call(upward_kernel, [block], [], [above, info], [edge, from_left, from_right, spill])
     below_rest = passed_along(upward, ROW, -1)
-    obj, spill, downward, keep, send = call(
-        second_kernel, [tile, side, (2, HALO, WIN), (2, WIN, WIN), (2, WIN, WIN)], fit_scratch, [positions, info],
-        obj, from_left, from_right, spill, below_mid, below_rest, probe_modes, amp, step, probe_sum, *tables)
+    whole, source = call(
+        merge_kernel, [(tile, AUTO), (2, WIN, WIDE)], [], [info], [(obj, AUTO), from_left, from_right, spill])
+    grad, spill, downward, keep, send = call(
+        second_kernel, [(window, HBM), (2, WIN, HALO), (2, HALO, WIN), window, window],
+        fit_scratch + [window, probe_shape], [positions, info],
+        [source, below_mid, below_rest, (probe_modes, HBM), (amp, HBM), step, (probe_sum, HBM), *tables], copies=7)
     own, other = summed_everywhere(keep, send, divisor)
+    from_above = passed_along(downward, ROW, 1)
+    (spill,) = call(spill_kernel, [side], [], [above], [spill, from_above])
     from_left = passed_along(spill, COL, 1)
-    (downward,) = call(down_kernel, [(2, HALO, WIN)], [], [], downward, from_left)
-    from_above = passed_along(downward, ROW, 1)
-    (object_out,) = call(object_kernel, [tile], [], [], obj, from_left, from_above, last=True)
-    (probe_out,) = call(probe_kernel, [probe_shape], [], [info], probe_modes, own, other, last=True)
+    (object_out,) = call(
+        object_kernel, [(tile, AUTO)], [], [above], [(whole, AUTO), (grad, AUTO), from_above, from_left])
+    (probe_out,) = call(probe_kernel, [(probe_shape, AUTO)], [], [info], [(probe_modes, AUTO), own, other])
     return (object_out, probe_out)
 
 

time: 177 us -> 170 us (0.960)
  the two profiles are of different devices: /device:TPU:25 before, /device:TPU:10 now
where the time goes in v2:
time: 170 us; the launch traced here: 169 us
  waiting for transfers between devices  50.8 us (30%)
  starting transfers between devices  47.3 us (28%)
  blocking collectives  46.1 us (27%)
  Pallas kernels  20.9 us (12%)
  local copies, waits for them, and re-layouts  2.61 us (2%)
    ppermute x8, waiting for transfers between devices, passed_along(): return lax.ppermute(block, axis, route)  46.3 us
    all_to_all x3, blocking collectives, exchanged(): return lax.all_to_all(parts, axes, 0, 0, tiled=False)  46.1 us
    ppermute x8, starting transfers between devices, passed_along(): return lax.ppermute(block, axis, route)  36.4 us
    pallas_call x8, Pallas kernels, call(): pl.pallas_call(kernel, out_shape=shapes, in_specs=[smem] * len(scalars) +...  20.9 us
    all_to_all x1, starting transfers between devices, exchanged(): return lax.all_to_all(parts, axes, 0, 0, tiled=False)  6.8 us
    ppermute x2, starting transfers between devices, swapped(): return lax.ppermute(block, CORE, [(0, 1), (1, 0)])  4.2 us
  transfers between devices with their start and end apart: 11, of which 7 were waited for; matrix products, arithmetic and copies ran while one was open for 0% of the time, Pallas kernels for 3%

profile of v2, /device:TPU:10, one launch (start us, length us, event | category | flops | bytes accessed | tf_op | source)
XLA Modules:
  0.0 168.9 jit_solution(10612043425293693852)
XLA Ops:
  0.6 0.0 copy-start.8
  0.6 0.0 copy-start.9
  0.7 1.1 slice.3
  1.7 0.0 copy-start.1
  1.7 2.1 %collective-permute-start.1 = (f32[2,384,128]{2,1,0:T(8,128)S(1)}, f32[2,384,128]{2,1,0:T(8,128)S(1)}, u32[]{:S(2)}, u32[]{:S(2)}) collective-permute-start(f32[2,384,128]{2,1,0:T(8,128)S(1)} %slice.3), channel_id=1, source_target_pairs={{1,0},{2,1},{3,2},{4,3},{5,4},{6,5},{7,6},{8,7},{9,8},{10,9},{11,1... | collective-permute-start | bytes 1179656 | tf_op jit(solution)/shard_map/ppermute | solution.py:346
  3.8 0.0 copy-start.4
  3.8 0.0 copy-start.5
  3.8 0.0 copy-start.6
  3.8 0.0 copy-start.7
  3.8 2.2 %shard_map.113 = (f32[2,256,256]{2,1,0:T(8,128)}, f32[8,128]{1,0:T(8,128)S(1)}) custom-call(f32[2,2,256,256]{3,2,1,0:T(8,128)} %probe.1, bf16[2,256,256]{2,1,0:T(8,128)(2,1)} %bitcast.12), custom_call_target="tpu_custom_call" | custom-call | tf_op jit(solution)/shard_map/pallas_call | solution.py:331
  6.0 3.0 %collective-permute-done.1.halo = f32[2,384,128]{2,1,0:T(8,128)S(1)} collective-permute-done((f32[2,384,128]{2,1,0:T(8,128)S(1)}, f32[2,384,128]{2,1,0:T(8,128)S(1)}, u32[]{:S(2)}, u32[]{:S(2)}) %collective-permute-start.1) | collective-permute-done | bytes 393248 | tf_op jit(solution)/shard_map/ppermute | solution.py:346
  9.1 0.0 copy-start.10
  9.1 0.0 copy-done.8
  9.1 0.0 copy-done.9
  9.1 0.0 copy-done.1
  9.1 0.0 copy-done.4
  9.1 0.0 copy-done.5
  9.1 0.0 copy-done.6
  9.1 0.0 copy-done.7
  9.1 0.6 copy-done.10
  9.7 6.9 %shard_map.114 = (f32[2,384,256]{2,1,0:T(8,128)}, f32[2,384,128]{2,1,0:T(8,128)S(1)}, f32[2,384,128]{2,1,0:T(8,128)S(1)}, f32[2,128,128]{2,1,0:T(8,128)S(1)}, f32[2,2,256,256]{3,2,1,0:T(8,128)}) custom-call(s32[2,2]{1,0:T(2,128)S(1)} %bitcast.8, f32[2,384,256]{2,1,0:T(8,128)S(1)} %copy-done.1, f32[2,384,128]{2,1,0:T(8,128)S(1)} %collective-permute-done.1.halo, ...), custom_call_target="tpu_custom_call" | custom-call | tf_op jit(solution)/shard_map/pallas_call | solution.py:331
  16.7 3.8 %collective-permute-start.3 = (f32[2,384,128]{2,1,0:T(8,128)S(1)}, f32[2,384,128]{2,1,0:T(8,128)S(1)}, u32[]{:S(2)}, u32[]{:S(2)}) collective-permute-start(f32[2,384,128]{2,1,0:T(8,128)S(1)} %get-tuple-element.20.edge), channel_id=1, source_target_pairs={{1,0},{2,1},{3,2},{4,3},{5,4},{6,5},{7,6},{8,7},{9,8},{10,9},{11,1... | collective-permute-start | bytes 1179656 | tf_op jit(solution)/shard_map/ppermute | solution.py:346
  20.5 1.9 %collective-permute-start.2 = (f32[2,384,128]{2,1,0:T(8,128)S(1)}, f32[2,384,128]{2,1,0:T(8,128)S(1)}, u32[]{:S(2)}, u32[]{:S(2)}) collective-permute-start(f32[2,384,128]{2,1,0:T(8,128)S(1)} %get-tuple-element.19.spill), channel_id=1, source_target_pairs={{0,1},{1,2},{2,3},{3,4},{4,5},{5,6},{6,7},{7,8},{8,9},{9,10},{10,1... | collective-permute-start | bytes 1179656 | tf_op jit(solution)/shard_map/ppermute | solution.py:346
  22.4 9.1 %collective-permute-start = (s32[2,2]{1,0:T(2,128)S(1)}, s32[2,2]{1,0:T(2,128)S(1)}, u32[]{:S(2)}, u32[]{:S(2)}) collective-permute-start(s32[2,2]{1,0:T(2,128)S(1)} %bitcast.9), channel_id=1, source_target_pairs={{0,32},{32,64},{64,96},{96,128},{128,160},{160,192},{192,224},{224... | collective-permute-start | bytes 56 | tf_op jit(solution)/shard_map/ppermute | solution.py:346
  31.5 0.1 pad_add_fusion.info
  31.6 0.0 copy-start.2
  31.6 5.5 %collective-permute-start.4 = (f32[2,128,128]{2,1,0:T(8,128)S(1)}, f32[2,128,128]{2,1,0:T(8,128)S(1)}, u32[]{:S(2)}, u32[]{:S(2)}) collective-permute-start(f32[2,128,128]{2,1,0:T(8,128)S(1)} %get-tuple-element.23), channel_id=1, source_target_pairs={{32,0},{64,32},{96,64},{128,96},{160,128},{192,160},{224,192},{256... | collective-permute-start | bytes 393224 | tf_op jit(solution)/shard_map/ppermute | solution.py:346
  37.2 0.0 collective-permute-done.above
  37.2 0.0 collective-permute-done.3.from_right
  37.2 0.0 collective-permute-done.2.from_left
  37.2 0.6 shard_map.116
  37.8 7.8 %collective-permute-start.5 = (f32[2,128,128]{2,1,0:T(8,128)S(1)}, f32[2,128,128]{2,1,0:T(8,128)S(1)}, u32[]{:S(2)}, u32[]{:S(2)}) collective-permute-start(f32[2,128,128]{2,1,0:T(8,128)S(1)} %shard_map.116), channel_id=1, source_target_pairs={{32,0},{64,32},{96,64},{128,96},{160,128},{192,160},{224,192},{256... | collective-permute-start | bytes 393224 | tf_op jit(solution)/shard_map/ppermute | solution.py:346
  45.6 0.0 copy-done.2
  45.6 0.7 shard_map.115
  46.3 12.4 %collective-permute-done.4.below_mid = f32[2,128,128]{2,1,0:T(8,128)S(1)} collective-permute-done((f32[2,128,128]{2,1,0:T(8,128)S(1)}, f32[2,128,128]{2,1,0:T(8,128)S(1)}, u32[]{:S(2)}, u32[]{:S(2)}) %collective-permute-start.4) | collective-permute-done | bytes 131104 | tf_op jit(solution)/shard_map/ppermute | solution.py:346
  58.7 5.6 %collective-permute-done.5.below_rest = f32[2,128,128]{2,1,0:T(8,128)S(1)} collective-permute-done((f32[2,128,128]{2,1,0:T(8,128)S(1)}, f32[2,128,128]{2,1,0:T(8,128)S(1)}, u32[]{:S(2)}, u32[]{:S(2)}) %collective-permute-start.5) | collective-permute-done | bytes 131104 | tf_op jit(solution)/shard_map/ppermute | solution.py:346
  64.4 6.8 %shard_map.117 = (f32[2,256,256]{2,1,0:T(8,128)}, f32[2,256,128]{2,1,0:T(8,128)S(1)}, f32[2,128,256]{2,1,0:T(8,128)S(1)}, f32[2,256,256]{2,1,0:T(8,128)S(1)}, f32[2,256,256]{2,1,0:T(8,128)S(1)}) custom-call(s32[2,2]{1,0:T(2,128)S(1)} %bitcast.10, s32[2]{0:T(128)S(1)} %pad_add_fusion.info, f32[2,256,384]{2,1,0:T(8,128)S(1)} %get-tuple-element.22.source, ...), custom_call_target="tpu_custom_call" | custom-call | tf_op jit(solution)/shard_map/pallas_call | solution.py:331
  71.2 2.3 %collective-permute-start.8 = (f32[2,256,256]{2,1,0:T(8,128)S(1)}, f32[2,256,256]{2,1,0:T(8,128)S(1)}, u32[]{:S(2)}, u32[]{:S(2)}) collective-permute-start(f32[2,256,256]{2,1,0:T(8,128)S(1)} %get-tuple-element.29), channel_id=1, source_target_pairs={{0,1},{1,0},{2,3},{3,2},{4,5},{5,4},{6,7},{7,6},{8,9},{9,8},{10,11... | collective-permute-start | bytes 1572872 | tf_op jit(solution)/shard_map/ppermute | solution.py:354
  73.5 1.5 collective-permute-done.8
  75.0 0.1 add.11
  75.1 16.1 %all_to_all.20 = f32[16,32,256]{2,1,0:T(8,128)S(1)} all-to-all(f32[16,32,256]{2,1,0:T(8,128)S(1)} %bitcast.11), channel_id=1, replica_groups=mesh['row_0'=4,'row_1'=4,'col_0'=4,'col_1'=4,'col_2'=2] {'row_0','col_1'}, dimensions={0} | all-to-all | bytes 1048576 | tf_op jit(solution)/shard_map/all_to_all | solution.py:350
  91.2 8.3 %all_to_all.21 = f32[4,32,256]{2,1,0:T(8,128)S(1)} all-to-all(f32[4,32,256]{2,1,0:T(8,128)S(1)} %broadcast_in_dim.9), channel_id=1, replica_groups=mesh['row_0'=4,'row_1'=4,'col_0'=4,'col_1'=4,'col_2'=2] {'col_0'}, dimensions={0} | all-to-all | bytes 262144 | tf_op jit(solution)/shard_map/all_to_all | solution.py:350
  99.5 21.8 %all_to_all.22 = f32[4,32,256]{2,1,0:T(8,128)S(1)} all-to-all(f32[4,32,256]{2,1,0:T(8,128)S(1)} %broadcast_in_dim.10), channel_id=1, replica_groups=mesh['row_0'=4,'row_1'=4,'col_0'=4,'col_1'=4,'col_2'=2] {'row_1'}, dimensions={0} | all-to-all | bytes 262144 | tf_op jit(solution)/shard_map/all_to_all | solution.py:350
  121.3 0.8 broadcast_in_dim.11
  122.2 6.8 %all-to-all-start.3 = ((f32[16,32,256]{2,1,0:T(8,128)}), f32[16,32,256]{2,1,0:T(8,128)S(1)}, u32[]{:S(2)}, u32[]{:S(2)}) async-start(f32[16,32,256]{2,1,0:T(8,128)} %broadcast_in_dim.11), calls=%async_computation.3 | async-start | bytes 1048576 | tf_op jit(solution)/shard_map/all_to_all | solution.py:350
  129.0 0.0 copy-start.3
  129.0 4.2 %collective-permute-start.6 = (f32[2,128,256]{2,1,0:T(8,128)S(1)}, f32[2,128,256]{2,1,0:T(8,128)S(1)}, u32[]{:S(2)}, u32[]{:S(2)}) collective-permute-start(f32[2,128,256]{2,1,0:T(8,128)S(1)} %get-tuple-element.26), channel_id=1, source_target_pairs={{0,32},{32,64},{64,96},{96,128},{128,160},{160,192},{192,224},{224... | collective-permute-start | bytes 786440 | tf_op jit(solution)/shard_map/ppermute | solution.py:346
  133.1 3.0 %all-to-all-done.3 = f32[16,32,256]{2,1,0:T(8,128)S(1)} async-done(((f32[16,32,256]{2,1,0:T(8,128)}), f32[16,32,256]{2,1,0:T(8,128)S(1)}, u32[]{:S(2)}, u32[]{:S(2)}) %all-to-all-start.3) | async-done | bytes 524320 | tf_op jit(solution)/shard_map/all_to_all | solution.py:350
  136.2 1.9 %collective-permute-start.9 = (f32[2,256,256]{2,1,0:T(8,128)S(1)}, f32[2,256,256]{2,1,0:T(8,128)S(1)}, u32[]{:S(2)}, u32[]{:S(2)}) collective-permute-start(f32[2,256,256]{2,1,0:T(8,128)S(1)} %bitcast.6), channel_id=1, source_target_pairs={{0,1},{1,0},{2,3},{3,2},{4,5},{5,4},{6,7},{7,6},{8,9},{9,8},{10,11... | collective-permute-start | bytes 1572872 | tf_op jit(solution)/shard_map/ppermute | solution.py:354
  138.1 18.0 %collective-permute-done.6.from_above = f32[2,128,256]{2,1,0:T(8,128)S(1)} collective-permute-done((f32[2,128,256]{2,1,0:T(8,128)S(1)}, f32[2,128,256]{2,1,0:T(8,128)S(1)}, u32[]{:S(2)}, u32[]{:S(2)}) %collective-permute-start.6) | collective-permute-done | bytes 262176 | tf_op jit(solution)/shard_map/ppermute | solution.py:346
  156.1 0.6 shard_map.118
  156.7 1.9 %collective-permute-start.7 = (f32[2,384,128]{2,1,0:T(8,128)S(1)}, f32[2,384,128]{2,1,0:T(8,128)S(1)}, u32[]{:S(2)}, u32[]{:S(2)}) collective-permute-start(f32[2,384,128]{2,1,0:T(8,128)S(1)} %shard_map.118), channel_id=1, source_target_pairs={{0,1},{1,2},{2,3},{3,4},{4,5},{5,6},{6,7},{7,8},{8,9},{9,10},{10,1... | collective-permute-start | bytes 1179656 | tf_op jit(solution)/shard_map/ppermute | solution.py:346
  158.6 7.2 %collective-permute-done.7.from_left = f32[2,384,128]{2,1,0:T(8,128)S(1)} collective-permute-done((f32[2,384,128]{2,1,0:T(8,128)S(1)}, f32[2,384,128]{2,1,0:T(8,128)S(1)}, u32[]{:S(2)}, u32[]{:S(2)}) %collective-permute-start.7) | collective-permute-done | bytes 393248 | tf_op jit(solution)/shard_map/ppermute | solution.py:346
  165.8 0.0 copy-done.3
  165.8 0.0 copy-start
  165.8 1.5 shard_map.119
  167.3 0.0 collective-permute-done.9.other
  167.3 0.0 copy-done
  167.3 1.6 shard_map.120
  (6 shorter events, 0.1 us)
Async XLA Ops:
  0.6 8.4 %copy-start.8 = (bf16[256,256]{1,0:T(8,128)(2,1)S(1)}, bf16[256,256]{1,0:T(8,128)(2,1)}, u32[]{:S(2)}) copy-start(bf16[256,256]{1,0:T(8,128)(2,1)} %constant.34.clone.high) | copy-start | bytes 393220
  0.6 8.4 %copy-start.9 = (f32[2,8,128]{2,1,0:T(8,128)S(1)}, f32[2,8,128]{2,1,0:T(8,128)}, u32[]{:S(2)}) copy-start(f32[2,8,128]{2,1,0:T(8,128)} %constant.39.clone.cols) | copy-start | bytes 24580
  1.7 7.4 %copy-start.1 = (f32[2,384,256]{2,1,0:T(8,128)S(1)}, f32[2,384,256]{2,1,0:T(8,128)}, u32[]{:S(2)}) copy-start(f32[2,384,256]{2,1,0:T(8,128)} %obj.1) | copy-start | bytes 2359300
  1.7 7.3 %collective-permute-start.1 = (f32[2,384,128]{2,1,0:T(8,128)S(1)}, f32[2,384,128]{2,1,0:T(8,128)S(1)}, u32[]{:S(2)}, u32[]{:S(2)}) collective-permute-start(f32[2,384,128]{2,1,0:T(8,128)S(1)} %slice.3), channel_id=1, source_target_pairs={{1,0},{2,1},{3,2},{4,3},{5,4},{6,5},{7,6},{8,7},{9,8},{10,9},{11,1... | collective-permute-start | bytes 1179656 | tf_op jit(solution)/shard_map/ppermute | solution.py:346
  3.8 5.3 %copy-start.4 = (f32[2,128,128]{2,1,0:T(8,128)S(1)}, f32[2,128,128]{2,1,0:T(8,128)}, u32[]{:S(2)}) copy-start(f32[2,128,128]{2,1,0:T(8,128)} %constant.38.clone.rows) | copy-start | bytes 393220
  3.8 5.3 %copy-start.5 = (bf16[256,256]{1,0:T(8,128)(2,1)S(1)}, bf16[256,256]{1,0:T(8,128)(2,1)}, u32[]{:S(2)}) copy-start(bf16[256,256]{1,0:T(8,128)(2,1)} %constant.37.clone.low_t) | copy-start | bytes 393220
  3.8 5.3 %copy-start.6 = (bf16[256,256]{1,0:T(8,128)(2,1)S(1)}, bf16[256,256]{1,0:T(8,128)(2,1)}, u32[]{:S(2)}) copy-start(bf16[256,256]{1,0:T(8,128)(2,1)} %constant.36.clone.high_t) | copy-start | bytes 393220
  3.8 5.3 %copy-start.7 = (bf16[256,256]{1,0:T(8,128)(2,1)S(1)}, bf16[256,256]{1,0:T(8,128)(2,1)}, u32[]{:S(2)}) copy-start(bf16[256,256]{1,0:T(8,128)(2,1)} %constant.35.clone.low) | copy-start | bytes 393220
  9.1 0.7 copy-start.10
  16.7 20.5 %collective-permute-start.3 = (f32[2,384,128]{2,1,0:T(8,128)S(1)}, f32[2,384,128]{2,1,0:T(8,128)S(1)}, u32[]{:S(2)}, u32[]{:S(2)}) collective-permute-start(f32[2,384,128]{2,1,0:T(8,128)S(1)} %get-tuple-element.20.edge), channel_id=1, source_target_pairs={{1,0},{2,1},{3,2},{4,3},{5,4},{6,5},{7,6},{8,7},{9,8},{10,9},{11,1... | collective-permute-start | bytes 1179656 | tf_op jit(solution)/shard_map/ppermute | solution.py:346
  20.5 16.7 %collective-permute-start.2 = (f32[2,384,128]{2,1,0:T(8,128)S(1)}, f32[2,384,128]{2,1,0:T(8,128)S(1)}, u32[]{:S(2)}, u32[]{:S(2)}) collective-permute-start(f32[2,384,128]{2,1,0:T(8,128)S(1)} %get-tuple-element.19.spill), channel_id=1, source_target_pairs={{0,1},{1,2},{2,3},{3,4},{4,5},{5,6},{6,7},{7,8},{8,9},{9,10},{10,1... | collective-permute-start | bytes 1179656 | tf_op jit(solution)/shard_map/ppermute | solution.py:346
  22.4 14.8 %collective-permute-start = (s32[2,2]{1,0:T(2,128)S(1)}, s32[2,2]{1,0:T(2,128)S(1)}, u32[]{:S(2)}, u32[]{:S(2)}) collective-permute-start(s32[2,2]{1,0:T(2,128)S(1)} %bitcast.9), channel_id=1, source_target_pairs={{0,32},{32,64},{64,96},{96,128},{128,160},{160,192},{192,224},{224... | collective-permute-start | bytes 56 | tf_op jit(solution)/shard_map/ppermute | solution.py:346
  31.6 14.0 %copy-start.2 = (f32[2,384,256]{2,1,0:T(8,128)S(1)}, f32[2,384,256]{2,1,0:T(8,128)}, u32[]{:S(2)}) copy-start(f32[2,384,256]{2,1,0:T(8,128)} %get-tuple-element.18.obj) | copy-start | bytes 2359300
  31.6 27.1 %collective-permute-start.4 = (f32[2,128,128]{2,1,0:T(8,128)S(1)}, f32[2,128,128]{2,1,0:T(8,128)S(1)}, u32[]{:S(2)}, u32[]{:S(2)}) collective-permute-start(f32[2,128,128]{2,1,0:T(8,128)S(1)} %get-tuple-element.23), channel_id=1, source_target_pairs={{32,0},{64,32},{96,64},{128,96},{160,128},{192,160},{224,192},{256... | collective-permute-start | bytes 393224 | tf_op jit(solution)/shard_map/ppermute | solution.py:346
  37.8 26.6 %collective-permute-start.5 = (f32[2,128,128]{2,1,0:T(8,128)S(1)}, f32[2,128,128]{2,1,0:T(8,128)S(1)}, u32[]{:S(2)}, u32[]{:S(2)}) collective-permute-start(f32[2,128,128]{2,1,0:T(8,128)S(1)} %shard_map.116), channel_id=1, source_target_pairs={{32,0},{64,32},{96,64},{128,96},{160,128},{192,160},{224,192},{256... | collective-permute-start | bytes 393224 | tf_op jit(solution)/shard_map/ppermute | solution.py:346
  71.2 3.8 %collective-permute-start.8 = (f32[2,256,256]{2,1,0:T(8,128)S(1)}, f32[2,256,256]{2,1,0:T(8,128)S(1)}, u32[]{:S(2)}, u32[]{:S(2)}) collective-permute-start(f32[2,256,256]{2,1,0:T(8,128)S(1)} %get-tuple-element.29), channel_id=1, source_target_pairs={{0,1},{1,0},{2,3},{3,2},{4,5},{5,4},{6,7},{7,6},{8,9},{9,8},{10,11... | collective-permute-start | bytes 1572872 | tf_op jit(solution)/shard_map/ppermute | solution.py:354
  122.2 14.0 %all-to-all-start.3 = ((f32[16,32,256]{2,1,0:T(8,128)}), f32[16,32,256]{2,1,0:T(8,128)S(1)}, u32[]{:S(2)}, u32[]{:S(2)}) async-start(f32[16,32,256]{2,1,0:T(8,128)} %broadcast_in_dim.11), calls=%async_computation.3 | async-start | bytes 1048576 | tf_op jit(solution)/shard_map/all_to_all | solution.py:350
  129.0 36.8 %copy-start.3 = (f32[2,256,256]{2,1,0:T(8,128)S(1)}, f32[2,256,256]{2,1,0:T(8,128)}, u32[]{:S(2)}) copy-start(f32[2,256,256]{2,1,0:T(8,128)} %get-tuple-element.25.grad) | copy-start | bytes 1572868
  129.0 27.1 %collective-permute-start.6 = (f32[2,128,256]{2,1,0:T(8,128)S(1)}, f32[2,128,256]{2,1,0:T(8,128)S(1)}, u32[]{:S(2)}, u32[]{:S(2)}) collective-permute-start(f32[2,128,256]{2,1,0:T(8,128)S(1)} %get-tuple-element.26), channel_id=1, source_target_pairs={{0,32},{32,64},{64,96},{96,128},{128,160},{160,192},{192,224},{224... | collective-permute-start | bytes 786440 | tf_op jit(solution)/shard_map/ppermute | solution.py:346
  136.2 31.1 %collective-permute-start.9 = (f32[2,256,256]{2,1,0:T(8,128)S(1)}, f32[2,256,256]{2,1,0:T(8,128)S(1)}, u32[]{:S(2)}, u32[]{:S(2)}) collective-permute-start(f32[2,256,256]{2,1,0:T(8,128)S(1)} %bitcast.6), channel_id=1, source_target_pairs={{0,1},{1,0},{2,3},{3,2},{4,5},{5,4},{6,7},{7,6},{8,9},{9,8},{10,11... | collective-permute-start | bytes 1572872 | tf_op jit(solution)/shard_map/ppermute | solution.py:354
  156.7 9.1 %collective-permute-start.7 = (f32[2,384,128]{2,1,0:T(8,128)S(1)}, f32[2,384,128]{2,1,0:T(8,128)S(1)}, u32[]{:S(2)}, u32[]{:S(2)}) collective-permute-start(f32[2,384,128]{2,1,0:T(8,128)S(1)} %shard_map.118), channel_id=1, source_target_pairs={{0,1},{1,2},{2,3},{3,4},{4,5},{5,6},{6,7},{7,8},{8,9},{9,10},{10,1... | collective-permute-start | bytes 1179656 | tf_op jit(solution)/shard_map/ppermute | solution.py:346
  165.8 1.5 copy-start

commit v3 on v2

--- a/solution.py
+++ b/solution.py
@@ -179,12 +179,12 @@
 
 
 def first_kernel(pos, obj, halo, probe_hbm, amp_hbm, step, high, low, high_t, low_t, rows, cols,
-                 obj_hbm, spill, edge, middle, sum_hbm, far, win, grad, probe, amp, new_obj, probe_sum, sems):
+                 new_obj, spill_top, spill_low, edge_top, edge_low, middle, sum_hbm,
+                 far, win, grad, probe, amp, probe_sum, sems):
     row, col = pos[0, 0], pos[0, 1]
     probe_copy = lambda m: pltpu.make_async_copy(probe_hbm.at[m], probe.at[m], sems.at[m])
     sum_copy = lambda m: pltpu.make_async_copy(probe_sum.at[m], sum_hbm.at[m], sems.at[2 + m])
-    obj_copy = lambda k: pltpu.make_async_copy(new_obj.at[k], obj_hbm.at[k], sems.at[4 + k])
-    amp_copy = pltpu.make_async_copy(amp_hbm.at[0], amp, sems.at[6])
+    amp_copy = pltpu.make_async_copy(amp_hbm.at[0], amp, sems.at[4])
     probe_copy(0).start()
     probe_copy(1).start()
     amp_copy.start()
@@ -209,13 +209,13 @@
         g = pltpu.roll(g, col, 1)
         updated = obj[k] + g[:, :WIN]
         new_obj[k] = updated
-        obj_copy(k).start()
-        edge[k] = updated[:, :HALO]
+        edge_top[k] = updated[:LAST, :HALO]
+        edge_low[k] = updated[LAST:, :HALO]
         middle[k] = updated[:HALO, HALO:]
-        spill[k] = g[:, WIN:]
+        spill_top[k] = g[:LAST, WIN:]
+        spill_low[k] = g[LAST:, WIN:]
     for k in range(2):
         sum_copy(k).wait()
-        obj_copy(k).wait()
 
 
 def lanes():
@@ -225,29 +225,33 @@
 def upward_kernel(above, info, edge, from_left, from_right, spill, upward):
     keep = info[0].astype(jnp.float32)
     for k in range(2):
-        own = edge[k, :HALO] + from_left[k, :HALO]
-        upward[k] = jnp.where(lanes() >= above[1, 1], own, from_right[k, :HALO] + spill[k, :HALO] * keep)
-
-
-def merge_kernel(info, obj, from_left, from_right, spill, whole, source):
+        own = edge[k] + from_left[k]
+        upward[k] = jnp.where(lanes() >= above[1, 1], own, from_right[k] + spill[k] * keep)
+
+
+def merge_kernel(info, obj, left_top, left_low, right_low, spill_low, whole_hbm, source, whole, sems):
     keep = info[0].astype(jnp.float32)
-    for k in range(2):
-        left = obj[k, :, :HALO] + from_left[k]
-        whole[k, :, :HALO] = left
+    whole_copy = lambda k: pltpu.make_async_copy(whole.at[k], whole_hbm.at[k], sems.at[k])
+    for k in range(2):
+        low = obj[k, LAST:, :HALO] + left_low[k]
+        whole[k, :LAST, :HALO] = obj[k, :LAST, :HALO] + left_top[k]
+        whole[k, LAST:, :HALO] = low
         whole[k, :, HALO:] = obj[k, :, HALO:]
-        source[k, :, :HALO] = left[LAST:]
+        whole_copy(k).start()
+        source[k, :, :HALO] = low
         source[k, :, HALO:WIN] = obj[k, LAST:, HALO:]
-        source[k, :, WIN:] = from_right[k, LAST:] + spill[k, LAST:] * keep
+        source[k, :, WIN:] = right_low[k] + spill_low[k] * keep
+    for k in range(2):
+        whole_copy(k).wait()
 
 
 def second_kernel(pos, info, source, below_mid, below_rest, probe_hbm, amp_hbm, step, before_hbm,
                   high, low, high_t, low_t, rows, cols,
-                  grad_hbm, spill, downward, keep_sum, send_sum, far, win, grad, probe, amp, own_grad, before, sems):
+                  own_grad, packed, middle, keep_sum, send_sum, far, win, grad, probe, amp, before, sems):
     row, col, core = pos[1, 0] - LAST, pos[1, 1], info[1]
     probe_copy = lambda m: pltpu.make_async_copy(probe_hbm.at[m], probe.at[m], sems.at[m])
     before_copy = lambda m: pltpu.make_async_copy(before_hbm.at[m], before.at[m], sems.at[2 + m])
-    grad_copy = lambda k: pltpu.make_async_copy(own_grad.at[k], grad_hbm.at[k], sems.at[4 + k])
-    amp_copy = pltpu.make_async_copy(amp_hbm.at[1], amp, sems.at[6])
+    amp_copy = pltpu.make_async_copy(amp_hbm.at[1], amp, sems.at[4])
     probe_copy(0).start()
     probe_copy(1).start()
     amp_copy.start()
@@ -280,28 +284,24 @@
         g = pltpu.roll(g, row, 0)
         g = jnp.concatenate([g, jnp.zeros((TILE_R, HALO), jnp.float32)], axis=1)
         g = pltpu.roll(g, col, 1)
-        own_grad[k] = g[:WIN, :WIN]
-        grad_copy(k).start()
-        downward[k, :, :HALO] = g[WIN:, :HALO] + g[WIN:, WIN:]
-        downward[k, :, HALO:] = g[WIN:, HALO:WIN]
-        spill[k] = g[:WIN, WIN:]
-    for k in range(2):
-        grad_copy(k).wait()
-
-
-def spill_kernel(above, spill, from_above, new_spill):
-    for k in range(2):
-        new_spill[k, :HALO] = jnp.where(lanes() < above[1, 1], from_above[k, :, :HALO], 0.0)
-        new_spill[k, HALO:] = spill[k]
-
-
-def object_kernel(above, whole, grad, from_above, from_left, out):
-    for k in range(2):
-        fell = jnp.where(lanes() >= above[1, 1], from_above[k, :, :HALO], 0.0)
+        own_grad[k] = g[:WIN]
+        packed[k] = g[WIN:, :HALO] + g[WIN:, WIN:]
+        middle[k] = g[WIN:, HALO:WIN]
+
+
+def spill_kernel(above, own_grad, from_above, new_spill):
+    for k in range(2):
+        new_spill[k, :HALO] = jnp.where(lanes() < above[1, 1], from_above[k], 0.0)
+        new_spill[k, HALO:] = own_grad[k, :, WIN:]
+
+
+def object_kernel(above, whole, own_grad, from_above, mid_above, from_left, out):
+    for k in range(2):
+        fell = jnp.where(lanes() >= above[1, 1], from_above[k], 0.0)
         out[k, :LAST, :HALO] = whole[k, :LAST, :HALO] + fell + from_left[k, :LAST]
-        out[k, :LAST, HALO:] = whole[k, :LAST, HALO:] + from_above[k, :, HALO:]
-        out[k, LAST:, :HALO] = whole[k, LAST:, :HALO] + grad[k, :, :HALO] + from_left[k, LAST:]
-        out[k, LAST:, HALO:] = whole[k, LAST:, HALO:] + grad[k, :, HALO:]
+        out[k, :LAST, HALO:] = whole[k, :LAST, HALO:] + mid_above[k]
+        out[k, LAST:, :HALO] = whole[k, LAST:, :HALO] + own_grad[k, :, :HALO] + from_left[k, LAST:]
+        out[k, LAST:, HALO:] = whole[k, LAST:, HALO:] + own_grad[k, :, HALO:WIN]
 
 
 def probe_kernel(info, probe, own, other, out):
@@ -314,7 +314,7 @@
 AUTO = object()
 
 
-def call(kernel, outs, scratch, scalars, arrays, copies=0):
+def call(kernel, outs, scratch, scalars, arrays, copies=0, in_place=None):
     smem = pl.BlockSpec(memory_space=pltpu.SMEM)
     specs = {None: pl.BlockSpec(memory_space=pltpu.VMEM), HBM: pl.BlockSpec(memory_space=pltpu.HBM)}
     specs[AUTO] = specs[None]
@@ -336,6 +336,7 @@
         scratch_shapes=[pltpu.VMEM(s, jnp.float32) if isinstance(s, tuple) else s for s in scratch]
         + ([pltpu.SemaphoreType.DMA((copies,))] if copies else []),
         compiler_params=pltpu.CompilerParams(vmem_limit_bytes=24 * 1024 * 1024),
+        input_output_aliases={} if in_place is None else {in_place: 0},
         interpret=INTERPRET,
     )(*scalars, *operands)
 
@@ -384,26 +385,30 @@
         before_kernel, [((BATCHES, WIN, WIN), HBM), (8, HALF)],
         [probe_shape, pltpu.VMEM((BATCHES, WIN, WIN), jnp.bfloat16), (BATCHES, WIN, WIN)],
         [], [(probe_modes, HBM), (amplitudes[0, 0], HBM)], copies=4)
-    obj, spill, edge, middle, probe_sum = call(
-        first_kernel, [(tile, HBM), side, side, block, (probe_shape, HBM)], fit_scratch + [tile, probe_shape],
-        [positions], [object_field, halo, (probe_modes, HBM), (amp, HBM), step, *tables], copies=7)
+    low = (2, WIN, HALO)
+    obj, spill_top, spill_low, edge_top, edge_low, middle, probe_sum = call(
+        first_kernel, [tile, block, low, block, low, block, (probe_shape, HBM)], fit_scratch + [probe_shape],
+        [positions], [object_field, halo, (probe_modes, HBM), (amp, HBM), step, *tables], copies=5, in_place=1)
     below_mid = passed_along(middle, ROW, -1)
-    from_right = passed_along(edge, COL, -1)
+    right_top = passed_along(edge_top, COL, -1)
+    left_top = passed_along(spill_top, COL, 1)
+    (upward,) = call(upward_kernel, [block], [], [above, info], [edge_top, left_top, right_top, spill_top])
+    below_rest = passed_along(upward, ROW, -1)
+    right_low = passed_along(edge_low, COL, -1)
+    left_low = passed_along(spill_low, COL, 1)
+    whole, source = call(
+        merge_kernel, [(tile, HBM), (2, WIN, WIDE)], [tile], [info], [obj, left_top, left_low, right_low, spill_low], copies=2)
+    grad, packed, middle, keep, send = call(
+        second_kernel, [(2, WIN, WIDE), block, block, window, window],
+        fit_scratch + [probe_shape], [positions, info],
+        [source, below_mid, below_rest, (probe_modes, HBM), (amp, HBM), step, (probe_sum, HBM), *tables], copies=5, in_place=2)
+    own, other = summed_everywhere(keep, send, divisor)
+    from_above = passed_along(packed, ROW, 1)
+    (spill,) = call(spill_kernel, [side], [], [above], [grad, from_above])
     from_left = passed_along(spill, COL, 1)
-    (upward,) = call(upward_kernel, [block], [], [above, info], [edge, from_left, from_right, spill])
-    below_rest = passed_along(upward, ROW, -1)
-    whole, source = call(
-        merge_kernel, [(tile, AUTO), (2, WIN, WIDE)], [], [info], [(obj, AUTO), from_left, from_right, spill])
-    grad, spill, downward, keep, send = call(
-        second_kernel, [(window, HBM), (2, WIN, HALO), (2, HALO, WIN), window, window],
-        fit_scratch + [window, probe_shape], [positions, info],
-        [source, below_mid, below_rest, (probe_modes, HBM), (amp, HBM), step, (probe_sum, HBM), *tables], copies=7)
-    own, other = summed_everywhere(keep, send, divisor)
-    from_above = passed_along(downward, ROW, 1)
-    (spill,) = call(spill_kernel, [side], [], [above], [spill, from_above])
-    from_left = passed_along(spill, COL, 1)
+    mid_above = passed_along(middle, ROW, 1)
     (object_out,) = call(
-        object_kernel, [(tile, AUTO)], [], [above], [(whole, AUTO), (grad, AUTO), from_above, from_left])
+        object_kernel, [(tile, AUTO)], [], [above], [(whole, AUTO), (grad, AUTO), from_above, mid_above, from_left])
     (probe_out,) = call(probe_kernel, [(probe_shape, AUTO)], [], [info], [(probe_modes, AUTO), own, other])
     return (object_out, probe_out)
 

time: 170 us -> 182 us (1.071)
  the two profiles are of different devices: /device:TPU:10 before, /device:TPU:93 now
where the time goes in v3:
time: 182 us; the launch traced here: 181 us
  starting transfers between devices  71.8 us (39%)
  blocking collectives  51.3 us (28%)
  waiting for transfers between devices  33.5 us (18%)
  Pallas kernels  20.5 us (11%)
  local copies, waits for them, and re-layouts  2.71 us (1%)
    ppermute x11, starting transfers between devices, passed_along(): return lax.ppermute(block, axis, route)  52.2 us
    all_to_all x3, blocking collectives, exchanged(): return lax.all_to_all(parts, axes, 0, 0, tiled=False)  51.3 us
    ppermute x11, waiting for transfers between devices, passed_along(): return lax.ppermute(block, axis, route)  30.5 us
    pallas_call x8, Pallas kernels, call(): pl.pallas_call(kernel, out_shape=shapes, in_specs=[smem] * len(scalars) +...  20.5 us
    ppermute x2, starting transfers between devices, swapped(): return lax.ppermute(block, CORE, [(0, 1), (1, 0)])  12.4 us
    all_to_all x1, starting transfers between devices, exchanged(): return lax.all_to_all(parts, axes, 0, 0, tiled=False)  7.25 us
  transfers between devices with their start and end apart: 14, of which 6 were waited for; matrix products, arithmetic and copies ran while one was open for 0% of the time, Pallas kernels for 4%

profile of v3, /device:TPU:93, one launch (start us, length us, event | category | flops | bytes accessed | tf_op | source)
XLA Modules:
  0.0 181.0 jit_solution(11917718795708125155)
XLA Ops:
  0.6 1.1 copy.17.obj
  1.8 2.6 %collective-permute-start.1 = (f32[2,384,128]{2,1,0:T(8,128)S(1)}, f32[2,384,128]{2,1,0:T(8,128)S(1)}, u32[]{:S(2)}, u32[]{:S(2)}) collective-permute-start(f32[2,384,128]{2,1,0:T(8,128)S(1)} %slice.3), channel_id=1, source_target_pairs={{1,0},{2,1},{3,2},{4,3},{5,4},{6,5},{7,6},{8,7},{9,8},{10,9},{11,1... | collective-permute-start | bytes 1179656 | tf_op jit(solution)/shard_map/ppermute | solution.py:347
  4.4 0.0 copy-start.2
  4.4 0.0 copy-start.3
  4.4 0.0 copy-start.4
  4.4 0.0 copy-start.5
  4.4 0.0 copy-start.6
  4.4 0.0 copy-start.7
  4.5 2.2 %shard_map.113 = (f32[2,256,256]{2,1,0:T(8,128)}, f32[8,128]{1,0:T(8,128)S(1)}) custom-call(f32[2,2,256,256]{3,2,1,0:T(8,128)} %probe.1, bf16[2,256,256]{2,1,0:T(8,128)(2,1)} %bitcast.12), custom_call_target="tpu_custom_call" | custom-call | tf_op jit(solution)/shard_map/pallas_call | solution.py:331
  6.7 4.2 %collective-permute-done.1.halo = f32[2,384,128]{2,1,0:T(8,128)S(1)} collective-permute-done((f32[2,384,128]{2,1,0:T(8,128)S(1)}, f32[2,384,128]{2,1,0:T(8,128)S(1)}, u32[]{:S(2)}, u32[]{:S(2)}) %collective-permute-start.1) | collective-permute-done | bytes 393248 | tf_op jit(solution)/shard_map/ppermute | solution.py:347
  10.9 0.0 copy-start.8
  10.9 0.0 copy-done.2
  10.9 0.0 copy-done.3
  10.9 0.0 copy-done.4
  10.9 0.0 copy-done.5
  10.9 0.0 copy-done.6
  10.9 0.0 copy-done.7
  10.9 0.6 copy-done.8
  11.6 6.4 %shard_map.114 = (f32[2,384,256]{2,1,0:T(8,128)S(1)}, f32[2,128,128]{2,1,0:T(8,128)S(1)}, f32[2,256,128]{2,1,0:T(8,128)S(1)}, f32[2,128,128]{2,1,0:T(8,128)S(1)}...) custom-call(s32[2,2]{1,0:T(2,128)S(1)} %bitcast.8, ...), custom_call_target="tpu_custom_call", output_to_operand_aliasing={{0}: (1, {})} | custom-call | tf_op jit(solution)/shard_map/pallas_call | solution.py:331
  18.0 1.9 %collective-permute-start.2 = (f32[2,128,128]{2,1,0:T(8,128)S(1)}, f32[2,128,128]{2,1,0:T(8,128)S(1)}, u32[]{:S(2)}, u32[]{:S(2)}) collective-permute-start(f32[2,128,128]{2,1,0:T(8,128)S(1)} %get-tuple-element.21.spill), channel_id=1, source_target_pairs={{0,1},{1,2},{2,3},{3,4},{4,5},{5,6},{6,7},{7,8},{8,9},{9,10},{10,1... | collective-permute-start | bytes 393224 | tf_op jit(solution)/shard_map/ppermute | solution.py:347
  19.9 2.4 %collective-permute-start.4 = (f32[2,256,128]{2,1,0:T(8,128)S(1)}, f32[2,256,128]{2,1,0:T(8,128)S(1)}, u32[]{:S(2)}, u32[]{:S(2)}) collective-permute-start(f32[2,256,128]{2,1,0:T(8,128)S(1)} %get-tuple-element.23), channel_id=1, source_target_pairs={{1,0},{2,1},{3,2},{4,3},{5,4},{6,5},{7,6},{8,7},{9,8},{10,9},{11,1... | collective-permute-start | bytes 786440 | tf_op jit(solution)/shard_map/ppermute | solution.py:347
  22.3 4.8 %collective-permute-start.3 = (f32[2,256,128]{2,1,0:T(8,128)S(1)}, f32[2,256,128]{2,1,0:T(8,128)S(1)}, u32[]{:S(2)}, u32[]{:S(2)}) collective-permute-start(f32[2,256,128]{2,1,0:T(8,128)S(1)} %get-tuple-element.22.spill_low), channel_id=1, source_target_pairs={{0,1},{1,2},{2,3},{3,4},{4,5},{5,6},{6,7},{7,8},{8,9},{9,10},{10,1... | collective-permute-start | bytes 786440 | tf_op jit(solution)/shard_map/ppermute | solution.py:347
  27.2 1.9 %collective-permute-start.6 = (f32[2,128,128]{2,1,0:T(8,128)S(1)}, f32[2,128,128]{2,1,0:T(8,128)S(1)}, u32[]{:S(2)}, u32[]{:S(2)}) collective-permute-start(f32[2,128,128]{2,1,0:T(8,128)S(1)} %get-tuple-element.27.edge), channel_id=1, source_target_pairs={{1,0},{2,1},{3,2},{4,3},{5,4},{6,5},{7,6},{8,7},{9,8},{10,9},{11,1... | collective-permute-start | bytes 393224 | tf_op jit(solution)/shard_map/ppermute | solution.py:347
  29.1 8.8 %collective-permute-start = (s32[2,2]{1,0:T(2,128)S(1)}, s32[2,2]{1,0:T(2,128)S(1)}, u32[]{:S(2)}, u32[]{:S(2)}) collective-permute-start(s32[2,2]{1,0:T(2,128)S(1)} %bitcast.9), channel_id=1, source_target_pairs={{0,32},{32,64},{64,96},{96,128},{128,160},{160,192},{192,224},{224... | collective-permute-start | bytes 56 | tf_op jit(solution)/shard_map/ppermute | solution.py:347
  37.9 0.1 pad_add_fusion.info
  38.0 2.9 %collective-permute-done.above = s32[2,2]{1,0:T(2,128)S(1)} collective-permute-done((s32[2,2]{1,0:T(2,128)S(1)}, s32[2,2]{1,0:T(2,128)S(1)}, u32[]{:S(2)}, u32[]{:S(2)}) %collective-permute-start) | collective-permute-done | bytes 48 | tf_op jit(solution)/shard_map/ppermute | solution.py:347
  40.9 7.3 %collective-permute-start.5 = (f32[2,128,128]{2,1,0:T(8,128)S(1)}, f32[2,128,128]{2,1,0:T(8,128)S(1)}, u32[]{:S(2)}, u32[]{:S(2)}) collective-permute-start(f32[2,128,128]{2,1,0:T(8,128)S(1)} %get-tuple-element.26), channel_id=1, source_target_pairs={{32,0},{64,32},{96,64},{128,96},{160,128},{192,160},{224,192},{256... | collective-permute-start | bytes 393224 | tf_op jit(solution)/shard_map/ppermute | solution.py:347
  48.1 0.0 collective-permute-done.2.left_top.from_left
  48.1 0.0 collective-permute-done.6.from_right
  48.2 0.6 shard_map.116
  48.7 5.2 %collective-permute-start.7 = (f32[2,128,128]{2,1,0:T(8,128)S(1)}, f32[2,128,128]{2,1,0:T(8,128)S(1)}, u32[]{:S(2)}, u32[]{:S(2)}) collective-permute-start(f32[2,128,128]{2,1,0:T(8,128)S(1)} %shard_map.116), channel_id=1, source_target_pairs={{32,0},{64,32},{96,64},{128,96},{160,128},{192,160},{224,192},{256... | collective-permute-start | bytes 393224 | tf_op jit(solution)/shard_map/ppermute | solution.py:347
  53.9 0.0 collective-permute-done.4.right_low
  53.9 0.0 collective-permute-done.3.left_low
  54.0 1.5 shard_map.115
  55.4 0.0 collective-permute-done.5.below_mid
  55.4 5.7 %collective-permute-done.7.below_rest = f32[2,128,128]{2,1,0:T(8,128)S(1)} collective-permute-done((f32[2,128,128]{2,1,0:T(8,128)S(1)}, f32[2,128,128]{2,1,0:T(8,128)S(1)}, u32[]{:S(2)}, u32[]{:S(2)}) %collective-permute-start.7) | collective-permute-done | bytes 131104 | tf_op jit(solution)/shard_map/ppermute | solution.py:347
  61.1 6.1 %shard_map.117 = (f32[2,256,384]{2,1,0:T(8,128)S(1)}, f32[2,128,128]{2,1,0:T(8,128)S(1)}, f32[2,128,128]{2,1,0:T(8,128)S(1)}, f32[2,256,256]{2,1,0:T(8,128)S(1)}, f32[2,256,256]{2,1,0:T(8,128)S(1)}) custom-call(s32[2,2]{1,0:T(2,128)S(1)} %bitcast.10, s32[2]{0:T(128)S(1)} %pad_add_fusion.info, ...), custom_call_target="tpu_custom_call", output_to_operand_aliasing={{0}: (2, {})} | custom-call | tf_op jit(solution)/shard_map/pallas_call | solution.py:331
  67.2 3.9 %collective-permute-start.11 = (f32[2,256,256]{2,1,0:T(8,128)S(1)}, f32[2,256,256]{2,1,0:T(8,128)S(1)}, u32[]{:S(2)}, u32[]{:S(2)}) collective-permute-start(f32[2,256,256]{2,1,0:T(8,128)S(1)} %get-tuple-element.33), channel_id=1, source_target_pairs={{0,1},{1,0},{2,3},{3,2},{4,5},{5,4},{6,7},{7,6},{8,9},{9,8},{10,11... | collective-permute-start | bytes 1572872 | tf_op jit(solution)/shard_map/ppermute | solution.py:355
  71.1 1.5 collective-permute-done.11
  72.6 0.1 add.11
  72.7 16.7 %all_to_all.20 = f32[16,32,256]{2,1,0:T(8,128)S(1)} all-to-all(f32[16,32,256]{2,1,0:T(8,128)S(1)} %bitcast.11), channel_id=1, replica_groups=mesh['row_0'=4,'row_1'=4,'col_0'=4,'col_1'=4,'col_2'=2] {'row_0','col_1'}, dimensions={0} | all-to-all | bytes 1048576 | tf_op jit(solution)/shard_map/all_to_all | solution.py:351
  89.4 15.2 %all_to_all.21 = f32[4,32,256]{2,1,0:T(8,128)S(1)} all-to-all(f32[4,32,256]{2,1,0:T(8,128)S(1)} %broadcast_in_dim.9), channel_id=1, replica_groups=mesh['row_0'=4,'row_1'=4,'col_0'=4,'col_1'=4,'col_2'=2] {'col_0'}, dimensions={0} | all-to-all | bytes 262144 | tf_op jit(solution)/shard_map/all_to_all | solution.py:351
  104.6 19.5 %all_to_all.22 = f32[4,32,256]{2,1,0:T(8,128)S(1)} all-to-all(f32[4,32,256]{2,1,0:T(8,128)S(1)} %broadcast_in_dim.10), channel_id=1, replica_groups=mesh['row_0'=4,'row_1'=4,'col_0'=4,'col_1'=4,'col_2'=2] {'row_1'}, dimensions={0} | all-to-all | bytes 262144 | tf_op jit(solution)/shard_map/all_to_all | solution.py:351
  124.1 0.8 broadcast_in_dim.11
  125.0 7.3 %all-to-all-start.3 = ((f32[16,32,256]{2,1,0:T(8,128)}), f32[16,32,256]{2,1,0:T(8,128)S(1)}, u32[]{:S(2)}, u32[]{:S(2)}) async-start(f32[16,32,256]{2,1,0:T(8,128)} %broadcast_in_dim.11), calls=%async_computation.3 | async-start | bytes 1048576 | tf_op jit(solution)/shard_map/all_to_all | solution.py:351
  132.2 0.0 copy-start.1
  132.2 3.7 %collective-permute-start.8 = (f32[2,128,128]{2,1,0:T(8,128)S(1)}, f32[2,128,128]{2,1,0:T(8,128)S(1)}, u32[]{:S(2)}, u32[]{:S(2)}) collective-permute-start(f32[2,128,128]{2,1,0:T(8,128)S(1)} %get-tuple-element.30), channel_id=1, source_target_pairs={{0,32},{32,64},{64,96},{96,128},{128,160},{160,192},{192,224},{224... | collective-permute-start | bytes 393224 | tf_op jit(solution)/shard_map/ppermute | solution.py:347
  135.9 1.4 all-to-all-done.3
  137.3 8.5 %collective-permute-start.12 = (f32[2,256,256]{2,1,0:T(8,128)S(1)}, f32[2,256,256]{2,1,0:T(8,128)S(1)}, u32[]{:S(2)}, u32[]{:S(2)}) collective-permute-start(f32[2,256,256]{2,1,0:T(8,128)S(1)} %bitcast.6), channel_id=1, source_target_pairs={{0,1},{1,0},{2,3},{3,2},{4,5},{5,4},{6,7},{7,6},{8,9},{9,8},{10,11... | collective-permute-start | bytes 1572872 | tf_op jit(solution)/shard_map/ppermute | solution.py:355
  145.9 0.0 collective-permute-done.8.from_above
  145.9 0.6 shard_map.118
  146.5 11.7 %collective-permute-start.10 = (f32[2,384,128]{2,1,0:T(8,128)S(1)}, f32[2,384,128]{2,1,0:T(8,128)S(1)}, u32[]{:S(2)}, u32[]{:S(2)}) collective-permute-start(f32[2,384,128]{2,1,0:T(8,128)S(1)} %shard_map.118), channel_id=1, source_target_pairs={{0,1},{1,2},{2,3},{3,4},{4,5},{5,6},{6,7},{7,8},{8,9},{9,10},{10,1... | collective-permute-start | bytes 1179656 | tf_op jit(solution)/shard_map/ppermute | solution.py:347
  158.1 1.9 %collective-permute-start.9 = (f32[2,128,128]{2,1,0:T(8,128)S(1)}, f32[2,128,128]{2,1,0:T(8,128)S(1)}, u32[]{:S(2)}, u32[]{:S(2)}) collective-permute-start(f32[2,128,128]{2,1,0:T(8,128)S(1)} %get-tuple-element.31), channel_id=1, source_target_pairs={{0,32},{32,64},{64,96},{96,128},{128,160},{160,192},{192,224},{224... | collective-permute-start | bytes 393224 | tf_op jit(solution)/shard_map/ppermute | solution.py:347
  160.1 17.8 %collective-permute-done.9.mid_above = f32[2,128,128]{2,1,0:T(8,128)S(1)} collective-permute-done((f32[2,128,128]{2,1,0:T(8,128)S(1)}, f32[2,128,128]{2,1,0:T(8,128)S(1)}, u32[]{:S(2)}, u32[]{:S(2)}) %collective-permute-start.9) | collective-permute-done | bytes 131104 | tf_op jit(solution)/shard_map/ppermute | solution.py:347
  177.8 0.0 collective-permute-done.10.from_left
  177.8 0.0 copy-done.1
  177.9 0.0 copy-start
  177.9 1.6 shard_map.119
  179.4 0.0 collective-permute-done.12.other
  179.4 0.0 copy-done
  179.4 1.6 shard_map.120
  (7 shorter events, 0.1 us)
Async XLA Ops:
  1.8 9.1 %collective-permute-start.1 = (f32[2,384,128]{2,1,0:T(8,128)S(1)}, f32[2,384,128]{2,1,0:T(8,128)S(1)}, u32[]{:S(2)}, u32[]{:S(2)}) collective-permute-start(f32[2,384,128]{2,1,0:T(8,128)S(1)} %slice.3), channel_id=1, source_target_pairs={{1,0},{2,1},{3,2},{4,3},{5,4},{6,5},{7,6},{8,7},{9,8},{10,9},{11,1... | collective-permute-start | bytes 1179656 | tf_op jit(solution)/shard_map/ppermute | solution.py:347
  4.4 6.5 %copy-start.2 = (f32[2,128,128]{2,1,0:T(8,128)S(1)}, f32[2,128,128]{2,1,0:T(8,128)}, u32[]{:S(2)}) copy-start(f32[2,128,128]{2,1,0:T(8,128)} %constant.38.clone.rows) | copy-start | bytes 393220
  4.4 6.5 %copy-start.3 = (bf16[256,256]{1,0:T(8,128)(2,1)S(1)}, bf16[256,256]{1,0:T(8,128)(2,1)}, u32[]{:S(2)}) copy-start(bf16[256,256]{1,0:T(8,128)(2,1)} %constant.37.clone.low_t) | copy-start | bytes 393220
  4.4 6.5 %copy-start.4 = (bf16[256,256]{1,0:T(8,128)(2,1)S(1)}, bf16[256,256]{1,0:T(8,128)(2,1)}, u32[]{:S(2)}) copy-start(bf16[256,256]{1,0:T(8,128)(2,1)} %constant.36.clone.high_t) | copy-start | bytes 393220
  4.4 6.5 %copy-start.5 = (bf16[256,256]{1,0:T(8,128)(2,1)S(1)}, bf16[256,256]{1,0:T(8,128)(2,1)}, u32[]{:S(2)}) copy-start(bf16[256,256]{1,0:T(8,128)(2,1)} %constant.35.clone.low) | copy-start | bytes 393220
  4.4 6.5 %copy-start.6 = (bf16[256,256]{1,0:T(8,128)(2,1)S(1)}, bf16[256,256]{1,0:T(8,128)(2,1)}, u32[]{:S(2)}) copy-start(bf16[256,256]{1,0:T(8,128)(2,1)} %constant.34.clone.high) | copy-start | bytes 393220
  4.4 6.5 %copy-start.7 = (f32[2,8,128]{2,1,0:T(8,128)S(1)}, f32[2,8,128]{2,1,0:T(8,128)}, u32[]{:S(2)}) copy-start(f32[2,8,128]{2,1,0:T(8,128)} %constant.39.clone.cols) | copy-start | bytes 24580
  10.9 0.7 copy-start.8
  18.0 30.2 %collective-permute-start.2 = (f32[2,128,128]{2,1,0:T(8,128)S(1)}, f32[2,128,128]{2,1,0:T(8,128)S(1)}, u32[]{:S(2)}, u32[]{:S(2)}) collective-permute-start(f32[2,128,128]{2,1,0:T(8,128)S(1)} %get-tuple-element.21.spill), channel_id=1, source_target_pairs={{0,1},{1,2},{2,3},{3,4},{4,5},{5,6},{6,7},{7,8},{8,9},{9,10},{10,1... | collective-permute-start | bytes 393224 | tf_op jit(solution)/shard_map/ppermute | solution.py:347
  19.9 34.0 %collective-permute-start.4 = (f32[2,256,128]{2,1,0:T(8,128)S(1)}, f32[2,256,128]{2,1,0:T(8,128)S(1)}, u32[]{:S(2)}, u32[]{:S(2)}) collective-permute-start(f32[2,256,128]{2,1,0:T(8,128)S(1)} %get-tuple-element.23), channel_id=1, source_target_pairs={{1,0},{2,1},{3,2},{4,3},{5,4},{6,5},{7,6},{8,7},{9,8},{10,9},{11,1... | collective-permute-start | bytes 786440 | tf_op jit(solution)/shard_map/ppermute | solution.py:347
  22.3 31.6 %collective-permute-start.3 = (f32[2,256,128]{2,1,0:T(8,128)S(1)}, f32[2,256,128]{2,1,0:T(8,128)S(1)}, u32[]{:S(2)}, u32[]{:S(2)}) collective-permute-start(f32[2,256,128]{2,1,0:T(8,128)S(1)} %get-tuple-element.22.spill_low), channel_id=1, source_target_pairs={{0,1},{1,2},{2,3},{3,4},{4,5},{5,6},{6,7},{7,8},{8,9},{9,10},{10,1... | collective-permute-start | bytes 786440 | tf_op jit(solution)/shard_map/ppermute | solution.py:347
  27.2 21.0 %collective-permute-start.6 = (f32[2,128,128]{2,1,0:T(8,128)S(1)}, f32[2,128,128]{2,1,0:T(8,128)S(1)}, u32[]{:S(2)}, u32[]{:S(2)}) collective-permute-start(f32[2,128,128]{2,1,0:T(8,128)S(1)} %get-tuple-element.27.edge), channel_id=1, source_target_pairs={{1,0},{2,1},{3,2},{4,3},{5,4},{6,5},{7,6},{8,7},{9,8},{10,9},{11,1... | collective-permute-start | bytes 393224 | tf_op jit(solution)/shard_map/ppermute | solution.py:347
  29.1 11.8 %collective-permute-start = (s32[2,2]{1,0:T(2,128)S(1)}, s32[2,2]{1,0:T(2,128)S(1)}, u32[]{:S(2)}, u32[]{:S(2)}) collective-permute-start(s32[2,2]{1,0:T(2,128)S(1)} %bitcast.9), channel_id=1, source_target_pairs={{0,32},{32,64},{64,96},{96,128},{128,160},{160,192},{192,224},{224... | collective-permute-start | bytes 56 | tf_op jit(solution)/shard_map/ppermute | solution.py:347
  40.9 14.6 %collective-permute-start.5 = (f32[2,128,128]{2,1,0:T(8,128)S(1)}, f32[2,128,128]{2,1,0:T(8,128)S(1)}, u32[]{:S(2)}, u32[]{:S(2)}) collective-permute-start(f32[2,128,128]{2,1,0:T(8,128)S(1)} %get-tuple-element.26), channel_id=1, source_target_pairs={{32,0},{64,32},{96,64},{128,96},{160,128},{192,160},{224,192},{256... | collective-permute-start | bytes 393224 | tf_op jit(solution)/shard_map/ppermute | solution.py:347
  48.7 12.4 %collective-permute-start.7 = (f32[2,128,128]{2,1,0:T(8,128)S(1)}, f32[2,128,128]{2,1,0:T(8,128)S(1)}, u32[]{:S(2)}, u32[]{:S(2)}) collective-permute-start(f32[2,128,128]{2,1,0:T(8,128)S(1)} %shard_map.116), channel_id=1, source_target_pairs={{32,0},{64,32},{96,64},{128,96},{160,128},{192,160},{224,192},{256... | collective-permute-start | bytes 393224 | tf_op jit(solution)/shard_map/ppermute | solution.py:347
  67.2 5.4 %collective-permute-start.11 = (f32[2,256,256]{2,1,0:T(8,128)S(1)}, f32[2,256,256]{2,1,0:T(8,128)S(1)}, u32[]{:S(2)}, u32[]{:S(2)}) collective-permute-start(f32[2,256,256]{2,1,0:T(8,128)S(1)} %get-tuple-element.33), channel_id=1, source_target_pairs={{0,1},{1,0},{2,3},{3,2},{4,5},{5,4},{6,7},{7,6},{8,9},{9,8},{10,11... | collective-permute-start | bytes 1572872 | tf_op jit(solution)/shard_map/ppermute | solution.py:355
  125.0 12.3 %all-to-all-start.3 = ((f32[16,32,256]{2,1,0:T(8,128)}), f32[16,32,256]{2,1,0:T(8,128)S(1)}, u32[]{:S(2)}, u32[]{:S(2)}) async-start(f32[16,32,256]{2,1,0:T(8,128)} %broadcast_in_dim.11), calls=%async_computation.3 | async-start | bytes 1048576 | tf_op jit(solution)/shard_map/all_to_all | solution.py:351
  132.2 45.6 %copy-start.1 = (f32[2,384,256]{2,1,0:T(8,128)S(1)}, f32[2,384,256]{2,1,0:T(8,128)}, u32[]{:S(2)}) copy-start(f32[2,384,256]{2,1,0:T(8,128)} %get-tuple-element.24.whole) | copy-start | bytes 2359300
  132.2 13.6 %collective-permute-start.8 = (f32[2,128,128]{2,1,0:T(8,128)S(1)}, f32[2,128,128]{2,1,0:T(8,128)S(1)}, u32[]{:S(2)}, u32[]{:S(2)}) collective-permute-start(f32[2,128,128]{2,1,0:T(8,128)S(1)} %get-tuple-element.30), channel_id=1, source_target_pairs={{0,32},{32,64},{64,96},{96,128},{128,160},{160,192},{192,224},{224... | collective-permute-start | bytes 393224 | tf_op jit(solution)/shard_map/ppermute | solution.py:347
  137.3 42.1 %collective-permute-start.12 = (f32[2,256,256]{2,1,0:T(8,128)S(1)}, f32[2,256,256]{2,1,0:T(8,128)S(1)}, u32[]{:S(2)}, u32[]{:S(2)}) collective-permute-start(f32[2,256,256]{2,1,0:T(8,128)S(1)} %bitcast.6), channel_id=1, source_target_pairs={{0,1},{1,0},{2,3},{3,2},{4,5},{5,4},{6,7},{7,6},{8,9},{9,8},{10,11... | collective-permute-start | bytes 1572872 | tf_op jit(solution)/shard_map/ppermute | solution.py:355
  146.5 31.4 %collective-permute-start.10 = (f32[2,384,128]{2,1,0:T(8,128)S(1)}, f32[2,384,128]{2,1,0:T(8,128)S(1)}, u32[]{:S(2)}, u32[]{:S(2)}) collective-permute-start(f32[2,384,128]{2,1,0:T(8,128)S(1)} %shard_map.118), channel_id=1, source_target_pairs={{0,1},{1,2},{2,3},{3,4},{4,5},{5,6},{6,7},{7,8},{8,9},{9,10},{10,1... | collective-permute-start | bytes 1179656 | tf_op jit(solution)/shard_map/ppermute | solution.py:347
  158.1 19.7 %collective-permute-start.9 = (f32[2,128,128]{2,1,0:T(8,128)S(1)}, f32[2,128,128]{2,1,0:T(8,128)S(1)}, u32[]{:S(2)}, u32[]{:S(2)}) collective-permute-start(f32[2,128,128]{2,1,0:T(8,128)S(1)} %get-tuple-element.31), channel_id=1, source_target_pairs={{0,32},{32,64},{64,96},{96,128},{128,160},{160,192},{192,224},{224... | collective-permute-start | bytes 393224 | tf_op jit(solution)/shard_map/ppermute | solution.py:347
  177.9 1.6 copy-start

commit v4 on v2

--- a/solution.py
+++ b/solution.py
@@ -179,12 +179,12 @@
 
 
 def first_kernel(pos, obj, halo, probe_hbm, amp_hbm, step, high, low, high_t, low_t, rows, cols,
-                 obj_hbm, spill, edge, middle, sum_hbm, far, win, grad, probe, amp, new_obj, probe_sum, sems):
+                 new_obj, spill, edge, middle, sum_hbm,
+                 far, win, grad, probe, amp, probe_sum, sems):
     row, col = pos[0, 0], pos[0, 1]
     probe_copy = lambda m: pltpu.make_async_copy(probe_hbm.at[m], probe.at[m], sems.at[m])
     sum_copy = lambda m: pltpu.make_async_copy(probe_sum.at[m], sum_hbm.at[m], sems.at[2 + m])
-    obj_copy = lambda k: pltpu.make_async_copy(new_obj.at[k], obj_hbm.at[k], sems.at[4 + k])
-    amp_copy = pltpu.make_async_copy(amp_hbm.at[0], amp, sems.at[6])
+    amp_copy = pltpu.make_async_copy(amp_hbm.at[0], amp, sems.at[4])
     probe_copy(0).start()
     probe_copy(1).start()
     amp_copy.start()
@@ -209,13 +209,11 @@
         g = pltpu.roll(g, col, 1)
         updated = obj[k] + g[:, :WIN]
         new_obj[k] = updated
-        obj_copy(k).start()
         edge[k] = updated[:, :HALO]
         middle[k] = updated[:HALO, HALO:]
         spill[k] = g[:, WIN:]
     for k in range(2):
         sum_copy(k).wait()
-        obj_copy(k).wait()
 
 
 def lanes():
@@ -229,25 +227,28 @@
         upward[k] = jnp.where(lanes() >= above[1, 1], own, from_right[k, :HALO] + spill[k, :HALO] * keep)
 
 
-def merge_kernel(info, obj, from_left, from_right, spill, whole, source):
+def merge_kernel(info, obj, from_left, from_right, spill, whole_hbm, source, whole, sems):
     keep = info[0].astype(jnp.float32)
+    whole_copy = lambda k: pltpu.make_async_copy(whole.at[k], whole_hbm.at[k], sems.at[k])
     for k in range(2):
         left = obj[k, :, :HALO] + from_left[k]
         whole[k, :, :HALO] = left
         whole[k, :, HALO:] = obj[k, :, HALO:]
+        whole_copy(k).start()
         source[k, :, :HALO] = left[LAST:]
         source[k, :, HALO:WIN] = obj[k, LAST:, HALO:]
         source[k, :, WIN:] = from_right[k, LAST:] + spill[k, LAST:] * keep
+    for k in range(2):
+        whole_copy(k).wait()
 
 
 def second_kernel(pos, info, source, below_mid, below_rest, probe_hbm, amp_hbm, step, before_hbm,
                   high, low, high_t, low_t, rows, cols,
-                  grad_hbm, spill, downward, keep_sum, send_sum, far, win, grad, probe, amp, own_grad, before, sems):
+                  own_grad, downward, keep_sum, send_sum, far, win, grad, probe, amp, before, sems):
     row, col, core = pos[1, 0] - LAST, pos[1, 1], info[1]
     probe_copy = lambda m: pltpu.make_async_copy(probe_hbm.at[m], probe.at[m], sems.at[m])
     before_copy = lambda m: pltpu.make_async_copy(before_hbm.at[m], before.at[m], sems.at[2 + m])
-    grad_copy = lambda k: pltpu.make_async_copy(own_grad.at[k], grad_hbm.at[k], sems.at[4 + k])
-    amp_copy = pltpu.make_async_copy(amp_hbm.at[1], amp, sems.at[6])
+    amp_copy = pltpu.make_async_copy(amp_hbm.at[1], amp, sems.at[4])
     probe_copy(0).start()
     probe_copy(1).start()
     amp_copy.start()
@@ -280,28 +281,24 @@
         g = pltpu.roll(g, row, 0)
         g = jnp.concatenate([g, jnp.zeros((TILE_R, HALO), jnp.float32)], axis=1)
         g = pltpu.roll(g, col, 1)
-        own_grad[k] = g[:WIN, :WIN]
-        grad_copy(k).start()
+        own_grad[k] = g[:WIN]
         downward[k, :, :HALO] = g[WIN:, :HALO] + g[WIN:, WIN:]
         downward[k, :, HALO:] = g[WIN:, HALO:WIN]
-        spill[k] = g[:WIN, WIN:]
-    for k in range(2):
-        grad_copy(k).wait()
-
-
-def spill_kernel(above, spill, from_above, new_spill):
+
+
+def spill_kernel(above, own_grad, from_above, new_spill):
     for k in range(2):
         new_spill[k, :HALO] = jnp.where(lanes() < above[1, 1], from_above[k, :, :HALO], 0.0)
-        new_spill[k, HALO:] = spill[k]
-
-
-def object_kernel(above, whole, grad, from_above, from_left, out):
+        new_spill[k, HALO:] = own_grad[k, :, WIN:]
+
+
+def object_kernel(above, whole, own_grad, from_above, from_left, out):
     for k in range(2):
         fell = jnp.where(lanes() >= above[1, 1], from_above[k, :, :HALO], 0.0)
         out[k, :LAST, :HALO] = whole[k, :LAST, :HALO] + fell + from_left[k, :LAST]
         out[k, :LAST, HALO:] = whole[k, :LAST, HALO:] + from_above[k, :, HALO:]
-        out[k, LAST:, :HALO] = whole[k, LAST:, :HALO] + grad[k, :, :HALO] + from_left[k, LAST:]
-        out[k, LAST:, HALO:] = whole[k, LAST:, HALO:] + grad[k, :, HALO:]
+        out[k, LAST:, :HALO] = whole[k, LAST:, :HALO] + own_grad[k, :, :HALO] + from_left[k, LAST:]
+        out[k, LAST:, HALO:] = whole[k, LAST:, HALO:] + own_grad[k, :, HALO:WIN]
 
 
 def probe_kernel(info, probe, own, other, out):
@@ -314,7 +311,7 @@
 AUTO = object()
 
 
-def call(kernel, outs, scratch, scalars, arrays, copies=0):
+def call(kernel, outs, scratch, scalars, arrays, copies=0, in_place=None):
     smem = pl.BlockSpec(memory_space=pltpu.SMEM)
     specs = {None: pl.BlockSpec(memory_space=pltpu.VMEM), HBM: pl.BlockSpec(memory_space=pltpu.HBM)}
     specs[AUTO] = specs[None]
@@ -336,6 +333,7 @@
         scratch_shapes=[pltpu.VMEM(s, jnp.float32) if isinstance(s, tuple) else s for s in scratch]
         + ([pltpu.SemaphoreType.DMA((copies,))] if copies else []),
         compiler_params=pltpu.CompilerParams(vmem_limit_bytes=24 * 1024 * 1024),
+        input_output_aliases={} if in_place is None else {in_place: 0},
         interpret=INTERPRET,
     )(*scalars, *operands)
 
@@ -385,22 +383,22 @@
         [probe_shape, pltpu.VMEM((BATCHES, WIN, WIN), jnp.bfloat16), (BATCHES, WIN, WIN)],
         [], [(probe_modes, HBM), (amplitudes[0, 0], HBM)], copies=4)
     obj, spill, edge, middle, probe_sum = call(
-        first_kernel, [(tile, HBM), side, side, block, (probe_shape, HBM)], fit_scratch + [tile, probe_shape],
-        [positions], [object_field, halo, (probe_modes, HBM), (amp, HBM), step, *tables], copies=7)
-    below_mid = passed_along(middle, ROW, -1)
+        first_kernel, [tile, side, side, block, (probe_shape, HBM)], fit_scratch + [probe_shape],
+        [positions], [object_field, halo, (probe_modes, HBM), (amp, HBM), step, *tables], copies=5, in_place=1)
     from_right = passed_along(edge, COL, -1)
     from_left = passed_along(spill, COL, 1)
+    below_mid = passed_along(middle, ROW, -1)
     (upward,) = call(upward_kernel, [block], [], [above, info], [edge, from_left, from_right, spill])
     below_rest = passed_along(upward, ROW, -1)
     whole, source = call(
-        merge_kernel, [(tile, AUTO), (2, WIN, WIDE)], [], [info], [(obj, AUTO), from_left, from_right, spill])
-    grad, spill, downward, keep, send = call(
-        second_kernel, [(window, HBM), (2, WIN, HALO), (2, HALO, WIN), window, window],
-        fit_scratch + [window, probe_shape], [positions, info],
-        [source, below_mid, below_rest, (probe_modes, HBM), (amp, HBM), step, (probe_sum, HBM), *tables], copies=7)
+        merge_kernel, [(tile, HBM), (2, WIN, WIDE)], [tile], [info], [obj, from_left, from_right, spill], copies=2)
+    grad, downward, keep, send = call(
+        second_kernel, [(2, WIN, WIDE), (2, HALO, WIN), window, window],
+        fit_scratch + [probe_shape], [positions, info],
+        [source, below_mid, below_rest, (probe_modes, HBM), (amp, HBM), step, (probe_sum, HBM), *tables], copies=5, in_place=2)
     own, other = summed_everywhere(keep, send, divisor)
     from_above = passed_along(downward, ROW, 1)
-    (spill,) = call(spill_kernel, [side], [], [above], [spill, from_above])
+    (spill,) = call(spill_kernel, [side], [], [above], [grad, from_above])
     from_left = passed_along(spill, COL, 1)
     (object_out,) = call(
         object_kernel, [(tile, AUTO)], [], [above], [(whole, AUTO), (grad, AUTO), from_above, from_left])

time: 170 us -> 169 us (level)
  the two profiles are of different devices: /device:TPU:10 before, /device:TPU:26 now
where the time goes in v4:
time: 169 us; the launch traced here: 168 us
  waiting for transfers between devices  50.2 us (30%)
  starting transfers between devices  47.3 us (28%)
  blocking collectives  46 us (27%)
  Pallas kernels  21.2 us (13%)
  local copies, waits for them, and re-layouts  2.71 us (2%)
    all_to_all x3, blocking collectives, exchanged(): return lax.all_to_all(parts, axes, 0, 0, tiled=False)  46 us
    ppermute x8, waiting for transfers between devices, passed_along(): return lax.ppermute(block, axis, route)  45.5 us
    ppermute x8, starting transfers between devices, passed_along(): return lax.ppermute(block, axis, route)  36.4 us
    pallas_call x8, Pallas kernels, call(): pl.pallas_call(kernel, out_shape=shapes, in_specs=[smem] * len(scalars) +...  21.2 us
    all_to_all x1, starting transfers between devices, exchanged(): return lax.all_to_all(parts, axes, 0, 0, tiled=False)  6.72 us
    ppermute x2, starting transfers between devices, swapped(): return lax.ppermute(block, CORE, [(0, 1), (1, 0)])  4.21 us
  transfers between devices with their start and end apart: 11, of which 7 were waited for; matrix products, arithmetic and copies ran while one was open for 0% of the time, Pallas kernels for 4%

profile of v4, /device:TPU:26, one launch (start us, length us, event | category | flops | bytes accessed | tf_op | source)
XLA Modules:
  0.0 168.4 jit_solution(4263334940864144448)
XLA Ops:
  0.6 1.1 copy.17.obj
  1.8 1.9 %collective-permute-start.1 = (f32[2,384,128]{2,1,0:T(8,128)S(1)}, f32[2,384,128]{2,1,0:T(8,128)S(1)}, u32[]{:S(2)}, u32[]{:S(2)}) collective-permute-start(f32[2,384,128]{2,1,0:T(8,128)S(1)} %slice.3), channel_id=1, source_target_pairs={{1,0},{2,1},{3,2},{4,3},{5,4},{6,5},{7,6},{8,7},{9,8},{10,9},{11,1... | collective-permute-start | bytes 1179656 | tf_op jit(solution)/shard_map/ppermute | solution.py:344
  3.7 0.0 copy-start.2
  3.7 0.0 copy-start.3
  3.7 0.0 copy-start.4
  3.8 0.0 copy-start.5
  3.8 0.0 copy-start.6
  3.8 0.0 copy-start.7
  3.8 2.2 %shard_map.113 = (f32[2,256,256]{2,1,0:T(8,128)}, f32[8,128]{1,0:T(8,128)S(1)}) custom-call(f32[2,2,256,256]{3,2,1,0:T(8,128)} %probe.1, bf16[2,256,256]{2,1,0:T(8,128)(2,1)} %bitcast.12), custom_call_target="tpu_custom_call" | custom-call | tf_op jit(solution)/shard_map/pallas_call | solution.py:328
  6.0 3.0 %collective-permute-done.1.halo = f32[2,384,128]{2,1,0:T(8,128)S(1)} collective-permute-done((f32[2,384,128]{2,1,0:T(8,128)S(1)}, f32[2,384,128]{2,1,0:T(8,128)S(1)}, u32[]{:S(2)}, u32[]{:S(2)}) %collective-permute-start.1) | collective-permute-done | bytes 393248 | tf_op jit(solution)/shard_map/ppermute | solution.py:344
  9.0 0.0 copy-start.8
  9.0 0.0 copy-done.2
  9.0 0.0 copy-done.3
  9.0 0.0 copy-done.4
  9.0 0.0 copy-done.5
  9.0 0.0 copy-done.6
  9.0 0.0 copy-done.7
  9.0 0.6 copy-done.8
  9.7 7.1 %shard_map.114 = (f32[2,384,256]{2,1,0:T(8,128)S(1)}, f32[2,384,128]{2,1,0:T(8,128)S(1)}, f32[2,384,128]{2,1,0:T(8,128)S(1)}, f32[2,128,128]{2,1,0:T(8,128)}, f32[2,2,256,256]{3,2,1,0:T(8,128)}) custom-call(s32[2,2]{1,0:T(2,128)S(1)} %bitcast.8, f32[2,384,256]{2,1,0:T(8,128)S(1)} %copy.17.obj, ...), custom_call_target="tpu_custom_call", output_to_operand_aliasing={{0}: (1, {})} | custom-call | tf_op jit(solution)/shard_map/pallas_call | solution.py:328
  16.7 3.8 %collective-permute-start.3 = (f32[2,384,128]{2,1,0:T(8,128)S(1)}, f32[2,384,128]{2,1,0:T(8,128)S(1)}, u32[]{:S(2)}, u32[]{:S(2)}) collective-permute-start(f32[2,384,128]{2,1,0:T(8,128)S(1)} %get-tuple-element.19.edge), channel_id=1, source_target_pairs={{1,0},{2,1},{3,2},{4,3},{5,4},{6,5},{7,6},{8,7},{9,8},{10,9},{11,1... | collective-permute-start | bytes 1179656 | tf_op jit(solution)/shard_map/ppermute | solution.py:344
  20.6 1.9 %collective-permute-start.2 = (f32[2,384,128]{2,1,0:T(8,128)S(1)}, f32[2,384,128]{2,1,0:T(8,128)S(1)}, u32[]{:S(2)}, u32[]{:S(2)}) collective-permute-start(f32[2,384,128]{2,1,0:T(8,128)S(1)} %get-tuple-element.18.spill), channel_id=1, source_target_pairs={{0,1},{1,2},{2,3},{3,4},{4,5},{5,6},{6,7},{7,8},{8,9},{9,10},{10,1... | collective-permute-start | bytes 1179656 | tf_op jit(solution)/shard_map/ppermute | solution.py:344
  22.5 9.1 %collective-permute-start = (s32[2,2]{1,0:T(2,128)S(1)}, s32[2,2]{1,0:T(2,128)S(1)}, u32[]{:S(2)}, u32[]{:S(2)}) collective-permute-start(s32[2,2]{1,0:T(2,128)S(1)} %bitcast.9), channel_id=1, source_target_pairs={{0,32},{32,64},{64,96},{96,128},{128,160},{160,192},{192,224},{224... | collective-permute-start | bytes 56 | tf_op jit(solution)/shard_map/ppermute | solution.py:344
  31.6 0.1 pad_add_fusion.info
  31.7 5.7 %collective-permute-start.4 = (f32[2,128,128]{2,1,0:T(8,128)}, f32[2,128,128]{2,1,0:T(8,128)S(1)}, u32[]{:S(2)}, u32[]{:S(2)}) collective-permute-start(f32[2,128,128]{2,1,0:T(8,128)} %get-tuple-element.22), channel_id=1, source_target_pairs={{32,0},{64,32},{96,64},{128,96},{160,128},{192,160},{224,192},{256... | collective-permute-start | bytes 393224 | tf_op jit(solution)/shard_map/ppermute | solution.py:344
  37.4 0.0 collective-permute-done.above
  37.4 0.0 collective-permute-done.3.from_right
  37.4 0.0 collective-permute-done.2.from_left
  37.4 0.6 shard_map.116
  38.0 7.8 %collective-permute-start.5 = (f32[2,128,128]{2,1,0:T(8,128)S(1)}, f32[2,128,128]{2,1,0:T(8,128)S(1)}, u32[]{:S(2)}, u32[]{:S(2)}) collective-permute-start(f32[2,128,128]{2,1,0:T(8,128)S(1)} %shard_map.116), channel_id=1, source_target_pairs={{32,0},{64,32},{96,64},{128,96},{160,128},{192,160},{224,192},{256... | collective-permute-start | bytes 393224 | tf_op jit(solution)/shard_map/ppermute | solution.py:344
  45.9 1.5 shard_map.115
  47.4 11.3 %collective-permute-done.4.below_mid = f32[2,128,128]{2,1,0:T(8,128)S(1)} collective-permute-done((f32[2,128,128]{2,1,0:T(8,128)}, f32[2,128,128]{2,1,0:T(8,128)S(1)}, u32[]{:S(2)}, u32[]{:S(2)}) %collective-permute-start.4) | collective-permute-done | bytes 131104 | tf_op jit(solution)/shard_map/ppermute | solution.py:344
  58.7 5.8 %collective-permute-done.5.below_rest = f32[2,128,128]{2,1,0:T(8,128)S(1)} collective-permute-done((f32[2,128,128]{2,1,0:T(8,128)S(1)}, f32[2,128,128]{2,1,0:T(8,128)S(1)}, u32[]{:S(2)}, u32[]{:S(2)}) %collective-permute-start.5) | collective-permute-done | bytes 131104 | tf_op jit(solution)/shard_map/ppermute | solution.py:344
  64.5 6.1 %shard_map.117 = (f32[2,256,384]{2,1,0:T(8,128)S(1)}, f32[2,128,256]{2,1,0:T(8,128)S(1)}, f32[2,256,256]{2,1,0:T(8,128)S(1)}, f32[2,256,256]{2,1,0:T(8,128)S(1)}) custom-call(s32[2,2]{1,0:T(2,128)S(1)} %bitcast.10, s32[2]{0:T(128)S(1)} %pad_add_fusion.info, f32[2,256,384]{2,1,0:T(8,128)S(1)} %get-tuple-element.21.source, ...), custom_call_target="tpu_custom_call", output_to_operand_aliasing={{0}: (2, {})} | custom-call | tf_op jit(solution)/shard_map/pallas_call | solution.py:328
  70.6 2.3 %collective-permute-start.8 = (f32[2,256,256]{2,1,0:T(8,128)S(1)}, f32[2,256,256]{2,1,0:T(8,128)S(1)}, u32[]{:S(2)}, u32[]{:S(2)}) collective-permute-start(f32[2,256,256]{2,1,0:T(8,128)S(1)} %get-tuple-element.27), channel_id=1, source_target_pairs={{0,1},{1,0},{2,3},{3,2},{4,5},{5,4},{6,7},{7,6},{8,9},{9,8},{10,11... | collective-permute-start | bytes 1572872 | tf_op jit(solution)/shard_map/ppermute | solution.py:352
  72.9 1.5 collective-permute-done.8
  74.4 0.1 add.11
  74.5 16.1 %all_to_all.20 = f32[16,32,256]{2,1,0:T(8,128)S(1)} all-to-all(f32[16,32,256]{2,1,0:T(8,128)S(1)} %bitcast.11), channel_id=1, replica_groups=mesh['row_0'=4,'row_1'=4,'col_0'=4,'col_1'=4,'col_2'=2] {'row_0','col_1'}, dimensions={0} | all-to-all | bytes 1048576 | tf_op jit(solution)/shard_map/all_to_all | solution.py:348
  90.6 8.3 %all_to_all.21 = f32[4,32,256]{2,1,0:T(8,128)S(1)} all-to-all(f32[4,32,256]{2,1,0:T(8,128)S(1)} %broadcast_in_dim.9), channel_id=1, replica_groups=mesh['row_0'=4,'row_1'=4,'col_0'=4,'col_1'=4,'col_2'=2] {'col_0'}, dimensions={0} | all-to-all | bytes 262144 | tf_op jit(solution)/shard_map/all_to_all | solution.py:348
  99.0 21.6 %all_to_all.22 = f32[4,32,256]{2,1,0:T(8,128)S(1)} all-to-all(f32[4,32,256]{2,1,0:T(8,128)S(1)} %broadcast_in_dim.10), channel_id=1, replica_groups=mesh['row_0'=4,'row_1'=4,'col_0'=4,'col_1'=4,'col_2'=2] {'row_1'}, dimensions={0} | all-to-all | bytes 262144 | tf_op jit(solution)/shard_map/all_to_all | solution.py:348
  120.6 0.8 broadcast_in_dim.11
  121.4 6.7 %all-to-all-start.3 = ((f32[16,32,256]{2,1,0:T(8,128)}), f32[16,32,256]{2,1,0:T(8,128)S(1)}, u32[]{:S(2)}, u32[]{:S(2)}) async-start(f32[16,32,256]{2,1,0:T(8,128)} %broadcast_in_dim.11), calls=%async_computation.3 | async-start | bytes 1048576 | tf_op jit(solution)/shard_map/all_to_all | solution.py:348
  128.2 0.0 copy-start.1
  128.2 4.1 %collective-permute-start.6 = (f32[2,128,256]{2,1,0:T(8,128)S(1)}, f32[2,128,256]{2,1,0:T(8,128)S(1)}, u32[]{:S(2)}, u32[]{:S(2)}) collective-permute-start(f32[2,128,256]{2,1,0:T(8,128)S(1)} %get-tuple-element.25), channel_id=1, source_target_pairs={{0,32},{32,64},{64,96},{96,128},{128,160},{160,192},{192,224},{224... | collective-permute-start | bytes 786440 | tf_op jit(solution)/shard_map/ppermute | solution.py:344
  132.3 3.1 %all-to-all-done.3 = f32[16,32,256]{2,1,0:T(8,128)S(1)} async-done(((f32[16,32,256]{2,1,0:T(8,128)}), f32[16,32,256]{2,1,0:T(8,128)S(1)}, u32[]{:S(2)}, u32[]{:S(2)}) %all-to-all-start.3) | async-done | bytes 524320 | tf_op jit(solution)/shard_map/all_to_all | solution.py:348
  135.5 1.9 %collective-permute-start.9 = (f32[2,256,256]{2,1,0:T(8,128)S(1)}, f32[2,256,256]{2,1,0:T(8,128)S(1)}, u32[]{:S(2)}, u32[]{:S(2)}) collective-permute-start(f32[2,256,256]{2,1,0:T(8,128)S(1)} %bitcast.6), channel_id=1, source_target_pairs={{0,1},{1,0},{2,3},{3,2},{4,5},{5,4},{6,7},{7,6},{8,9},{9,8},{10,11... | collective-permute-start | bytes 1572872 | tf_op jit(solution)/shard_map/ppermute | solution.py:352
  137.4 18.2 %collective-permute-done.6.from_above = f32[2,128,256]{2,1,0:T(8,128)S(1)} collective-permute-done((f32[2,128,256]{2,1,0:T(8,128)S(1)}, f32[2,128,256]{2,1,0:T(8,128)S(1)}, u32[]{:S(2)}, u32[]{:S(2)}) %collective-permute-start.6) | collective-permute-done | bytes 262176 | tf_op jit(solution)/shard_map/ppermute | solution.py:344
  155.6 0.6 shard_map.118
  156.2 1.9 %collective-permute-start.7 = (f32[2,384,128]{2,1,0:T(8,128)S(1)}, f32[2,384,128]{2,1,0:T(8,128)S(1)}, u32[]{:S(2)}, u32[]{:S(2)}) collective-permute-start(f32[2,384,128]{2,1,0:T(8,128)S(1)} %shard_map.118), channel_id=1, source_target_pairs={{0,1},{1,2},{2,3},{3,4},{4,5},{5,6},{6,7},{7,8},{8,9},{9,10},{10,1... | collective-permute-start | bytes 1179656 | tf_op jit(solution)/shard_map/ppermute | solution.py:344
  158.1 7.2 %collective-permute-done.7.from_left = f32[2,384,128]{2,1,0:T(8,128)S(1)} collective-permute-done((f32[2,384,128]{2,1,0:T(8,128)S(1)}, f32[2,384,128]{2,1,0:T(8,128)S(1)}, u32[]{:S(2)}, u32[]{:S(2)}) %collective-permute-start.7) | collective-permute-done | bytes 393248 | tf_op jit(solution)/shard_map/ppermute | solution.py:344
  165.3 0.0 copy-done.1
  165.3 0.0 copy-start
  165.3 1.5 shard_map.119
  166.8 0.0 collective-permute-done.9.other
  166.8 0.0 copy-done
  166.8 1.6 shard_map.120
  (7 shorter events, 0.1 us)
Async XLA Ops:
  1.8 7.2 %collective-permute-start.1 = (f32[2,384,128]{2,1,0:T(8,128)S(1)}, f32[2,384,128]{2,1,0:T(8,128)S(1)}, u32[]{:S(2)}, u32[]{:S(2)}) collective-permute-start(f32[2,384,128]{2,1,0:T(8,128)S(1)} %slice.3), channel_id=1, source_target_pairs={{1,0},{2,1},{3,2},{4,3},{5,4},{6,5},{7,6},{8,7},{9,8},{10,9},{11,1... | collective-permute-start | bytes 1179656 | tf_op jit(solution)/shard_map/ppermute | solution.py:344
  3.7 5.3 %copy-start.2 = (f32[2,128,128]{2,1,0:T(8,128)S(1)}, f32[2,128,128]{2,1,0:T(8,128)}, u32[]{:S(2)}) copy-start(f32[2,128,128]{2,1,0:T(8,128)} %constant.38.clone.rows) | copy-start | bytes 393220
  3.7 5.3 %copy-start.3 = (bf16[256,256]{1,0:T(8,128)(2,1)S(1)}, bf16[256,256]{1,0:T(8,128)(2,1)}, u32[]{:S(2)}) copy-start(bf16[256,256]{1,0:T(8,128)(2,1)} %constant.37.clone.low_t) | copy-start | bytes 393220
  3.7 5.3 %copy-start.4 = (bf16[256,256]{1,0:T(8,128)(2,1)S(1)}, bf16[256,256]{1,0:T(8,128)(2,1)}, u32[]{:S(2)}) copy-start(bf16[256,256]{1,0:T(8,128)(2,1)} %constant.36.clone.high_t) | copy-start | bytes 393220
  3.8 5.3 %copy-start.5 = (bf16[256,256]{1,0:T(8,128)(2,1)S(1)}, bf16[256,256]{1,0:T(8,128)(2,1)}, u32[]{:S(2)}) copy-start(bf16[256,256]{1,0:T(8,128)(2,1)} %constant.35.clone.low) | copy-start | bytes 393220
  3.8 5.2 %copy-start.6 = (bf16[256,256]{1,0:T(8,128)(2,1)S(1)}, bf16[256,256]{1,0:T(8,128)(2,1)}, u32[]{:S(2)}) copy-start(bf16[256,256]{1,0:T(8,128)(2,1)} %constant.34.clone.high) | copy-start | bytes 393220
  3.8 5.2 %copy-start.7 = (f32[2,8,128]{2,1,0:T(8,128)S(1)}, f32[2,8,128]{2,1,0:T(8,128)}, u32[]{:S(2)}) copy-start(f32[2,8,128]{2,1,0:T(8,128)} %constant.39.clone.cols) | copy-start | bytes 24580
  9.0 0.7 copy-start.8
  16.7 20.7 %collective-permute-start.3 = (f32[2,384,128]{2,1,0:T(8,128)S(1)}, f32[2,384,128]{2,1,0:T(8,128)S(1)}, u32[]{:S(2)}, u32[]{:S(2)}) collective-permute-start(f32[2,384,128]{2,1,0:T(8,128)S(1)} %get-tuple-element.19.edge), channel_id=1, source_target_pairs={{1,0},{2,1},{3,2},{4,3},{5,4},{6,5},{7,6},{8,7},{9,8},{10,9},{11,1... | collective-permute-start | bytes 1179656 | tf_op jit(solution)/shard_map/ppermute | solution.py:344
  20.6 16.9 %collective-permute-start.2 = (f32[2,384,128]{2,1,0:T(8,128)S(1)}, f32[2,384,128]{2,1,0:T(8,128)S(1)}, u32[]{:S(2)}, u32[]{:S(2)}) collective-permute-start(f32[2,384,128]{2,1,0:T(8,128)S(1)} %get-tuple-element.18.spill), channel_id=1, source_target_pairs={{0,1},{1,2},{2,3},{3,4},{4,5},{5,6},{6,7},{7,8},{8,9},{9,10},{10,1... | collective-permute-start | bytes 1179656 | tf_op jit(solution)/shard_map/ppermute | solution.py:344
  22.5 14.9 %collective-permute-start = (s32[2,2]{1,0:T(2,128)S(1)}, s32[2,2]{1,0:T(2,128)S(1)}, u32[]{:S(2)}, u32[]{:S(2)}) collective-permute-start(s32[2,2]{1,0:T(2,128)S(1)} %bitcast.9), channel_id=1, source_target_pairs={{0,32},{32,64},{64,96},{96,128},{128,160},{160,192},{192,224},{224... | collective-permute-start | bytes 56 | tf_op jit(solution)/shard_map/ppermute | solution.py:344
  31.7 27.0 %collective-permute-start.4 = (f32[2,128,128]{2,1,0:T(8,128)}, f32[2,128,128]{2,1,0:T(8,128)S(1)}, u32[]{:S(2)}, u32[]{:S(2)}) collective-permute-start(f32[2,128,128]{2,1,0:T(8,128)} %get-tuple-element.22), channel_id=1, source_target_pairs={{32,0},{64,32},{96,64},{128,96},{160,128},{192,160},{224,192},{256... | collective-permute-start | bytes 393224 | tf_op jit(solution)/shard_map/ppermute | solution.py:344
  38.0 26.5 %collective-permute-start.5 = (f32[2,128,128]{2,1,0:T(8,128)S(1)}, f32[2,128,128]{2,1,0:T(8,128)S(1)}, u32[]{:S(2)}, u32[]{:S(2)}) collective-permute-start(f32[2,128,128]{2,1,0:T(8,128)S(1)} %shard_map.116), channel_id=1, source_target_pairs={{32,0},{64,32},{96,64},{128,96},{160,128},{192,160},{224,192},{256... | collective-permute-start | bytes 393224 | tf_op jit(solution)/shard_map/ppermute | solution.py:344
  70.6 3.8 %collective-permute-start.8 = (f32[2,256,256]{2,1,0:T(8,128)S(1)}, f32[2,256,256]{2,1,0:T(8,128)S(1)}, u32[]{:S(2)}, u32[]{:S(2)}) collective-permute-start(f32[2,256,256]{2,1,0:T(8,128)S(1)} %get-tuple-element.27), channel_id=1, source_target_pairs={{0,1},{1,0},{2,3},{3,2},{4,5},{5,4},{6,7},{7,6},{8,9},{9,8},{10,11... | collective-permute-start | bytes 1572872 | tf_op jit(solution)/shard_map/ppermute | solution.py:352
  121.4 14.0 %all-to-all-start.3 = ((f32[16,32,256]{2,1,0:T(8,128)}), f32[16,32,256]{2,1,0:T(8,128)S(1)}, u32[]{:S(2)}, u32[]{:S(2)}) async-start(f32[16,32,256]{2,1,0:T(8,128)} %broadcast_in_dim.11), calls=%async_computation.3 | async-start | bytes 1048576 | tf_op jit(solution)/shard_map/all_to_all | solution.py:348
  128.2 37.1 %copy-start.1 = (f32[2,384,256]{2,1,0:T(8,128)S(1)}, f32[2,384,256]{2,1,0:T(8,128)}, u32[]{:S(2)}) copy-start(f32[2,384,256]{2,1,0:T(8,128)} %get-tuple-element.20.whole) | copy-start | bytes 2359300
  128.2 27.4 %collective-permute-start.6 = (f32[2,128,256]{2,1,0:T(8,128)S(1)}, f32[2,128,256]{2,1,0:T(8,128)S(1)}, u32[]{:S(2)}, u32[]{:S(2)}) collective-permute-start(f32[2,128,256]{2,1,0:T(8,128)S(1)} %get-tuple-element.25), channel_id=1, source_target_pairs={{0,32},{32,64},{64,96},{96,128},{128,160},{160,192},{192,224},{224... | collective-permute-start | bytes 786440 | tf_op jit(solution)/shard_map/ppermute | solution.py:344
  135.5 31.4 %collective-permute-start.9 = (f32[2,256,256]{2,1,0:T(8,128)S(1)}, f32[2,256,256]{2,1,0:T(8,128)S(1)}, u32[]{:S(2)}, u32[]{:S(2)}) collective-permute-start(f32[2,256,256]{2,1,0:T(8,128)S(1)} %bitcast.6), channel_id=1, source_target_pairs={{0,1},{1,0},{2,3},{3,2},{4,5},{5,4},{6,7},{7,6},{8,9},{9,8},{10,11... | collective-permute-start | bytes 1572872 | tf_op jit(solution)/shard_map/ppermute | solution.py:352
  156.2 9.1 %collective-permute-start.7 = (f32[2,384,128]{2,1,0:T(8,128)S(1)}, f32[2,384,128]{2,1,0:T(8,128)S(1)}, u32[]{:S(2)}, u32[]{:S(2)}) collective-permute-start(f32[2,384,128]{2,1,0:T(8,128)S(1)} %shard_map.118), channel_id=1, source_target_pairs={{0,1},{1,2},{2,3},{3,4},{4,5},{5,6},{6,7},{7,8},{8,9},{9,10},{10,1... | collective-permute-start | bytes 1179656 | tf_op jit(solution)/shard_map/ppermute | solution.py:344
  165.3 1.6 copy-start

commit v5 on v4

--- a/solution.py
+++ b/solution.py
@@ -101,10 +101,8 @@
     return jnp.concatenate([high[...], high[...], low[...]], axis=0)
 
 
-def window_fit(window, probe, amplitude, tables, far, window_ref, gradient, add_probe, probe_copy, amp_copy):
+def window_fit(probe, amplitude, tables, far, window_ref, gradient, add_probe, probe_copy, amp_copy):
     high, low, high_t, low_t, rows, cols = tables
-    window_ref[0] = window[0]
-    window_ref[1] = window[1]
 
     def twiddles():
         twr = tuple(jnp.concatenate([rows[k], rows[k]], axis=1) for k in range(2))
@@ -112,7 +110,8 @@
         return twr, twc
 
     def outward(m, carry):
-        probe_copy(m).wait()
+        if probe_copy is not None:
+            probe_copy(m).wait()
         twr, twc = twiddles()
         w_r, w_i = window_ref[0], window_ref[1]
         p_r, p_i = probe[m, 0], probe[m, 1]
@@ -126,7 +125,7 @@
     intensity = far[0, 0] * far[0, 0] + far[0, 1] * far[0, 1]
     intensity = intensity + (far[1, 0] * far[1, 0] + far[1, 1] * far[1, 1])
     amp_copy.wait()
-    factor = amplitude[...] / jnp.sqrt(jnp.maximum(intensity, 0.1)) - 1.0
+    factor = amplitude[...] * lax.rsqrt(jnp.maximum(intensity, 0.1)) - 1.0
     for m in range(2):
         far[m, 0] = far[m, 0] * factor
         far[m, 1] = far[m, 1] * factor
@@ -178,35 +177,54 @@
 WIDE = WIN + HALO
 
 
-def first_kernel(pos, obj, halo, probe_hbm, amp_hbm, step, high, low, high_t, low_t, rows, cols,
-                 new_obj, spill, edge, middle, sum_hbm,
-                 far, win, grad, probe, amp, probe_sum, sems):
+def cut_window(tiles, tall, win, row, col):
+    base, rest = pl.multiple_of(row // 8 * 8, 8), lax.rem(row, 8)
+    near = lax.broadcasted_iota(jnp.int32, (TILE_R, HALF), 1) < HALF - col
+    upper = lax.broadcasted_iota(jnp.int32, (WIN // 8, 8, WIN), 1) < 8 - rest
+    for k in range(2):
+        first, second, third = (pltpu.roll(t, HALF - col, 1) for t in tiles(k))
+        tall[k, :TILE_R, :HALF] = jnp.where(near, first, second)
+        tall[k, :TILE_R, HALF:] = jnp.where(near, second, third)
+        x = tall[k, pl.ds(base, WIN + 8), :].reshape(WIN // 8 + 1, 8, WIN)
+        x = pltpu.roll(x, lax.rem(8 - rest, 8), 1)
+        win[k] = jnp.where(upper, x[:-1], x[1:]).reshape(WIN, WIN)
+        tall[k] = jnp.zeros((TILE_R + 8, WIN), jnp.float32)
+
+
+def placed(grad, scale, tall, row, col, k):
+    base, rest = pl.multiple_of(row // 8 * 8, 8), lax.rem(row, 8)
+    lower = lax.broadcasted_iota(jnp.int32, (WIN // 8 + 1, 8, WIN), 1) >= rest
+    x = pltpu.roll((grad[k] * scale).reshape(WIN // 8, 8, WIN), rest, 1)
+    gap = jnp.zeros((1, 8, WIN), jnp.float32)
+    x = jnp.where(lower, jnp.concatenate([x, gap], axis=0), jnp.concatenate([gap, x], axis=0))
+    tall[k, pl.ds(base, WIN + 8), :] = x.reshape(WIN + 8, WIN)
+    inside = lax.broadcasted_iota(jnp.int32, (TILE_R, HALF), 1) >= col
+    first = pltpu.roll(tall[k, :TILE_R, :HALF], lax.rem(col, HALF), 1)
+    second = pltpu.roll(tall[k, :TILE_R, HALF:], lax.rem(col, HALF), 1)
+    return jnp.concatenate(
+        [jnp.where(inside, first, 0.0), jnp.where(inside, second, first), jnp.where(inside, 0.0, second)], axis=1)
+
+
+def first_kernel(pos, obj, halo, probe, amp_hbm, step, high, low, high_t, low_t, rows, cols,
+                 new_obj, edge, spill, middle, sum_hbm,
+                 far, win, grad, tall, amp, probe_sum, sems):
     row, col = pos[0, 0], pos[0, 1]
-    probe_copy = lambda m: pltpu.make_async_copy(probe_hbm.at[m], probe.at[m], sems.at[m])
     sum_copy = lambda m: pltpu.make_async_copy(probe_sum.at[m], sum_hbm.at[m], sems.at[2 + m])
     amp_copy = pltpu.make_async_copy(amp_hbm.at[0], amp, sems.at[4])
-    probe_copy(0).start()
-    probe_copy(1).start()
     amp_copy.start()
 
-    def cut(k):
-        wide = jnp.concatenate([obj[k], halo[k]], axis=1)
-        wide = pltpu.roll(wide, WIDE - col, 1)[:, :WIN]
-        return pltpu.roll(wide, lax.rem(TILE_R - row, TILE_R), 0)[:WIN]
+    cut_window(lambda k: (obj[k, :, :HALO], obj[k, :, HALO:], halo[k]), tall, win, row, col)
 
     def add_probe(m, real, imag):
         probe_sum[m, 0] = real
         probe_sum[m, 1] = imag
         sum_copy(m).start()
 
-    window_fit((cut(0), cut(1)), probe, amp, (high, low, high_t, low_t, rows, cols), far, win, grad, add_probe,
-               probe_copy, amp_copy)
+    window_fit(probe, amp, (high, low, high_t, low_t, rows, cols), far, win, grad, add_probe,
+               None, amp_copy)
     scale = step[:1, :1]
     for k in range(2):
-        g = jnp.concatenate([grad[k] * scale, jnp.zeros((TILE_R - WIN, WIN), jnp.float32)], axis=0)
-        g = pltpu.roll(g, row, 0)
-        g = jnp.concatenate([g, jnp.zeros((TILE_R, HALO), jnp.float32)], axis=1)
-        g = pltpu.roll(g, col, 1)
+        g = placed(grad, scale, tall, row, col, k)
         updated = obj[k] + g[:, :WIN]
         new_obj[k] = updated
         edge[k] = updated[:, :HALO]
@@ -244,7 +262,7 @@
 
 def second_kernel(pos, info, source, below_mid, below_rest, probe_hbm, amp_hbm, step, before_hbm,
                   high, low, high_t, low_t, rows, cols,
-                  own_grad, downward, keep_sum, send_sum, far, win, grad, probe, amp, before, sems):
+                  own_grad, downward, keep_sum, send_sum, far, win, grad, tall, amp, probe, before, sems):
     row, col, core = pos[1, 0] - LAST, pos[1, 1], info[1]
     probe_copy = lambda m: pltpu.make_async_copy(probe_hbm.at[m], probe.at[m], sems.at[m])
     before_copy = lambda m: pltpu.make_async_copy(before_hbm.at[m], before.at[m], sems.at[2 + m])
@@ -255,10 +273,11 @@
     before_copy(0).start()
     before_copy(1).start()
 
-    def cut(k):
-        lower = jnp.concatenate([below_rest[k], below_mid[k], below_rest[k]], axis=1)
-        tall = pltpu.roll(jnp.concatenate([source[k], lower], axis=0), WIDE - col, 1)[:, :WIN]
-        return pltpu.roll(tall, lax.rem(TILE_R - row, TILE_R), 0)[:WIN]
+    def tiles(k):
+        lower = (below_rest[k], below_mid[k], below_rest[k])
+        return [jnp.concatenate([source[k, :, HALO * t:HALO * t + HALO], lower[t]], axis=0) for t in range(3)]
+
+    cut_window(tiles, tall, win, row, col)
 
     def add_probe(m, real, imag):
         before_copy(m).wait()
@@ -273,14 +292,11 @@
             send_sum[0] = before[m, 0] + real
             send_sum[1] = before[m, 1] + imag
 
-    window_fit((cut(0), cut(1)), probe, amp, (high, low, high_t, low_t, rows, cols), far, win, grad, add_probe,
+    window_fit(probe, amp, (high, low, high_t, low_t, rows, cols), far, win, grad, add_probe,
                probe_copy, amp_copy)
     scale = step[:1, :1]
     for k in range(2):
-        g = jnp.concatenate([grad[k] * scale, jnp.zeros((TILE_R - WIN, WIN), jnp.float32)], axis=0)
-        g = pltpu.roll(g, row, 0)
-        g = jnp.concatenate([g, jnp.zeros((TILE_R, HALO), jnp.float32)], axis=1)
-        g = pltpu.roll(g, col, 1)
+        g = placed(grad, scale, tall, row, col, k)
         own_grad[k] = g[:WIN]
         downward[k, :, :HALO] = g[WIN:, :HALO] + g[WIN:, WIN:]
         downward[k, :, HALO:] = g[WIN:, HALO:WIN]
@@ -333,7 +349,7 @@
         scratch_shapes=[pltpu.VMEM(s, jnp.float32) if isinstance(s, tuple) else s for s in scratch]
         + ([pltpu.SemaphoreType.DMA((copies,))] if copies else []),
         compiler_params=pltpu.CompilerParams(vmem_limit_bytes=24 * 1024 * 1024),
-        input_output_aliases={} if in_place is None else {in_place: 0},
+        input_output_aliases=in_place or {},
         interpret=INTERPRET,
     )(*scalars, *operands)
 
@@ -373,7 +389,7 @@
     has_right = (lax.axis_index(COL) < lax.axis_size(COL) - 1).astype(jnp.int32)
     tile, side, probe_shape = (2, TILE_R, WIN), (2, TILE_R, HALO), (2, 2, WIN, WIN)
     block, window = (2, HALO, HALO), (2, WIN, WIN)
-    fit_scratch = [probe_shape, window, window, probe_shape, (WIN, WIN)]
+    fit_scratch = [probe_shape, window, window, (2, TILE_R + 8, WIN), (WIN, WIN), probe_shape]
 
     halo = passed_along(object_field[:, :, :HALO], COL, -1)
     above = passed_along(positions, ROW, 1)
@@ -382,9 +398,9 @@
         before_kernel, [((BATCHES, WIN, WIN), HBM), (8, HALF)],
         [probe_shape, pltpu.VMEM((BATCHES, WIN, WIN), jnp.bfloat16), (BATCHES, WIN, WIN)],
         [], [(probe_modes, HBM), (amplitudes[0, 0], HBM)], copies=4)
-    obj, spill, edge, middle, probe_sum = call(
-        first_kernel, [tile, side, side, block, (probe_shape, HBM)], fit_scratch + [probe_shape],
-        [positions], [object_field, halo, (probe_modes, HBM), (amp, HBM), step, *tables], copies=5, in_place=1)
+    obj, edge, spill, middle, probe_sum = call(
+        first_kernel, [tile, side, side, block, (probe_shape, HBM)], fit_scratch, [positions],
+        [object_field, halo, probe_modes, (amp, HBM), step, *tables], copies=5, in_place={1: 0, 2: 1})
     from_right = passed_along(edge, COL, -1)
     from_left = passed_along(spill, COL, 1)
     below_mid = passed_along(middle, ROW, -1)
@@ -395,13 +411,13 @@
     grad, downward, keep, send = call(
         second_kernel, [(2, WIN, WIDE), (2, HALO, WIN), window, window],
         fit_scratch + [probe_shape], [positions, info],
-        [source, below_mid, below_rest, (probe_modes, HBM), (amp, HBM), step, (probe_sum, HBM), *tables], copies=5, in_place=2)
+        [source, below_mid, below_rest, (probe_modes, HBM), (amp, HBM), step, (probe_sum, HBM), *tables], copies=5, in_place={2: 0})
     own, other = summed_everywhere(keep, send, divisor)
     from_above = passed_along(downward, ROW, 1)
     (spill,) = call(spill_kernel, [side], [], [above], [grad, from_above])
     from_left = passed_along(spill, COL, 1)
     (object_out,) = call(
-        object_kernel, [(tile, AUTO)], [], [above], [(whole, AUTO), (grad, AUTO), from_above, from_left])
+        object_kernel, [(tile, AUTO)], [], [above], [(whole, AUTO), (grad, AUTO), (from_above, AUTO), (from_left, AUTO)])
     (probe_out,) = call(probe_kernel, [(probe_shape, AUTO)], [], [info], [(probe_modes, AUTO), own, other])
     return (object_out, probe_out)
 

time: 169 us -> 168 us (level)
  no operation moved by 1% of the time
where the time goes in v5:
time: 168 us; the launch traced here: 167 us
  waiting for transfers between devices  50.1 us (30%)
  starting transfers between devices  47.4 us (28%)
  blocking collectives  46 us (27%)
  Pallas kernels  19.8 us (12%)
  local copies, waits for them, and re-layouts  2.77 us (2%)
    all_to_all x3, blocking collectives, exchanged(): return lax.all_to_all(parts, axes, 0, 0, tiled=False)  46 us
    ppermute x8, waiting for transfers between devices, passed_along(): return lax.ppermute(block, axis, route)  45.4 us
    ppermute x8, starting transfers between devices, passed_along(): return lax.ppermute(block, axis, route)  36.5 us
    pallas_call x8, Pallas kernels, call(): pl.pallas_call(kernel, out_shape=shapes, in_specs=[smem] * len(scalars) +...  19.8 us
    all_to_all x1, starting transfers between devices, exchanged(): return lax.all_to_all(parts, axes, 0, 0, tiled=False)  6.72 us
    ppermute x2, starting transfers between devices, swapped(): return lax.ppermute(block, CORE, [(0, 1), (1, 0)])  4.19 us
  transfers between devices with their start and end apart: 11, of which 7 were waited for; matrix products, arithmetic and copies ran while one was open for 0% of the time, Pallas kernels for 4%

profile of v5, /device:TPU:26, one launch (start us, length us, event | category | flops | bytes accessed | tf_op | source)
XLA Modules:
  0.0 167.3 jit_solution(11818276912700826603)
XLA Ops:
  0.6 1.1 copy.19.obj
  1.8 2.1 %collective-permute-start.1 = (f32[2,384,128]{2,1,0:T(8,128)S(1)}, f32[2,384,128]{2,1,0:T(8,128)S(1)}, u32[]{:S(2)}, u32[]{:S(2)}) collective-permute-start(f32[2,384,128]{2,1,0:T(8,128)S(1)} %slice.3), channel_id=1, source_target_pairs={{1,0},{2,1},{3,2},{4,3},{5,4},{6,5},{7,6},{8,7},{9,8},{10,9},{11,1... | collective-permute-start | bytes 1179656 | tf_op jit(solution)/shard_map/ppermute | solution.py:360
  3.9 0.0 copy-start.3
  3.9 0.0 copy-start.4
  3.9 0.0 copy-start.6
  3.9 0.0 copy-start.8
  3.9 0.0 copy-start.10
  3.9 0.0 copy-start.12
  3.9 2.2 %shard_map.113 = (f32[2,256,256]{2,1,0:T(8,128)}, f32[8,128]{1,0:T(8,128)S(1)}) custom-call(f32[2,2,256,256]{3,2,1,0:T(8,128)} %probe.3, bf16[2,256,256]{2,1,0:T(8,128)(2,1)} %bitcast.9), custom_call_target="tpu_custom_call" | custom-call | tf_op jit(solution)/shard_map/pallas_call | solution.py:344
  6.2 3.0 %collective-permute-done.1.halo = f32[2,384,128]{2,1,0:T(8,128)S(1)} collective-permute-done((f32[2,384,128]{2,1,0:T(8,128)S(1)}, f32[2,384,128]{2,1,0:T(8,128)S(1)}, u32[]{:S(2)}, u32[]{:S(2)}) %collective-permute-start.1) | collective-permute-done | bytes 393248 | tf_op jit(solution)/shard_map/ppermute | solution.py:360
  9.1 0.0 copy-done
  9.1 0.0 copy-done.3
  9.1 0.0 copy-done.4
  9.1 0.0 copy-done.6
  9.1 0.0 copy-done.8
  9.2 0.0 copy-done.10
  9.2 0.0 copy-done.12
  9.2 5.6 %shard_map.114 = (f32[2,384,256]{2,1,0:T(8,128)S(1)}, f32[2,384,128]{2,1,0:T(8,128)S(1)}, f32[2,384,128]{2,1,0:T(8,128)S(1)}, f32[2,128,128]{2,1,0:T(8,128)S(1)}, f32[2,2,256,256]{3,2,1,0:T(8,128)}) custom-call(s32[2,2]{1,0:T(2,128)} %bitcast.pos, f32[2,384,256]{2,1,0:T(8,128)S(1)} %copy.19.obj, ...), custom_call_target="tpu_custom_call", output_to_operand_aliasing={{0}: (1, {}), {1}: (2, {})} | custom-call | tf_op jit(solution)/shard_map/pallas_call | solution.py:344
  14.8 0.0 copy-start.15
  14.8 0.7 copy-done.15
  15.5 3.8 %collective-permute-start.3 = (f32[2,384,128]{2,1,0:T(8,128)S(1)}, f32[2,384,128]{2,1,0:T(8,128)S(1)}, u32[]{:S(2)}, u32[]{:S(2)}) collective-permute-start(f32[2,384,128]{2,1,0:T(8,128)S(1)} %get-tuple-element.19.edge), channel_id=1, source_target_pairs={{1,0},{2,1},{3,2},{4,3},{5,4},{6,5},{7,6},{8,7},{9,8},{10,9},{11,1... | collective-permute-start | bytes 1179656 | tf_op jit(solution)/shard_map/ppermute | solution.py:360
  19.3 1.9 %collective-permute-start.2 = (f32[2,384,128]{2,1,0:T(8,128)S(1)}, f32[2,384,128]{2,1,0:T(8,128)S(1)}, u32[]{:S(2)}, u32[]{:S(2)}) collective-permute-start(f32[2,384,128]{2,1,0:T(8,128)S(1)} %get-tuple-element.18.spill), channel_id=1, source_target_pairs={{0,1},{1,2},{2,3},{3,4},{4,5},{5,6},{6,7},{7,8},{8,9},{9,10},{10,1... | collective-permute-start | bytes 1179656 | tf_op jit(solution)/shard_map/ppermute | solution.py:360
  21.2 9.1 %collective-permute-start = (s32[2,2]{1,0:T(2,128)}, s32[2,2]{1,0:T(2,128)S(1)}, u32[]{:S(2)}, u32[]{:S(2)}) collective-permute-start(s32[2,2]{1,0:T(2,128)} %bitcast.pos), channel_id=1, source_target_pairs={{0,32},{32,64},{64,96},{96,128},{128,160},{160,192},{192,224},{224... | collective-permute-start | bytes 56 | tf_op jit(solution)/shard_map/ppermute | solution.py:360
  30.3 0.1 pad_add_fusion.info
  30.4 5.7 %collective-permute-start.4 = (f32[2,128,128]{2,1,0:T(8,128)}, f32[2,128,128]{2,1,0:T(8,128)S(1)}, u32[]{:S(2)}, u32[]{:S(2)}) collective-permute-start(f32[2,128,128]{2,1,0:T(8,128)} %copy-done.15), channel_id=1, source_target_pairs={{32,0},{64,32},{96,64},{128,96},{160,128},{192,160},{224,192},{256... | collective-permute-start | bytes 393224 | tf_op jit(solution)/shard_map/ppermute | solution.py:360
  36.2 0.0 collective-permute-done.above
  36.2 0.0 collective-permute-done.3.from_right
  36.2 0.0 collective-permute-done.2.from_left
  36.2 0.6 shard_map.116
  36.8 7.8 %collective-permute-start.5 = (f32[2,128,128]{2,1,0:T(8,128)S(1)}, f32[2,128,128]{2,1,0:T(8,128)S(1)}, u32[]{:S(2)}, u32[]{:S(2)}) collective-permute-start(f32[2,128,128]{2,1,0:T(8,128)S(1)} %shard_map.116), channel_id=1, source_target_pairs={{32,0},{64,32},{96,64},{128,96},{160,128},{192,160},{224,192},{256... | collective-permute-start | bytes 393224 | tf_op jit(solution)/shard_map/ppermute | solution.py:360
  44.6 0.0 copy-start.5
  44.6 0.0 copy-start.7
  44.6 0.0 copy-start.9
  44.6 0.0 copy-start.11
  44.7 1.5 shard_map.115
  46.1 11.3 %collective-permute-done.4.below_mid = f32[2,128,128]{2,1,0:T(8,128)S(1)} collective-permute-done((f32[2,128,128]{2,1,0:T(8,128)}, f32[2,128,128]{2,1,0:T(8,128)S(1)}, u32[]{:S(2)}, u32[]{:S(2)}) %collective-permute-start.4) | collective-permute-done | bytes 131104 | tf_op jit(solution)/shard_map/ppermute | solution.py:360
  57.4 5.8 %collective-permute-done.5.below_rest = f32[2,128,128]{2,1,0:T(8,128)S(1)} collective-permute-done((f32[2,128,128]{2,1,0:T(8,128)S(1)}, f32[2,128,128]{2,1,0:T(8,128)S(1)}, u32[]{:S(2)}, u32[]{:S(2)}) %collective-permute-start.5) | collective-permute-done | bytes 131104 | tf_op jit(solution)/shard_map/ppermute | solution.py:360
  63.2 0.0 copy-done.13
  63.2 0.0 copy-done.5
  63.3 0.0 copy-done.7
  63.3 0.0 copy-done.9
  63.3 0.0 copy-done.11
  63.3 6.2 %shard_map.117 = (f32[2,256,384]{2,1,0:T(8,128)S(1)}, f32[2,128,256]{2,1,0:T(8,128)S(1)}, f32[2,256,256]{2,1,0:T(8,128)S(1)}, f32[2,256,256]{2,1,0:T(8,128)S(1)}) custom-call(s32[2,2]{1,0:T(2,128)} %bitcast.pos, s32[2]{0:T(128)S(1)} %pad_add_fusion.info, f32[2,256,384]{2,1,0:T(8,128)S(1)} %get-tuple-element.21.source, ...), custom_call_target="tpu_custom_call", output_to_operand_aliasing={{0}: (2, {})} | custom-call | tf_op jit(solution)/shard_map/pallas_call | solution.py:344
  69.5 2.3 %collective-permute-start.8 = (f32[2,256,256]{2,1,0:T(8,128)S(1)}, f32[2,256,256]{2,1,0:T(8,128)S(1)}, u32[]{:S(2)}, u32[]{:S(2)}) collective-permute-start(f32[2,256,256]{2,1,0:T(8,128)S(1)} %get-tuple-element.27), channel_id=1, source_target_pairs={{0,1},{1,0},{2,3},{3,2},{4,5},{5,4},{6,7},{7,6},{8,9},{9,8},{10,11... | collective-permute-start | bytes 1572872 | tf_op jit(solution)/shard_map/ppermute | solution.py:368
  71.8 1.5 collective-permute-done.8
  73.3 0.1 add.11
  73.3 16.1 %all_to_all.20 = f32[16,32,256]{2,1,0:T(8,128)S(1)} all-to-all(f32[16,32,256]{2,1,0:T(8,128)S(1)} %bitcast.8), channel_id=1, replica_groups=mesh['row_0'=4,'row_1'=4,'col_0'=4,'col_1'=4,'col_2'=2] {'row_0','col_1'}, dimensions={0} | all-to-all | bytes 1048576 | tf_op jit(solution)/shard_map/all_to_all | solution.py:364
  89.5 8.3 %all_to_all.21 = f32[4,32,256]{2,1,0:T(8,128)S(1)} all-to-all(f32[4,32,256]{2,1,0:T(8,128)S(1)} %broadcast_in_dim.9), channel_id=1, replica_groups=mesh['row_0'=4,'row_1'=4,'col_0'=4,'col_1'=4,'col_2'=2] {'col_0'}, dimensions={0} | all-to-all | bytes 262144 | tf_op jit(solution)/shard_map/all_to_all | solution.py:364
  97.8 21.6 %all_to_all.22 = f32[4,32,256]{2,1,0:T(8,128)S(1)} all-to-all(f32[4,32,256]{2,1,0:T(8,128)S(1)} %broadcast_in_dim.10), channel_id=1, replica_groups=mesh['row_0'=4,'row_1'=4,'col_0'=4,'col_1'=4,'col_2'=2] {'row_1'}, dimensions={0} | all-to-all | bytes 262144 | tf_op jit(solution)/shard_map/all_to_all | solution.py:364
  119.5 0.8 broadcast_in_dim.11
  120.3 6.7 %all-to-all-start.3 = ((f32[16,32,256]{2,1,0:T(8,128)}), f32[16,32,256]{2,1,0:T(8,128)S(1)}, u32[]{:S(2)}, u32[]{:S(2)}) async-start(f32[16,32,256]{2,1,0:T(8,128)} %broadcast_in_dim.11), calls=%async_computation.3 | async-start | bytes 1048576 | tf_op jit(solution)/shard_map/all_to_all | solution.py:364
  127.0 4.1 %collective-permute-start.6 = (f32[2,128,256]{2,1,0:T(8,128)S(1)}, f32[2,128,256]{2,1,0:T(8,128)S(1)}, u32[]{:S(2)}, u32[]{:S(2)}) collective-permute-start(f32[2,128,256]{2,1,0:T(8,128)S(1)} %get-tuple-element.25), channel_id=1, source_target_pairs={{0,32},{32,64},{64,96},{96,128},{128,160},{160,192},{192,224},{224... | collective-permute-start | bytes 786440 | tf_op jit(solution)/shard_map/ppermute | solution.py:360
  131.2 3.1 %all-to-all-done.3 = f32[16,32,256]{2,1,0:T(8,128)S(1)} async-done(((f32[16,32,256]{2,1,0:T(8,128)}), f32[16,32,256]{2,1,0:T(8,128)S(1)}, u32[]{:S(2)}, u32[]{:S(2)}) %all-to-all-start.3) | async-done | bytes 524320 | tf_op jit(solution)/shard_map/all_to_all | solution.py:364
  134.3 1.9 %collective-permute-start.9 = (f32[2,256,256]{2,1,0:T(8,128)S(1)}, f32[2,256,256]{2,1,0:T(8,128)S(1)}, u32[]{:S(2)}, u32[]{:S(2)}) collective-permute-start(f32[2,256,256]{2,1,0:T(8,128)S(1)} %bitcast.6), channel_id=1, source_target_pairs={{0,1},{1,0},{2,3},{3,2},{4,5},{5,4},{6,7},{7,6},{8,9},{9,8},{10,11... | collective-permute-start | bytes 1572872 | tf_op jit(solution)/shard_map/ppermute | solution.py:368
  136.2 18.2 %collective-permute-done.6.from_above = f32[2,128,256]{2,1,0:T(8,128)S(1)} collective-permute-done((f32[2,128,256]{2,1,0:T(8,128)S(1)}, f32[2,128,256]{2,1,0:T(8,128)S(1)}, u32[]{:S(2)}, u32[]{:S(2)}) %collective-permute-start.6) | collective-permute-done | bytes 262176 | tf_op jit(solution)/shard_map/ppermute | solution.py:360
  154.5 0.6 shard_map.118
  155.0 1.9 %collective-permute-start.7 = (f32[2,384,128]{2,1,0:T(8,128)S(1)}, f32[2,384,128]{2,1,0:T(8,128)S(1)}, u32[]{:S(2)}, u32[]{:S(2)}) collective-permute-start(f32[2,384,128]{2,1,0:T(8,128)S(1)} %shard_map.118), channel_id=1, source_target_pairs={{0,1},{1,2},{2,3},{3,4},{4,5},{5,6},{6,7},{7,8},{8,9},{9,10},{10,1... | collective-permute-start | bytes 1179656 | tf_op jit(solution)/shard_map/ppermute | solution.py:360
  157.0 7.2 %collective-permute-done.7.from_left = f32[2,384,128]{2,1,0:T(8,128)S(1)} collective-permute-done((f32[2,384,128]{2,1,0:T(8,128)S(1)}, f32[2,384,128]{2,1,0:T(8,128)S(1)}, u32[]{:S(2)}, u32[]{:S(2)}) %collective-permute-start.7) | collective-permute-done | bytes 393248 | tf_op jit(solution)/shard_map/ppermute | solution.py:360
  164.1 0.0 copy-done.2
  164.1 1.5 shard_map.119
  165.7 0.0 collective-permute-done.9.other
  165.7 0.0 copy-done.1
  165.7 0.0 copy-done.14
  165.7 1.6 shard_map.120
  (12 shorter events, 0.1 us)
Async XLA Ops:
  1.8 7.4 %copy-start = (f32[2,2,256,256]{3,2,1,0:T(8,128)S(1)}, f32[2,2,256,256]{3,2,1,0:T(8,128)}, u32[]{:S(2)}) copy-start(f32[2,2,256,256]{3,2,1,0:T(8,128)} %probe.3) | copy-start | bytes 3145732
  1.8 7.3 %collective-permute-start.1 = (f32[2,384,128]{2,1,0:T(8,128)S(1)}, f32[2,384,128]{2,1,0:T(8,128)S(1)}, u32[]{:S(2)}, u32[]{:S(2)}) collective-permute-start(f32[2,384,128]{2,1,0:T(8,128)S(1)} %slice.3), channel_id=1, source_target_pairs={{1,0},{2,1},{3,2},{4,3},{5,4},{6,5},{7,6},{8,7},{9,8},{10,9},{11,1... | collective-permute-start | bytes 1179656 | tf_op jit(solution)/shard_map/ppermute | solution.py:360
  3.9 5.3 %copy-start.3 = (f32[2,128,128]{2,1,0:T(8,128)S(1)}, f32[2,128,128]{2,1,0:T(8,128)}, u32[]{:S(2)}) copy-start(f32[2,128,128]{2,1,0:T(8,128)} %constant.38.clone.rows) | copy-start | bytes 393220
  3.9 5.3 %copy-start.4 = (bf16[256,256]{1,0:T(8,128)(2,1)S(1)}, bf16[256,256]{1,0:T(8,128)(2,1)}, u32[]{:S(2)}) copy-start(bf16[256,256]{1,0:T(8,128)(2,1)} %constant.37.clone.low_t) | copy-start | bytes 393220
  3.9 5.3 %copy-start.6 = (bf16[256,256]{1,0:T(8,128)(2,1)S(1)}, bf16[256,256]{1,0:T(8,128)(2,1)}, u32[]{:S(2)}) copy-start(bf16[256,256]{1,0:T(8,128)(2,1)} %constant.36.clone.high_t) | copy-start | bytes 393220
  3.9 5.3 %copy-start.8 = (bf16[256,256]{1,0:T(8,128)(2,1)S(1)}, bf16[256,256]{1,0:T(8,128)(2,1)}, u32[]{:S(2)}) copy-start(bf16[256,256]{1,0:T(8,128)(2,1)} %constant.35.clone.low) | copy-start | bytes 393220
  3.9 5.2 %copy-start.10 = (bf16[256,256]{1,0:T(8,128)(2,1)S(1)}, bf16[256,256]{1,0:T(8,128)(2,1)}, u32[]{:S(2)}) copy-start(bf16[256,256]{1,0:T(8,128)(2,1)} %constant.34.clone.high) | copy-start | bytes 393220
  3.9 5.2 %copy-start.12 = (f32[2,8,128]{2,1,0:T(8,128)S(1)}, f32[2,8,128]{2,1,0:T(8,128)}, u32[]{:S(2)}) copy-start(f32[2,8,128]{2,1,0:T(8,128)} %constant.39.clone.cols) | copy-start | bytes 24580
  14.8 0.7 copy-start.15
  15.5 20.7 %collective-permute-start.3 = (f32[2,384,128]{2,1,0:T(8,128)S(1)}, f32[2,384,128]{2,1,0:T(8,128)S(1)}, u32[]{:S(2)}, u32[]{:S(2)}) collective-permute-start(f32[2,384,128]{2,1,0:T(8,128)S(1)} %get-tuple-element.19.edge), channel_id=1, source_target_pairs={{1,0},{2,1},{3,2},{4,3},{5,4},{6,5},{7,6},{8,7},{9,8},{10,9},{11,1... | collective-permute-start | bytes 1179656 | tf_op jit(solution)/shard_map/ppermute | solution.py:360
  19.3 16.9 %collective-permute-start.2 = (f32[2,384,128]{2,1,0:T(8,128)S(1)}, f32[2,384,128]{2,1,0:T(8,128)S(1)}, u32[]{:S(2)}, u32[]{:S(2)}) collective-permute-start(f32[2,384,128]{2,1,0:T(8,128)S(1)} %get-tuple-element.18.spill), channel_id=1, source_target_pairs={{0,1},{1,2},{2,3},{3,4},{4,5},{5,6},{6,7},{7,8},{8,9},{9,10},{10,1... | collective-permute-start | bytes 1179656 | tf_op jit(solution)/shard_map/ppermute | solution.py:360
  21.2 14.9 %collective-permute-start = (s32[2,2]{1,0:T(2,128)}, s32[2,2]{1,0:T(2,128)S(1)}, u32[]{:S(2)}, u32[]{:S(2)}) collective-permute-start(s32[2,2]{1,0:T(2,128)} %bitcast.pos), channel_id=1, source_target_pairs={{0,32},{32,64},{64,96},{96,128},{128,160},{160,192},{192,224},{224... | collective-permute-start | bytes 56 | tf_op jit(solution)/shard_map/ppermute | solution.py:360
  30.4 32.8 %copy-start.13 = (s32[2]{0:T(128)}, s32[2]{0:T(128)S(1)}, u32[]{:S(2)}) copy-start(s32[2]{0:T(128)S(1)} %pad_add_fusion.info) | copy-start | bytes 28
  30.4 27.0 %collective-permute-start.4 = (f32[2,128,128]{2,1,0:T(8,128)}, f32[2,128,128]{2,1,0:T(8,128)S(1)}, u32[]{:S(2)}, u32[]{:S(2)}) collective-permute-start(f32[2,128,128]{2,1,0:T(8,128)} %copy-done.15), channel_id=1, source_target_pairs={{32,0},{64,32},{96,64},{128,96},{160,128},{192,160},{224,192},{256... | collective-permute-start | bytes 393224 | tf_op jit(solution)/shard_map/ppermute | solution.py:360
  36.8 26.5 %collective-permute-start.5 = (f32[2,128,128]{2,1,0:T(8,128)S(1)}, f32[2,128,128]{2,1,0:T(8,128)S(1)}, u32[]{:S(2)}, u32[]{:S(2)}) collective-permute-start(f32[2,128,128]{2,1,0:T(8,128)S(1)} %shard_map.116), channel_id=1, source_target_pairs={{32,0},{64,32},{96,64},{128,96},{160,128},{192,160},{224,192},{256... | collective-permute-start | bytes 393224 | tf_op jit(solution)/shard_map/ppermute | solution.py:360
  44.6 18.6 %copy-start.5 = (bf16[256,256]{1,0:T(8,128)(2,1)S(1)}, bf16[256,256]{1,0:T(8,128)(2,1)}, u32[]{:S(2)}) copy-start(bf16[256,256]{1,0:T(8,128)(2,1)} %constant.37.clone.low_t) | copy-start | bytes 393220
  44.6 18.6 %copy-start.7 = (bf16[256,256]{1,0:T(8,128)(2,1)S(1)}, bf16[256,256]{1,0:T(8,128)(2,1)}, u32[]{:S(2)}) copy-start(bf16[256,256]{1,0:T(8,128)(2,1)} %constant.36.clone.high_t) | copy-start | bytes 393220
  44.6 18.6 %copy-start.9 = (bf16[256,256]{1,0:T(8,128)(2,1)S(1)}, bf16[256,256]{1,0:T(8,128)(2,1)}, u32[]{:S(2)}) copy-start(bf16[256,256]{1,0:T(8,128)(2,1)} %constant.35.clone.low) | copy-start | bytes 393220
  44.6 18.6 %copy-start.11 = (bf16[256,256]{1,0:T(8,128)(2,1)S(1)}, bf16[256,256]{1,0:T(8,128)(2,1)}, u32[]{:S(2)}) copy-start(bf16[256,256]{1,0:T(8,128)(2,1)} %constant.34.clone.high) | copy-start | bytes 393220
  69.5 3.8 %collective-permute-start.8 = (f32[2,256,256]{2,1,0:T(8,128)S(1)}, f32[2,256,256]{2,1,0:T(8,128)S(1)}, u32[]{:S(2)}, u32[]{:S(2)}) collective-permute-start(f32[2,256,256]{2,1,0:T(8,128)S(1)} %get-tuple-element.27), channel_id=1, source_target_pairs={{0,1},{1,0},{2,3},{3,2},{4,5},{5,4},{6,7},{7,6},{8,9},{9,8},{10,11... | collective-permute-start | bytes 1572872 | tf_op jit(solution)/shard_map/ppermute | solution.py:368
  120.3 14.0 %all-to-all-start.3 = ((f32[16,32,256]{2,1,0:T(8,128)}), f32[16,32,256]{2,1,0:T(8,128)S(1)}, u32[]{:S(2)}, u32[]{:S(2)}) async-start(f32[16,32,256]{2,1,0:T(8,128)} %broadcast_in_dim.11), calls=%async_computation.3 | async-start | bytes 1048576 | tf_op jit(solution)/shard_map/all_to_all | solution.py:364
  127.0 37.1 %copy-start.2 = (f32[2,384,256]{2,1,0:T(8,128)S(1)}, f32[2,384,256]{2,1,0:T(8,128)}, u32[]{:S(2)}) copy-start(f32[2,384,256]{2,1,0:T(8,128)} %get-tuple-element.20.whole) | copy-start | bytes 2359300
  127.0 27.4 %collective-permute-start.6 = (f32[2,128,256]{2,1,0:T(8,128)S(1)}, f32[2,128,256]{2,1,0:T(8,128)S(1)}, u32[]{:S(2)}, u32[]{:S(2)}) collective-permute-start(f32[2,128,256]{2,1,0:T(8,128)S(1)} %get-tuple-element.25), channel_id=1, source_target_pairs={{0,32},{32,64},{64,96},{96,128},{128,160},{160,192},{192,224},{224... | collective-permute-start | bytes 786440 | tf_op jit(solution)/shard_map/ppermute | solution.py:360
  134.3 31.4 %collective-permute-start.9 = (f32[2,256,256]{2,1,0:T(8,128)S(1)}, f32[2,256,256]{2,1,0:T(8,128)S(1)}, u32[]{:S(2)}, u32[]{:S(2)}) collective-permute-start(f32[2,256,256]{2,1,0:T(8,128)S(1)} %bitcast.6), channel_id=1, source_target_pairs={{0,1},{1,0},{2,3},{3,2},{4,5},{5,4},{6,7},{7,6},{8,9},{9,8},{10,11... | collective-permute-start | bytes 1572872 | tf_op jit(solution)/shard_map/ppermute | solution.py:368
  155.0 9.1 %collective-permute-start.7 = (f32[2,384,128]{2,1,0:T(8,128)S(1)}, f32[2,384,128]{2,1,0:T(8,128)S(1)}, u32[]{:S(2)}, u32[]{:S(2)}) collective-permute-start(f32[2,384,128]{2,1,0:T(8,128)S(1)} %shard_map.118), channel_id=1, source_target_pairs={{0,1},{1,2},{2,3},{3,4},{4,5},{5,6},{6,7},{7,8},{8,9},{9,10},{10,1... | collective-permute-start | bytes 1179656 | tf_op jit(solution)/shard_map/ppermute | solution.py:360
  164.1 1.6 copy-start.1
  164.1 1.6 copy-start.14

commit v6 on v5

--- a/solution.py
+++ b/solution.py
@@ -175,6 +175,7 @@
 TILE_R = 384
 LAST = TILE_R - WIN
 WIDE = WIN + HALO
+LOW = 192
 
 
 def cut_window(tiles, tall, win, row, col):
@@ -206,7 +207,7 @@
 
 
 def first_kernel(pos, obj, halo, probe, amp_hbm, step, high, low, high_t, low_t, rows, cols,
-                 new_obj, edge, spill, middle, sum_hbm,
+                 new_obj, spill, edge, middle, sum_hbm,
                  far, win, grad, tall, amp, probe_sum, sems):
     row, col = pos[0, 0], pos[0, 1]
     sum_copy = lambda m: pltpu.make_async_copy(probe_sum.at[m], sum_hbm.at[m], sems.at[2 + m])
@@ -227,7 +228,8 @@
         g = placed(grad, scale, tall, row, col, k)
         updated = obj[k] + g[:, :WIN]
         new_obj[k] = updated
-        edge[k] = updated[:, :HALO]
+        edge[k, :HALO] = updated[:HALO, :HALO]
+        edge[k, HALO:] = updated[LOW:, :HALO]
         middle[k] = updated[:HALO, HALO:]
         spill[k] = g[:, WIN:]
     for k in range(2):
@@ -255,7 +257,8 @@
         whole_copy(k).start()
         source[k, :, :HALO] = left[LAST:]
         source[k, :, HALO:WIN] = obj[k, LAST:, HALO:]
-        source[k, :, WIN:] = from_right[k, LAST:] + spill[k, LAST:] * keep
+        source[k, :LOW - LAST, WIN:] = jnp.zeros((LOW - LAST, HALO), jnp.float32)
+        source[k, LOW - LAST:, WIN:] = from_right[k, HALO:] + spill[k, LOW:] * keep
     for k in range(2):
         whole_copy(k).wait()
 
@@ -317,10 +320,25 @@
         out[k, LAST:, HALO:] = whole[k, LAST:, HALO:] + own_grad[k, :, HALO:WIN]
 
 
-def probe_kernel(info, probe, own, other, out):
+def own_kernel(info, probe_hbm, own, out_hbm, rest, probe, half, sems):
     core = info[1]
-    out[core] = probe[core] + own[...]
-    out[1 - core] = probe[1 - core] + other[...]
+    here = pltpu.make_async_copy(probe_hbm.at[core], probe, sems.at[0])
+    there = pltpu.make_async_copy(probe_hbm.at[1 - core], rest, sems.at[1])
+    done = pltpu.make_async_copy(half, out_hbm.at[core], sems.at[2])
+    here.start()
+    there.start()
+    here.wait()
+    half[...] = probe[...] + own[...]
+    done.start()
+    there.wait()
+    done.wait()
+
+
+def other_kernel(info, partial_hbm, rest, other, out_hbm, half, sems):
+    done = pltpu.make_async_copy(half, out_hbm.at[1 - info[1]], sems.at[0])
+    half[...] = rest[...] + other[...]
+    done.start()
+    done.wait()
 
 
 HBM = object()
@@ -341,6 +359,8 @@
     operands = [
         x if INTERPRET or where is AUTO else pltpu.with_memory_space_constraint(x, spaces[where]) for x, where in arrays
     ]
+    if not INTERPRET:
+        scalars = [pltpu.with_memory_space_constraint(x, pltpu.SMEM) for x in scalars]
     return pl.pallas_call(
         kernel,
         out_shape=shapes,
@@ -398,8 +418,8 @@
         before_kernel, [((BATCHES, WIN, WIN), HBM), (8, HALF)],
         [probe_shape, pltpu.VMEM((BATCHES, WIN, WIN), jnp.bfloat16), (BATCHES, WIN, WIN)],
         [], [(probe_modes, HBM), (amplitudes[0, 0], HBM)], copies=4)
-    obj, edge, spill, middle, probe_sum = call(
-        first_kernel, [tile, side, side, block, (probe_shape, HBM)], fit_scratch, [positions],
+    obj, spill, edge, middle, probe_sum = call(
+        first_kernel, [tile, side, (2, TILE_R - LOW + HALO, HALO), block, (probe_shape, HBM)], fit_scratch, [positions],
         [object_field, halo, probe_modes, (amp, HBM), step, *tables], copies=5, in_place={1: 0, 2: 1})
     from_right = passed_along(edge, COL, -1)
     from_left = passed_along(spill, COL, 1)
@@ -418,7 +438,10 @@
     from_left = passed_along(spill, COL, 1)
     (object_out,) = call(
         object_kernel, [(tile, AUTO)], [], [above], [(whole, AUTO), (grad, AUTO), (from_above, AUTO), (from_left, AUTO)])
-    (probe_out,) = call(probe_kernel, [(probe_shape, AUTO)], [], [info], [(probe_modes, AUTO), own, other])
+    partial, rest = call(
+        own_kernel, [(probe_shape, HBM), window], [window, window], [info], [(probe_modes, HBM), own], copies=3)
+    (probe_out,) = call(
+        other_kernel, [(probe_shape, HBM)], [window], [info], [(partial, HBM), rest, other], copies=1, in_place={1: 0})
     return (object_out, probe_out)
 
 

time: 168 us -> 170 us (1.012)
  the two profiles are of different devices: /device:TPU:26 before, /device:TPU:104 now
where the time goes in v6:
time: 170 us
  waiting for transfers between devices  48.7 us (29%)
  blocking collectives  47.7 us (28%)
  starting transfers between devices  46.1 us (27%)
  Pallas kernels  22.8 us (13%)
  local copies, waits for them, and re-layouts  3.35 us (2%)
    all_to_all x3, blocking collectives, exchanged(): return lax.all_to_all(parts, axes, 0, 0, tiled=False)  47.7 us
    ppermute x8, waiting for transfers between devices, passed_along(): return lax.ppermute(block, axis, route)  41.2 us
    ppermute x8, starting transfers between devices, passed_along(): return lax.ppermute(block, axis, route)  36.5 us
    pallas_call x9, Pallas kernels, call(): pl.pallas_call(kernel, out_shape=shapes, in_specs=[smem] * len(scalars) +...  22.8 us
    all_to_all x1, starting transfers between devices, exchanged(): return lax.all_to_all(parts, axes, 0, 0, tiled=False)  5.77 us
    all_to_all x1, waiting for transfers between devices, exchanged(): return lax.all_to_all(parts, axes, 0, 0, tiled=False)  5.61 us
    ppermute x2, starting transfers between devices, swapped(): return lax.ppermute(block, CORE, [(0, 1), (1, 0)])  3.83 us
  transfers between devices with their start and end apart: 11, of which 7 were waited for; matrix products, arithmetic and copies ran while one was open for 0% of the time, Pallas kernels for 5%

profile of v6, /device:TPU:104, one launch (start us, length us, event | category | flops | bytes accessed | tf_op | source)
XLA Modules:
  0.0 169.7 jit_solution(14784405267237450539)
XLA Ops:
  0.6 1.1 copy.21.obj
  1.8 0.0 copy-start
  1.8 3.8 %collective-permute-start.1 = (f32[2,384,128]{2,1,0:T(8,128)S(1)}, f32[2,384,128]{2,1,0:T(8,128)S(1)}, u32[]{:S(2)}, u32[]{:S(2)}) collective-permute-start(f32[2,384,128]{2,1,0:T(8,128)S(1)} %slice.3), channel_id=1, source_target_pairs={{1,0},{2,1},{3,2},{4,3},{5,4},{6,5},{7,6},{8,7},{9,8},{10,9},{11,1... | collective-permute-start | bytes 1179656 | tf_op jit(solution)/shard_map/ppermute | solution.py:380
  5.6 0.0 copy-start.2
  5.6 0.0 copy-start.3
  5.6 0.0 copy-start.4
  5.6 0.0 copy-start.5
  5.6 0.0 copy-start.6
  5.6 0.0 copy-start.8
  5.7 2.2 %shard_map.113 = (f32[2,256,256]{2,1,0:T(8,128)}, f32[8,128]{1,0:T(8,128)S(1)}) custom-call(f32[2,2,256,256]{3,2,1,0:T(8,128)} %probe_hbm.5, bf16[2,256,256]{2,1,0:T(8,128)(2,1)} %bitcast.12), custom_call_target="tpu_custom_call" | custom-call | tf_op jit(solution)/shard_map/pallas_call | solution.py:364
  7.9 3.0 %collective-permute-done.1.halo = f32[2,384,128]{2,1,0:T(8,128)S(1)} collective-permute-done((f32[2,384,128]{2,1,0:T(8,128)S(1)}, f32[2,384,128]{2,1,0:T(8,128)S(1)}, u32[]{:S(2)}, u32[]{:S(2)}) %collective-permute-start.1) | collective-permute-done | bytes 393248 | tf_op jit(solution)/shard_map/ppermute | solution.py:380
  10.9 0.0 copy-start.9
  10.9 0.0 copy-done
  10.9 0.0 copy-done.2
  10.9 0.0 copy-done.3
  10.9 0.0 copy-done.4
  10.9 0.0 copy-done.5
  10.9 0.0 copy-done.6
  10.9 0.0 copy-done.8
  10.9 0.6 copy-done.9
  11.5 6.2 %shard_map.114 = (f32[2,384,256]{2,1,0:T(8,128)S(1)}, f32[2,384,128]{2,1,0:T(8,128)S(1)}, f32[2,320,128]{2,1,0:T(8,128)}, f32[2,128,128]{2,1,0:T(8,128)S(1)}, f32[2,2,256,256]{3,2,1,0:T(8,128)}) custom-call(s32[2,2]{1,0:T(2,128)S(1)} %bitcast.8, f32[2,384,256]{2,1,0:T(8,128)S(1)} %copy.21.obj, ...), custom_call_target="tpu_custom_call", output_to_operand_aliasing={{0}: (1, {}), {1}: (2, {})} | custom-call | tf_op jit(solution)/shard_map/pallas_call | solution.py:364
  17.7 0.0 copy-start.10
  17.7 0.6 copy-done.10
  18.4 1.9 %collective-permute-start.2 = (f32[2,384,128]{2,1,0:T(8,128)S(1)}, f32[2,384,128]{2,1,0:T(8,128)S(1)}, u32[]{:S(2)}, u32[]{:S(2)}) collective-permute-start(f32[2,384,128]{2,1,0:T(8,128)S(1)} %get-tuple-element.20.spill), channel_id=1, source_target_pairs={{0,1},{1,2},{2,3},{3,4},{4,5},{5,6},{6,7},{7,8},{8,9},{9,10},{10,1... | collective-permute-start | bytes 1179656 | tf_op jit(solution)/shard_map/ppermute | solution.py:380
  20.3 5.9 %collective-permute-start.3 = (f32[2,320,128]{2,1,0:T(8,128)}, f32[2,320,128]{2,1,0:T(8,128)S(1)}, u32[]{:S(2)}, u32[]{:S(2)}) collective-permute-start(f32[2,320,128]{2,1,0:T(8,128)} %get-tuple-element.21.edge), channel_id=1, source_target_pairs={{1,0},{2,1},{3,2},{4,3},{5,4},{6,5},{7,6},{8,7},{9,8},{10,9},{11,1... | collective-permute-start | bytes 983048 | tf_op jit(solution)/shard_map/ppermute | solution.py:380
  26.2 9.1 %collective-permute-start = (s32[2,2]{1,0:T(2,128)S(1)}, s32[2,2]{1,0:T(2,128)S(1)}, u32[]{:S(2)}, u32[]{:S(2)}) collective-permute-start(s32[2,2]{1,0:T(2,128)S(1)} %bitcast.9), channel_id=1, source_target_pairs={{0,32},{32,64},{64,96},{96,128},{128,160},{160,192},{192,224},{224... | collective-permute-start | bytes 56 | tf_op jit(solution)/shard_map/ppermute | solution.py:380
  35.3 0.1 pad_add_fusion.info
  35.4 3.6 %collective-permute-start.4 = (f32[2,128,128]{2,1,0:T(8,128)}, f32[2,128,128]{2,1,0:T(8,128)S(1)}, u32[]{:S(2)}, u32[]{:S(2)}) collective-permute-start(f32[2,128,128]{2,1,0:T(8,128)} %copy-done.10), channel_id=1, source_target_pairs={{32,0},{64,32},{96,64},{128,96},{160,128},{192,160},{224,192},{256... | collective-permute-start | bytes 393224 | tf_op jit(solution)/shard_map/ppermute | solution.py:380
  39.0 0.0 collective-permute-done.above
  39.0 0.0 collective-permute-done.3.from_right
  39.1 0.0 collective-permute-done.2.from_left
  39.1 1.0 shard_map.116
  40.1 7.8 %collective-permute-start.5 = (f32[2,128,128]{2,1,0:T(8,128)S(1)}, f32[2,128,128]{2,1,0:T(8,128)S(1)}, u32[]{:S(2)}, u32[]{:S(2)}) collective-permute-start(f32[2,128,128]{2,1,0:T(8,128)S(1)} %shard_map.116), channel_id=1, source_target_pairs={{32,0},{64,32},{96,64},{128,96},{160,128},{192,160},{224,192},{256... | collective-permute-start | bytes 393224 | tf_op jit(solution)/shard_map/ppermute | solution.py:380
  47.9 0.0 copy-start.7
  47.9 1.5 shard_map.115
  49.4 8.4 %collective-permute-done.4.below_mid = f32[2,128,128]{2,1,0:T(8,128)S(1)} collective-permute-done((f32[2,128,128]{2,1,0:T(8,128)}, f32[2,128,128]{2,1,0:T(8,128)S(1)}, u32[]{:S(2)}, u32[]{:S(2)}) %collective-permute-start.4) | collective-permute-done | bytes 131104 | tf_op jit(solution)/shard_map/ppermute | solution.py:380
  57.8 3.3 %collective-permute-done.5.below_rest = f32[2,128,128]{2,1,0:T(8,128)S(1)} collective-permute-done((f32[2,128,128]{2,1,0:T(8,128)S(1)}, f32[2,128,128]{2,1,0:T(8,128)S(1)}, u32[]{:S(2)}, u32[]{:S(2)}) %collective-permute-start.5) | collective-permute-done | bytes 131104 | tf_op jit(solution)/shard_map/ppermute | solution.py:380
  61.1 0.0 copy-done.7
  61.1 6.0 %shard_map.117 = (f32[2,256,384]{2,1,0:T(8,128)S(1)}, f32[2,128,256]{2,1,0:T(8,128)S(1)}, f32[2,256,256]{2,1,0:T(8,128)S(1)}, f32[2,256,256]{2,1,0:T(8,128)S(1)}) custom-call(s32[2,2]{1,0:T(2,128)S(1)} %bitcast.10, s32[2]{0:T(128)S(1)} %pad_add_fusion.info, f32[2,256,384]{2,1,0:T(8,128)S(1)} %get-tuple-element.23.source, ...), custom_call_target="tpu_custom_call", output_to_operand_aliasing={{0}: (2, {})} | custom-call | tf_op jit(solution)/shard_map/pallas_call | solution.py:364
  67.1 1.9 %collective-permute-start.8 = (f32[2,256,256]{2,1,0:T(8,128)S(1)}, f32[2,256,256]{2,1,0:T(8,128)S(1)}, u32[]{:S(2)}, u32[]{:S(2)}) collective-permute-start(f32[2,256,256]{2,1,0:T(8,128)S(1)} %get-tuple-element.29), channel_id=1, source_target_pairs={{0,1},{1,0},{2,3},{3,2},{4,5},{5,4},{6,7},{7,6},{8,9},{9,8},{10,11... | collective-permute-start | bytes 1572872 | tf_op jit(solution)/shard_map/ppermute | solution.py:388
  69.0 1.9 %collective-permute-done.8 = f32[2,256,256]{2,1,0:T(8,128)S(1)} collective-permute-done((f32[2,256,256]{2,1,0:T(8,128)S(1)}, f32[2,256,256]{2,1,0:T(8,128)S(1)}, u32[]{:S(2)}, u32[]{:S(2)}) %collective-permute-start.8) | collective-permute-done | bytes 524320 | tf_op jit(solution)/shard_map/ppermute | solution.py:388
  70.9 0.1 add.11
  71.0 14.0 %all_to_all.20 = f32[16,32,256]{2,1,0:T(8,128)S(1)} all-to-all(f32[16,32,256]{2,1,0:T(8,128)S(1)} %bitcast.11), channel_id=1, replica_groups=mesh['row_0'=4,'row_1'=4,'col_0'=4,'col_1'=4,'col_2'=2] {'row_0','col_1'}, dimensions={0} | all-to-all | bytes 1048576 | tf_op jit(solution)/shard_map/all_to_all | solution.py:384
  85.0 11.5 %all_to_all.21 = f32[4,32,256]{2,1,0:T(8,128)S(1)} all-to-all(f32[4,32,256]{2,1,0:T(8,128)S(1)} %broadcast_in_dim.9), channel_id=1, replica_groups=mesh['row_0'=4,'row_1'=4,'col_0'=4,'col_1'=4,'col_2'=2] {'col_0'}, dimensions={0} | all-to-all | bytes 262144 | tf_op jit(solution)/shard_map/all_to_all | solution.py:384
  96.5 22.2 %all_to_all.22 = f32[4,32,256]{2,1,0:T(8,128)S(1)} all-to-all(f32[4,32,256]{2,1,0:T(8,128)S(1)} %broadcast_in_dim.10), channel_id=1, replica_groups=mesh['row_0'=4,'row_1'=4,'col_0'=4,'col_1'=4,'col_2'=2] {'row_1'}, dimensions={0} | all-to-all | bytes 262144 | tf_op jit(solution)/shard_map/all_to_all | solution.py:384
  118.7 0.8 broadcast_in_dim.11
  119.6 5.8 %all-to-all-start.3 = ((f32[16,32,256]{2,1,0:T(8,128)}), f32[16,32,256]{2,1,0:T(8,128)S(1)}, u32[]{:S(2)}, u32[]{:S(2)}) async-start(f32[16,32,256]{2,1,0:T(8,128)} %broadcast_in_dim.11), calls=%async_computation.3 | async-start | bytes 1048576 | tf_op jit(solution)/shard_map/all_to_all | solution.py:384
  125.4 0.0 copy-start.1
  125.4 2.4 %collective-permute-start.6 = (f32[2,128,256]{2,1,0:T(8,128)S(1)}, f32[2,128,256]{2,1,0:T(8,128)S(1)}, u32[]{:S(2)}, u32[]{:S(2)}) collective-permute-start(f32[2,128,256]{2,1,0:T(8,128)S(1)} %get-tuple-element.27), channel_id=1, source_target_pairs={{0,32},{32,64},{64,96},{96,128},{128,160},{160,192},{192,224},{224... | collective-permute-start | bytes 786440 | tf_op jit(solution)/shard_map/ppermute | solution.py:380
  127.8 5.6 %all-to-all-done.3 = f32[16,32,256]{2,1,0:T(8,128)S(1)} async-done(((f32[16,32,256]{2,1,0:T(8,128)}), f32[16,32,256]{2,1,0:T(8,128)S(1)}, u32[]{:S(2)}, u32[]{:S(2)}) %all-to-all-start.3) | async-done | bytes 524320 | tf_op jit(solution)/shard_map/all_to_all | solution.py:384
  133.4 1.9 %collective-permute-start.9 = (f32[2,256,256]{2,1,0:T(8,128)S(1)}, f32[2,256,256]{2,1,0:T(8,128)S(1)}, u32[]{:S(2)}, u32[]{:S(2)}) collective-permute-start(f32[2,256,256]{2,1,0:T(8,128)S(1)} %bitcast.6), channel_id=1, source_target_pairs={{0,1},{1,0},{2,3},{3,2},{4,5},{5,4},{6,7},{7,6},{8,9},{9,8},{10,11... | collective-permute-start | bytes 1572872 | tf_op jit(solution)/shard_map/ppermute | solution.py:388
  135.3 17.3 %collective-permute-done.6.from_above = f32[2,128,256]{2,1,0:T(8,128)S(1)} collective-permute-done((f32[2,128,256]{2,1,0:T(8,128)S(1)}, f32[2,128,256]{2,1,0:T(8,128)S(1)}, u32[]{:S(2)}, u32[]{:S(2)}) %collective-permute-start.6) | collective-permute-done | bytes 262176 | tf_op jit(solution)/shard_map/ppermute | solution.py:380
  152.6 0.6 shard_map.118
  153.1 1.9 %collective-permute-start.7 = (f32[2,384,128]{2,1,0:T(8,128)S(1)}, f32[2,384,128]{2,1,0:T(8,128)S(1)}, u32[]{:S(2)}, u32[]{:S(2)}) collective-permute-start(f32[2,384,128]{2,1,0:T(8,128)S(1)} %shard_map.118), channel_id=1, source_target_pairs={{0,1},{1,2},{2,3},{3,4},{4,5},{5,6},{6,7},{7,8},{8,9},{9,10},{10,1... | collective-permute-start | bytes 1179656 | tf_op jit(solution)/shard_map/ppermute | solution.py:380
  155.1 9.3 %collective-permute-done.7.from_left = f32[2,384,128]{2,1,0:T(8,128)S(1)} collective-permute-done((f32[2,384,128]{2,1,0:T(8,128)S(1)}, f32[2,384,128]{2,1,0:T(8,128)S(1)}, u32[]{:S(2)}, u32[]{:S(2)}) %collective-permute-start.7) | collective-permute-done | bytes 393248 | tf_op jit(solution)/shard_map/ppermute | solution.py:380
  164.3 0.0 copy-done.1
  164.3 1.5 shard_map.119
  165.9 2.5 %shard_map.120 = (f32[2,2,256,256]{3,2,1,0:T(8,128)}, f32[2,256,256]{2,1,0:T(8,128)S(1)}) custom-call(s32[2]{0:T(128)S(1)} %pad_add_fusion.info, f32[2,2,256,256]{3,2,1,0:T(8,128)} %probe_hbm.5, f32[2,256,256]{2,1,0:T(8,128)S(1)} %bitcast.7), custom_call_target="tpu_custom_call" | custom-call | tf_op jit(solution)/shard_map/pallas_call | solution.py:364
  168.3 0.0 collective-permute-done.9.other
  168.3 1.4 shard_map.121
  (7 shorter events, 0.1 us)
Async XLA Ops:
  1.8 9.1 %copy-start = (f32[2,2,256,256]{3,2,1,0:T(8,128)S(1)}, f32[2,2,256,256]{3,2,1,0:T(8,128)}, u32[]{:S(2)}) copy-start(f32[2,2,256,256]{3,2,1,0:T(8,128)} %probe_hbm.5) | copy-start | bytes 3145732
  1.8 9.1 %collective-permute-start.1 = (f32[2,384,128]{2,1,0:T(8,128)S(1)}, f32[2,384,128]{2,1,0:T(8,128)S(1)}, u32[]{:S(2)}, u32[]{:S(2)}) collective-permute-start(f32[2,384,128]{2,1,0:T(8,128)S(1)} %slice.3), channel_id=1, source_target_pairs={{1,0},{2,1},{3,2},{4,3},{5,4},{6,5},{7,6},{8,7},{9,8},{10,9},{11,1... | collective-permute-start | bytes 1179656 | tf_op jit(solution)/shard_map/ppermute | solution.py:380
  5.6 5.3 %copy-start.2 = (f32[2,128,128]{2,1,0:T(8,128)S(1)}, f32[2,128,128]{2,1,0:T(8,128)}, u32[]{:S(2)}) copy-start(f32[2,128,128]{2,1,0:T(8,128)} %constant.38.clone.rows) | copy-start | bytes 393220
  5.6 5.3 %copy-start.3 = (bf16[256,256]{1,0:T(8,128)(2,1)S(1)}, bf16[256,256]{1,0:T(8,128)(2,1)}, u32[]{:S(2)}) copy-start(bf16[256,256]{1,0:T(8,128)(2,1)} %constant.37.clone.low_t) | copy-start | bytes 393220
  5.6 5.3 %copy-start.4 = (bf16[256,256]{1,0:T(8,128)(2,1)S(1)}, bf16[256,256]{1,0:T(8,128)(2,1)}, u32[]{:S(2)}) copy-start(bf16[256,256]{1,0:T(8,128)(2,1)} %constant.36.clone.high_t) | copy-start | bytes 393220
  5.6 5.3 %copy-start.5 = (bf16[256,256]{1,0:T(8,128)(2,1)S(1)}, bf16[256,256]{1,0:T(8,128)(2,1)}, u32[]{:S(2)}) copy-start(bf16[256,256]{1,0:T(8,128)(2,1)} %constant.35.clone.low) | copy-start | bytes 393220
  5.6 5.3 %copy-start.6 = (bf16[256,256]{1,0:T(8,128)(2,1)S(1)}, bf16[256,256]{1,0:T(8,128)(2,1)}, u32[]{:S(2)}) copy-start(bf16[256,256]{1,0:T(8,128)(2,1)} %constant.34.clone.high) | copy-start | bytes 393220
  5.6 5.3 %copy-start.8 = (f32[2,8,128]{2,1,0:T(8,128)S(1)}, f32[2,8,128]{2,1,0:T(8,128)}, u32[]{:S(2)}) copy-start(f32[2,8,128]{2,1,0:T(8,128)} %constant.39.clone.cols) | copy-start | bytes 24580
  10.9 0.7 copy-start.9
  17.7 0.6 copy-start.10
  18.4 20.7 %collective-permute-start.2 = (f32[2,384,128]{2,1,0:T(8,128)S(1)}, f32[2,384,128]{2,1,0:T(8,128)S(1)}, u32[]{:S(2)}, u32[]{:S(2)}) collective-permute-start(f32[2,384,128]{2,1,0:T(8,128)S(1)} %get-tuple-element.20.spill), channel_id=1, source_target_pairs={{0,1},{1,2},{2,3},{3,4},{4,5},{5,6},{6,7},{7,8},{8,9},{9,10},{10,1... | collective-permute-start | bytes 1179656 | tf_op jit(solution)/shard_map/ppermute | solution.py:380
  20.3 18.8 %collective-permute-start.3 = (f32[2,320,128]{2,1,0:T(8,128)}, f32[2,320,128]{2,1,0:T(8,128)S(1)}, u32[]{:S(2)}, u32[]{:S(2)}) collective-permute-start(f32[2,320,128]{2,1,0:T(8,128)} %get-tuple-element.21.edge), channel_id=1, source_target_pairs={{1,0},{2,1},{3,2},{4,3},{5,4},{6,5},{7,6},{8,7},{9,8},{10,9},{11,1... | collective-permute-start | bytes 983048 | tf_op jit(solution)/shard_map/ppermute | solution.py:380
  26.2 12.9 %collective-permute-start = (s32[2,2]{1,0:T(2,128)S(1)}, s32[2,2]{1,0:T(2,128)S(1)}, u32[]{:S(2)}, u32[]{:S(2)}) collective-permute-start(s32[2,2]{1,0:T(2,128)S(1)} %bitcast.9), channel_id=1, source_target_pairs={{0,32},{32,64},{64,96},{96,128},{128,160},{160,192},{192,224},{224... | collective-permute-start | bytes 56 | tf_op jit(solution)/shard_map/ppermute | solution.py:380
  35.4 22.4 %collective-permute-start.4 = (f32[2,128,128]{2,1,0:T(8,128)}, f32[2,128,128]{2,1,0:T(8,128)S(1)}, u32[]{:S(2)}, u32[]{:S(2)}) collective-permute-start(f32[2,128,128]{2,1,0:T(8,128)} %copy-done.10), channel_id=1, source_target_pairs={{32,0},{64,32},{96,64},{128,96},{160,128},{192,160},{224,192},{256... | collective-permute-start | bytes 393224 | tf_op jit(solution)/shard_map/ppermute | solution.py:380
  40.1 21.0 %collective-permute-start.5 = (f32[2,128,128]{2,1,0:T(8,128)S(1)}, f32[2,128,128]{2,1,0:T(8,128)S(1)}, u32[]{:S(2)}, u32[]{:S(2)}) collective-permute-start(f32[2,128,128]{2,1,0:T(8,128)S(1)} %shard_map.116), channel_id=1, source_target_pairs={{32,0},{64,32},{96,64},{128,96},{160,128},{192,160},{224,192},{256... | collective-permute-start | bytes 393224 | tf_op jit(solution)/shard_map/ppermute | solution.py:380
  47.9 13.2 %copy-start.7 = (bf16[256,256]{1,0:T(8,128)(2,1)S(1)}, bf16[256,256]{1,0:T(8,128)(2,1)}, u32[]{:S(2)}) copy-start(bf16[256,256]{1,0:T(8,128)(2,1)} %constant.34.clone.high) | copy-start | bytes 393220
  67.1 3.8 %collective-permute-start.8 = (f32[2,256,256]{2,1,0:T(8,128)S(1)}, f32[2,256,256]{2,1,0:T(8,128)S(1)}, u32[]{:S(2)}, u32[]{:S(2)}) collective-permute-start(f32[2,256,256]{2,1,0:T(8,128)S(1)} %get-tuple-element.29), channel_id=1, source_target_pairs={{0,1},{1,0},{2,3},{3,2},{4,5},{5,4},{6,7},{7,6},{8,9},{9,8},{10,11... | collective-permute-start | bytes 1572872 | tf_op jit(solution)/shard_map/ppermute | solution.py:388
  119.6 13.8 %all-to-all-start.3 = ((f32[16,32,256]{2,1,0:T(8,128)}), f32[16,32,256]{2,1,0:T(8,128)S(1)}, u32[]{:S(2)}, u32[]{:S(2)}) async-start(f32[16,32,256]{2,1,0:T(8,128)} %broadcast_in_dim.11), calls=%async_computation.3 | async-start | bytes 1048576 | tf_op jit(solution)/shard_map/all_to_all | solution.py:384
  125.4 39.0 %copy-start.1 = (f32[2,384,256]{2,1,0:T(8,128)S(1)}, f32[2,384,256]{2,1,0:T(8,128)}, u32[]{:S(2)}) copy-start(f32[2,384,256]{2,1,0:T(8,128)} %get-tuple-element.22.whole) | copy-start | bytes 2359300
  125.4 27.2 %collective-permute-start.6 = (f32[2,128,256]{2,1,0:T(8,128)S(1)}, f32[2,128,256]{2,1,0:T(8,128)S(1)}, u32[]{:S(2)}, u32[]{:S(2)}) collective-permute-start(f32[2,128,256]{2,1,0:T(8,128)S(1)} %get-tuple-element.27), channel_id=1, source_target_pairs={{0,32},{32,64},{64,96},{96,128},{128,160},{160,192},{192,224},{224... | collective-permute-start | bytes 786440 | tf_op jit(solution)/shard_map/ppermute | solution.py:380
  133.4 35.0 %collective-permute-start.9 = (f32[2,256,256]{2,1,0:T(8,128)S(1)}, f32[2,256,256]{2,1,0:T(8,128)S(1)}, u32[]{:S(2)}, u32[]{:S(2)}) collective-permute-start(f32[2,256,256]{2,1,0:T(8,128)S(1)} %bitcast.6), channel_id=1, source_target_pairs={{0,1},{1,0},{2,3},{3,2},{4,5},{5,4},{6,7},{7,6},{8,9},{9,8},{10,11... | collective-permute-start | bytes 1572872 | tf_op jit(solution)/shard_map/ppermute | solution.py:388
  153.1 11.2 %collective-permute-start.7 = (f32[2,384,128]{2,1,0:T(8,128)S(1)}, f32[2,384,128]{2,1,0:T(8,128)S(1)}, u32[]{:S(2)}, u32[]{:S(2)}) collective-permute-start(f32[2,384,128]{2,1,0:T(8,128)S(1)} %shard_map.118), channel_id=1, source_target_pairs={{0,1},{1,2},{2,3},{3,4},{4,5},{5,6},{6,7},{7,8},{8,9},{9,10},{10,1... | collective-permute-start | bytes 1179656 | tf_op jit(solution)/shard_map/ppermute | solution.py:380

commit v7 on v5

--- a/solution.py
+++ b/solution.py
@@ -175,6 +175,7 @@
 TILE_R = 384
 LAST = TILE_R - WIN
 WIDE = WIN + HALO
+LOW = 192
 
 
 def cut_window(tiles, tall, win, row, col):
@@ -206,7 +207,7 @@
 
 
 def first_kernel(pos, obj, halo, probe, amp_hbm, step, high, low, high_t, low_t, rows, cols,
-                 new_obj, edge, spill, middle, sum_hbm,
+                 new_obj, spill, edge, middle, sum_hbm,
                  far, win, grad, tall, amp, probe_sum, sems):
     row, col = pos[0, 0], pos[0, 1]
     sum_copy = lambda m: pltpu.make_async_copy(probe_sum.at[m], sum_hbm.at[m], sems.at[2 + m])
@@ -227,7 +228,8 @@
         g = placed(grad, scale, tall, row, col, k)
         updated = obj[k] + g[:, :WIN]
         new_obj[k] = updated
-        edge[k] = updated[:, :HALO]
+        edge[k, :HALO] = updated[:HALO, :HALO]
+        edge[k, HALO:] = updated[LOW:, :HALO]
         middle[k] = updated[:HALO, HALO:]
         spill[k] = g[:, WIN:]
     for k in range(2):
@@ -255,14 +257,15 @@
         whole_copy(k).start()
         source[k, :, :HALO] = left[LAST:]
         source[k, :, HALO:WIN] = obj[k, LAST:, HALO:]
-        source[k, :, WIN:] = from_right[k, LAST:] + spill[k, LAST:] * keep
+        source[k, :LOW - LAST, WIN:] = jnp.zeros((LOW - LAST, HALO), jnp.float32)
+        source[k, LOW - LAST:, WIN:] = from_right[k, HALO:] + spill[k, LOW:] * keep
     for k in range(2):
         whole_copy(k).wait()
 
 
-def second_kernel(pos, info, source, below_mid, below_rest, probe_hbm, amp_hbm, step, before_hbm,
+def second_kernel(pos, info, source, below_mid, below_rest, probe_hbm, amp_hbm, before_hbm,
                   high, low, high_t, low_t, rows, cols,
-                  own_grad, downward, keep_sum, send_sum, far, win, grad, tall, amp, probe, before, sems):
+                  grad, keep_sum, send_sum, far, win, tall, amp, probe, before, sems):
     row, col, core = pos[1, 0] - LAST, pos[1, 1], info[1]
     probe_copy = lambda m: pltpu.make_async_copy(probe_hbm.at[m], probe.at[m], sems.at[m])
     before_copy = lambda m: pltpu.make_async_copy(before_hbm.at[m], before.at[m], sems.at[2 + m])
@@ -294,8 +297,13 @@
 
     window_fit(probe, amp, (high, low, high_t, low_t, rows, cols), far, win, grad, add_probe,
                probe_copy, amp_copy)
+
+
+def place_kernel(pos, grad, step, own_grad, downward, tall):
+    row, col = pos[1, 0] - LAST, pos[1, 1]
     scale = step[:1, :1]
     for k in range(2):
+        tall[k] = jnp.zeros((TILE_R + 8, WIN), jnp.float32)
         g = placed(grad, scale, tall, row, col, k)
         own_grad[k] = g[:WIN]
         downward[k, :, :HALO] = g[WIN:, :HALO] + g[WIN:, WIN:]
@@ -341,6 +349,8 @@
     operands = [
         x if INTERPRET or where is AUTO else pltpu.with_memory_space_constraint(x, spaces[where]) for x, where in arrays
     ]
+    if copies == 5 and not INTERPRET:
+        scalars = [pltpu.with_memory_space_constraint(x, pltpu.SMEM) for x in scalars]
     return pl.pallas_call(
         kernel,
         out_shape=shapes,
@@ -398,8 +408,8 @@
         before_kernel, [((BATCHES, WIN, WIN), HBM), (8, HALF)],
         [probe_shape, pltpu.VMEM((BATCHES, WIN, WIN), jnp.bfloat16), (BATCHES, WIN, WIN)],
         [], [(probe_modes, HBM), (amplitudes[0, 0], HBM)], copies=4)
-    obj, edge, spill, middle, probe_sum = call(
-        first_kernel, [tile, side, side, block, (probe_shape, HBM)], fit_scratch, [positions],
+    obj, spill, edge, middle, probe_sum = call(
+        first_kernel, [tile, side, (2, TILE_R - LOW + HALO, HALO), block, (probe_shape, HBM)], fit_scratch, [positions],
         [object_field, halo, probe_modes, (amp, HBM), step, *tables], copies=5, in_place={1: 0, 2: 1})
     from_right = passed_along(edge, COL, -1)
     from_left = passed_along(spill, COL, 1)
@@ -408,10 +418,12 @@
     below_rest = passed_along(upward, ROW, -1)
     whole, source = call(
         merge_kernel, [(tile, HBM), (2, WIN, WIDE)], [tile], [info], [obj, from_left, from_right, spill], copies=2)
-    grad, downward, keep, send = call(
-        second_kernel, [(2, WIN, WIDE), (2, HALO, WIN), window, window],
-        fit_scratch + [probe_shape], [positions, info],
-        [source, below_mid, below_rest, (probe_modes, HBM), (amp, HBM), step, (probe_sum, HBM), *tables], copies=5, in_place={2: 0})
+    grad, keep, send = call(
+        second_kernel, [window, window, window],
+        [probe_shape, window, (2, TILE_R + 8, WIN), (WIN, WIN), probe_shape, probe_shape], [positions, info],
+        [source, below_mid, below_rest, (probe_modes, HBM), (amp, HBM), (probe_sum, HBM), *tables], copies=5)
+    grad, downward = call(
+        place_kernel, [(2, WIN, WIDE), (2, HALO, WIN)], [(2, TILE_R + 8, WIN)], [positions], [grad, step])
     own, other = summed_everywhere(keep, send, divisor)
     from_above = passed_along(downward, ROW, 1)
     (spill,) = call(spill_kernel, [side], [], [above], [grad, from_above])

time: 168 us -> 169 us (level)
  the two profiles are of different devices: /device:TPU:26 before, /device:TPU:48 now
where the time goes in v7:
time: 169 us; the launch traced here: 168 us
  waiting for transfers between devices  49.1 us (29%)
  starting transfers between devices  48.9 us (29%)
  blocking collectives  46.4 us (27%)
  Pallas kernels  20 us (12%)
  local copies, waits for them, and re-layouts  2.71 us (2%)
    all_to_all x3, blocking collectives, exchanged(): return lax.all_to_all(parts, axes, 0, 0, tiled=False)  46.4 us
    ppermute x8, waiting for transfers between devices, passed_along(): return lax.ppermute(block, axis, route)  43.8 us
    ppermute x8, starting transfers between devices, passed_along(): return lax.ppermute(block, axis, route)  39 us
    pallas_call x9, Pallas kernels, call(): pl.pallas_call(kernel, out_shape=shapes, in_specs=[smem] * len(scalars) +...  20 us
    all_to_all x1, starting transfers between devices, exchanged(): return lax.all_to_all(parts, axes, 0, 0, tiled=False)  6.09 us
    ppermute x2, starting transfers between devices, swapped(): return lax.ppermute(block, CORE, [(0, 1), (1, 0)])  3.83 us
    all_to_all x1, waiting for transfers between devices, exchanged(): return lax.all_to_all(parts, axes, 0, 0, tiled=False)  3.48 us
  transfers between devices with their start and end apart: 11, of which 7 were waited for; matrix products, arithmetic and copies ran while one was open for 0% of the time, Pallas kernels for 4%

profile of v7, /device:TPU:48, one launch (start us, length us, event | category | flops | bytes accessed | tf_op | source)
XLA Modules:
  0.0 168.3 jit_solution(11175562820804107941)
XLA Ops:
  0.6 1.1 copy.17.obj
  1.8 0.0 copy-start
  1.8 3.8 %collective-permute-start.1 = (f32[2,384,128]{2,1,0:T(8,128)S(1)}, f32[2,384,128]{2,1,0:T(8,128)S(1)}, u32[]{:S(2)}, u32[]{:S(2)}) collective-permute-start(f32[2,384,128]{2,1,0:T(8,128)S(1)} %slice.3), channel_id=1, source_target_pairs={{1,0},{2,1},{3,2},{4,3},{5,4},{6,5},{7,6},{8,7},{9,8},{10,9},{11,1... | collective-permute-start | bytes 1179656 | tf_op jit(solution)/shard_map/ppermute | solution.py:370
  5.6 0.0 copy-start.3
  5.6 0.0 copy-start.4
  5.6 0.0 copy-start.5
  5.6 0.0 copy-start.6
  5.6 0.0 copy-start.7
  5.6 0.0 copy-start.8
  5.7 2.2 %shard_map.113 = (f32[2,256,256]{2,1,0:T(8,128)}, f32[8,128]{1,0:T(8,128)S(1)}) custom-call(f32[2,2,256,256]{3,2,1,0:T(8,128)} %probe.3, bf16[2,256,256]{2,1,0:T(8,128)(2,1)} %bitcast.13), custom_call_target="tpu_custom_call" | custom-call | tf_op jit(solution)/shard_map/pallas_call | solution.py:354
  7.9 3.0 %collective-permute-done.1.halo = f32[2,384,128]{2,1,0:T(8,128)S(1)} collective-permute-done((f32[2,384,128]{2,1,0:T(8,128)S(1)}, f32[2,384,128]{2,1,0:T(8,128)S(1)}, u32[]{:S(2)}, u32[]{:S(2)}) %collective-permute-start.1) | collective-permute-done | bytes 393248 | tf_op jit(solution)/shard_map/ppermute | solution.py:370
  10.9 0.0 copy-start.9
  10.9 0.0 copy-done
  10.9 0.0 copy-done.3
  10.9 0.0 copy-done.4
  10.9 0.0 copy-done.5
  10.9 0.0 copy-done.6
  10.9 0.0 copy-done.7
  10.9 0.0 copy-done.8
  10.9 0.6 copy-done.9
  11.5 5.4 %shard_map.114 = (f32[2,384,256]{2,1,0:T(8,128)S(1)}, f32[2,384,128]{2,1,0:T(8,128)S(1)}, f32[2,320,128]{2,1,0:T(8,128)S(1)}, f32[2,128,128]{2,1,0:T(8,128)S(1)}, f32[2,2,256,256]{3,2,1,0:T(8,128)}) custom-call(s32[2,2]{1,0:T(2,128)S(1)} %bitcast.8, f32[2,384,256]{2,1,0:T(8,128)S(1)} %copy.17.obj, ...), custom_call_target="tpu_custom_call", output_to_operand_aliasing={{0}: (1, {}), {1}: (2, {})} | custom-call | tf_op jit(solution)/shard_map/pallas_call | solution.py:354
  17.0 1.9 %collective-permute-start.2 = (f32[2,384,128]{2,1,0:T(8,128)S(1)}, f32[2,384,128]{2,1,0:T(8,128)S(1)}, u32[]{:S(2)}, u32[]{:S(2)}) collective-permute-start(f32[2,384,128]{2,1,0:T(8,128)S(1)} %get-tuple-element.19.spill), channel_id=1, source_target_pairs={{0,1},{1,2},{2,3},{3,4},{4,5},{5,6},{6,7},{7,8},{8,9},{9,10},{10,1... | collective-permute-start | bytes 1179656 | tf_op jit(solution)/shard_map/ppermute | solution.py:370
  18.9 5.9 %collective-permute-start.3 = (f32[2,320,128]{2,1,0:T(8,128)S(1)}, f32[2,320,128]{2,1,0:T(8,128)S(1)}, u32[]{:S(2)}, u32[]{:S(2)}) collective-permute-start(f32[2,320,128]{2,1,0:T(8,128)S(1)} %get-tuple-element.20.edge), channel_id=1, source_target_pairs={{1,0},{2,1},{3,2},{4,3},{5,4},{6,5},{7,6},{8,7},{9,8},{10,9},{11,1... | collective-permute-start | bytes 983048 | tf_op jit(solution)/shard_map/ppermute | solution.py:370
  24.8 9.1 %collective-permute-start = (s32[2,2]{1,0:T(2,128)S(1)}, s32[2,2]{1,0:T(2,128)S(1)}, u32[]{:S(2)}, u32[]{:S(2)}) collective-permute-start(s32[2,2]{1,0:T(2,128)S(1)} %bitcast.9), channel_id=1, source_target_pairs={{0,32},{32,64},{64,96},{96,128},{128,160},{160,192},{192,224},{224... | collective-permute-start | bytes 56 | tf_op jit(solution)/shard_map/ppermute | solution.py:370
  34.0 0.1 pad_add_fusion.info
  34.0 5.4 %collective-permute-start.4 = (f32[2,128,128]{2,1,0:T(8,128)S(1)}, f32[2,128,128]{2,1,0:T(8,128)S(1)}, u32[]{:S(2)}, u32[]{:S(2)}) collective-permute-start(f32[2,128,128]{2,1,0:T(8,128)S(1)} %get-tuple-element.23), channel_id=1, source_target_pairs={{32,0},{64,32},{96,64},{128,96},{160,128},{192,160},{224,192},{256... | collective-permute-start | bytes 393224 | tf_op jit(solution)/shard_map/ppermute | solution.py:370
  39.5 0.0 collective-permute-done.above
  39.5 0.0 collective-permute-done.3.from_right
  39.5 0.0 collective-permute-done.2.from_left
  39.5 0.6 shard_map.116
  40.1 7.8 %collective-permute-start.5 = (f32[2,128,128]{2,1,0:T(8,128)S(1)}, f32[2,128,128]{2,1,0:T(8,128)S(1)}, u32[]{:S(2)}, u32[]{:S(2)}) collective-permute-start(f32[2,128,128]{2,1,0:T(8,128)S(1)} %shard_map.116), channel_id=1, source_target_pairs={{32,0},{64,32},{96,64},{128,96},{160,128},{192,160},{224,192},{256... | collective-permute-start | bytes 393224 | tf_op jit(solution)/shard_map/ppermute | solution.py:370
  47.9 1.5 shard_map.115
  49.4 6.4 %collective-permute-done.4.below_mid = f32[2,128,128]{2,1,0:T(8,128)S(1)} collective-permute-done((f32[2,128,128]{2,1,0:T(8,128)S(1)}, f32[2,128,128]{2,1,0:T(8,128)S(1)}, u32[]{:S(2)}, u32[]{:S(2)}) %collective-permute-start.4) | collective-permute-done | bytes 131104 | tf_op jit(solution)/shard_map/ppermute | solution.py:370
  55.8 7.0 %collective-permute-done.5.below_rest = f32[2,128,128]{2,1,0:T(8,128)S(1)} collective-permute-done((f32[2,128,128]{2,1,0:T(8,128)S(1)}, f32[2,128,128]{2,1,0:T(8,128)S(1)}, u32[]{:S(2)}, u32[]{:S(2)}) %collective-permute-start.5) | collective-permute-done | bytes 131104 | tf_op jit(solution)/shard_map/ppermute | solution.py:370
  62.8 5.6 %shard_map.117 = (f32[2,256,256]{2,1,0:T(8,128)S(1)}, f32[2,256,256]{2,1,0:T(8,128)S(1)}, f32[2,256,256]{2,1,0:T(8,128)S(1)}) custom-call(s32[2,2]{1,0:T(2,128)S(1)} %bitcast.10, s32[2]{0:T(128)S(1)} %pad_add_fusion.info, f32[2,256,384]{2,1,0:T(8,128)S(1)} %get-tuple-element.22.source, f32[2,128,128]{2,1,0:T(8,128)S(1)} %collective-permute-done.4.below_mid, ...), custom_call_target="tpu_custom_call" | custom-call | tf_op jit(solution)/shard_map/pallas_call | solution.py:354
  68.4 1.9 %collective-permute-start.8 = (f32[2,256,256]{2,1,0:T(8,128)S(1)}, f32[2,256,256]{2,1,0:T(8,128)S(1)}, u32[]{:S(2)}, u32[]{:S(2)}) collective-permute-start(f32[2,256,256]{2,1,0:T(8,128)S(1)} %get-tuple-element.29), channel_id=1, source_target_pairs={{0,1},{1,0},{2,3},{3,2},{4,5},{5,4},{6,7},{7,6},{8,9},{9,8},{10,11... | collective-permute-start | bytes 1572872 | tf_op jit(solution)/shard_map/ppermute | solution.py:378
  70.3 1.9 %collective-permute-done.8 = f32[2,256,256]{2,1,0:T(8,128)S(1)} collective-permute-done((f32[2,256,256]{2,1,0:T(8,128)S(1)}, f32[2,256,256]{2,1,0:T(8,128)S(1)}, u32[]{:S(2)}, u32[]{:S(2)}) %collective-permute-start.8) | collective-permute-done | bytes 524320 | tf_op jit(solution)/shard_map/ppermute | solution.py:378
  72.2 0.1 add.11
  72.3 13.9 %all_to_all.20 = f32[16,32,256]{2,1,0:T(8,128)S(1)} all-to-all(f32[16,32,256]{2,1,0:T(8,128)S(1)} %bitcast.12), channel_id=1, replica_groups=mesh['row_0'=4,'row_1'=4,'col_0'=4,'col_1'=4,'col_2'=2] {'row_0','col_1'}, dimensions={0} | all-to-all | bytes 1048576 | tf_op jit(solution)/shard_map/all_to_all | solution.py:374
  86.2 10.7 %all_to_all.21 = f32[4,32,256]{2,1,0:T(8,128)S(1)} all-to-all(f32[4,32,256]{2,1,0:T(8,128)S(1)} %broadcast_in_dim.9), channel_id=1, replica_groups=mesh['row_0'=4,'row_1'=4,'col_0'=4,'col_1'=4,'col_2'=2] {'col_0'}, dimensions={0} | all-to-all | bytes 262144 | tf_op jit(solution)/shard_map/all_to_all | solution.py:374
  97.0 21.8 %all_to_all.22 = f32[4,32,256]{2,1,0:T(8,128)S(1)} all-to-all(f32[4,32,256]{2,1,0:T(8,128)S(1)} %broadcast_in_dim.10), channel_id=1, replica_groups=mesh['row_0'=4,'row_1'=4,'col_0'=4,'col_1'=4,'col_2'=2] {'row_1'}, dimensions={0} | all-to-all | bytes 262144 | tf_op jit(solution)/shard_map/all_to_all | solution.py:374
  118.8 0.8 broadcast_in_dim.11
  119.7 6.1 %all-to-all-start.3 = ((f32[16,32,256]{2,1,0:T(8,128)}), f32[16,32,256]{2,1,0:T(8,128)S(1)}, u32[]{:S(2)}, u32[]{:S(2)}) async-start(f32[16,32,256]{2,1,0:T(8,128)} %broadcast_in_dim.11), calls=%async_computation.3 | async-start | bytes 1048576 | tf_op jit(solution)/shard_map/all_to_all | solution.py:374
  125.8 0.9 shard_map.118
  126.7 0.0 copy-start.2
  126.7 3.1 %collective-permute-start.6 = (f32[2,128,256]{2,1,0:T(8,128)S(1)}, f32[2,128,256]{2,1,0:T(8,128)S(1)}, u32[]{:S(2)}, u32[]{:S(2)}) collective-permute-start(f32[2,128,256]{2,1,0:T(8,128)S(1)} %get-tuple-element.27), channel_id=1, source_target_pairs={{0,32},{32,64},{64,96},{96,128},{128,160},{160,192},{192,224},{224... | collective-permute-start | bytes 786440 | tf_op jit(solution)/shard_map/ppermute | solution.py:370
  129.8 3.5 %all-to-all-done.3 = f32[16,32,256]{2,1,0:T(8,128)S(1)} async-done(((f32[16,32,256]{2,1,0:T(8,128)}), f32[16,32,256]{2,1,0:T(8,128)S(1)}, u32[]{:S(2)}, u32[]{:S(2)}) %all-to-all-start.3) | async-done | bytes 524320 | tf_op jit(solution)/shard_map/all_to_all | solution.py:374
  133.3 1.9 %collective-permute-start.9 = (f32[2,256,256]{2,1,0:T(8,128)S(1)}, f32[2,256,256]{2,1,0:T(8,128)S(1)}, u32[]{:S(2)}, u32[]{:S(2)}) collective-permute-start(f32[2,256,256]{2,1,0:T(8,128)S(1)} %bitcast.6), channel_id=1, source_target_pairs={{0,1},{1,0},{2,3},{3,2},{4,5},{5,4},{6,7},{7,6},{8,9},{9,8},{10,11... | collective-permute-start | bytes 1572872 | tf_op jit(solution)/shard_map/ppermute | solution.py:378
  135.2 18.1 %collective-permute-done.6.from_above = f32[2,128,256]{2,1,0:T(8,128)S(1)} collective-permute-done((f32[2,128,256]{2,1,0:T(8,128)S(1)}, f32[2,128,256]{2,1,0:T(8,128)S(1)}, u32[]{:S(2)}, u32[]{:S(2)}) %collective-permute-start.6) | collective-permute-done | bytes 262176 | tf_op jit(solution)/shard_map/ppermute | solution.py:370
  153.4 0.6 shard_map.119
  154.0 1.9 %collective-permute-start.7 = (f32[2,384,128]{2,1,0:T(8,128)S(1)}, f32[2,384,128]{2,1,0:T(8,128)S(1)}, u32[]{:S(2)}, u32[]{:S(2)}) collective-permute-start(f32[2,384,128]{2,1,0:T(8,128)S(1)} %shard_map.119), channel_id=1, source_target_pairs={{0,1},{1,2},{2,3},{3,4},{4,5},{5,6},{6,7},{7,8},{8,9},{9,10},{10,1... | collective-permute-start | bytes 1179656 | tf_op jit(solution)/shard_map/ppermute | solution.py:370
  155.9 9.3 %collective-permute-done.7.from_left = f32[2,384,128]{2,1,0:T(8,128)S(1)} collective-permute-done((f32[2,384,128]{2,1,0:T(8,128)S(1)}, f32[2,384,128]{2,1,0:T(8,128)S(1)}, u32[]{:S(2)}, u32[]{:S(2)}) %collective-permute-start.7) | collective-permute-done | bytes 393248 | tf_op jit(solution)/shard_map/ppermute | solution.py:370
  165.2 0.0 copy-done.2
  165.2 0.0 copy-start.1
  165.2 1.5 shard_map.120
  166.7 0.0 collective-permute-done.9.other
  166.7 0.0 copy-done.1
  166.7 1.6 shard_map.121
  (7 shorter events, 0.1 us)
Async XLA Ops:
  1.8 9.1 %copy-start = (f32[2,2,256,256]{3,2,1,0:T(8,128)S(1)}, f32[2,2,256,256]{3,2,1,0:T(8,128)}, u32[]{:S(2)}) copy-start(f32[2,2,256,256]{3,2,1,0:T(8,128)} %probe.3) | copy-start | bytes 3145732
  1.8 9.1 %collective-permute-start.1 = (f32[2,384,128]{2,1,0:T(8,128)S(1)}, f32[2,384,128]{2,1,0:T(8,128)S(1)}, u32[]{:S(2)}, u32[]{:S(2)}) collective-permute-start(f32[2,384,128]{2,1,0:T(8,128)S(1)} %slice.3), channel_id=1, source_target_pairs={{1,0},{2,1},{3,2},{4,3},{5,4},{6,5},{7,6},{8,7},{9,8},{10,9},{11,1... | collective-permute-start | bytes 1179656 | tf_op jit(solution)/shard_map/ppermute | solution.py:370
  5.6 5.3 %copy-start.3 = (f32[2,128,128]{2,1,0:T(8,128)S(1)}, f32[2,128,128]{2,1,0:T(8,128)}, u32[]{:S(2)}) copy-start(f32[2,128,128]{2,1,0:T(8,128)} %constant.38.clone.rows) | copy-start | bytes 393220
  5.6 5.3 %copy-start.4 = (bf16[256,256]{1,0:T(8,128)(2,1)S(1)}, bf16[256,256]{1,0:T(8,128)(2,1)}, u32[]{:S(2)}) copy-start(bf16[256,256]{1,0:T(8,128)(2,1)} %constant.37.clone.low_t) | copy-start | bytes 393220
  5.6 5.3 %copy-start.5 = (bf16[256,256]{1,0:T(8,128)(2,1)S(1)}, bf16[256,256]{1,0:T(8,128)(2,1)}, u32[]{:S(2)}) copy-start(bf16[256,256]{1,0:T(8,128)(2,1)} %constant.36.clone.high_t) | copy-start | bytes 393220
  5.6 5.3 %copy-start.6 = (bf16[256,256]{1,0:T(8,128)(2,1)S(1)}, bf16[256,256]{1,0:T(8,128)(2,1)}, u32[]{:S(2)}) copy-start(bf16[256,256]{1,0:T(8,128)(2,1)} %constant.35.clone.low) | copy-start | bytes 393220
  5.6 5.3 %copy-start.7 = (bf16[256,256]{1,0:T(8,128)(2,1)S(1)}, bf16[256,256]{1,0:T(8,128)(2,1)}, u32[]{:S(2)}) copy-start(bf16[256,256]{1,0:T(8,128)(2,1)} %constant.34.clone.high) | copy-start | bytes 393220
  5.6 5.3 %copy-start.8 = (f32[2,8,128]{2,1,0:T(8,128)S(1)}, f32[2,8,128]{2,1,0:T(8,128)}, u32[]{:S(2)}) copy-start(f32[2,8,128]{2,1,0:T(8,128)} %constant.39.clone.cols) | copy-start | bytes 24580
  10.9 0.7 copy-start.9
  17.0 22.5 %collective-permute-start.2 = (f32[2,384,128]{2,1,0:T(8,128)S(1)}, f32[2,384,128]{2,1,0:T(8,128)S(1)}, u32[]{:S(2)}, u32[]{:S(2)}) collective-permute-start(f32[2,384,128]{2,1,0:T(8,128)S(1)} %get-tuple-element.19.spill), channel_id=1, source_target_pairs={{0,1},{1,2},{2,3},{3,4},{4,5},{5,6},{6,7},{7,8},{8,9},{9,10},{10,1... | collective-permute-start | bytes 1179656 | tf_op jit(solution)/shard_map/ppermute | solution.py:370
  18.9 20.6 %collective-permute-start.3 = (f32[2,320,128]{2,1,0:T(8,128)S(1)}, f32[2,320,128]{2,1,0:T(8,128)S(1)}, u32[]{:S(2)}, u32[]{:S(2)}) collective-permute-start(f32[2,320,128]{2,1,0:T(8,128)S(1)} %get-tuple-element.20.edge), channel_id=1, source_target_pairs={{1,0},{2,1},{3,2},{4,3},{5,4},{6,5},{7,6},{8,7},{9,8},{10,9},{11,1... | collective-permute-start | bytes 983048 | tf_op jit(solution)/shard_map/ppermute | solution.py:370
  24.8 14.6 %collective-permute-start = (s32[2,2]{1,0:T(2,128)S(1)}, s32[2,2]{1,0:T(2,128)S(1)}, u32[]{:S(2)}, u32[]{:S(2)}) collective-permute-start(s32[2,2]{1,0:T(2,128)S(1)} %bitcast.9), channel_id=1, source_target_pairs={{0,32},{32,64},{64,96},{96,128},{128,160},{160,192},{192,224},{224... | collective-permute-start | bytes 56 | tf_op jit(solution)/shard_map/ppermute | solution.py:370
  34.0 21.8 %collective-permute-start.4 = (f32[2,128,128]{2,1,0:T(8,128)S(1)}, f32[2,128,128]{2,1,0:T(8,128)S(1)}, u32[]{:S(2)}, u32[]{:S(2)}) collective-permute-start(f32[2,128,128]{2,1,0:T(8,128)S(1)} %get-tuple-element.23), channel_id=1, source_target_pairs={{32,0},{64,32},{96,64},{128,96},{160,128},{192,160},{224,192},{256... | collective-permute-start | bytes 393224 | tf_op jit(solution)/shard_map/ppermute | solution.py:370
  40.1 22.7 %collective-permute-start.5 = (f32[2,128,128]{2,1,0:T(8,128)S(1)}, f32[2,128,128]{2,1,0:T(8,128)S(1)}, u32[]{:S(2)}, u32[]{:S(2)}) collective-permute-start(f32[2,128,128]{2,1,0:T(8,128)S(1)} %shard_map.116), channel_id=1, source_target_pairs={{32,0},{64,32},{96,64},{128,96},{160,128},{192,160},{224,192},{256... | collective-permute-start | bytes 393224 | tf_op jit(solution)/shard_map/ppermute | solution.py:370
  68.4 3.8 %collective-permute-start.8 = (f32[2,256,256]{2,1,0:T(8,128)S(1)}, f32[2,256,256]{2,1,0:T(8,128)S(1)}, u32[]{:S(2)}, u32[]{:S(2)}) collective-permute-start(f32[2,256,256]{2,1,0:T(8,128)S(1)} %get-tuple-element.29), channel_id=1, source_target_pairs={{0,1},{1,0},{2,3},{3,2},{4,5},{5,4},{6,7},{7,6},{8,9},{9,8},{10,11... | collective-permute-start | bytes 1572872 | tf_op jit(solution)/shard_map/ppermute | solution.py:378
  119.7 13.6 %all-to-all-start.3 = ((f32[16,32,256]{2,1,0:T(8,128)}), f32[16,32,256]{2,1,0:T(8,128)S(1)}, u32[]{:S(2)}, u32[]{:S(2)}) async-start(f32[16,32,256]{2,1,0:T(8,128)} %broadcast_in_dim.11), calls=%async_computation.3 | async-start | bytes 1048576 | tf_op jit(solution)/shard_map/all_to_all | solution.py:374
  126.7 38.5 %copy-start.2 = (f32[2,384,256]{2,1,0:T(8,128)S(1)}, f32[2,384,256]{2,1,0:T(8,128)}, u32[]{:S(2)}) copy-start(f32[2,384,256]{2,1,0:T(8,128)} %get-tuple-element.21.whole) | copy-start | bytes 2359300
  126.7 26.7 %collective-permute-start.6 = (f32[2,128,256]{2,1,0:T(8,128)S(1)}, f32[2,128,256]{2,1,0:T(8,128)S(1)}, u32[]{:S(2)}, u32[]{:S(2)}) collective-permute-start(f32[2,128,256]{2,1,0:T(8,128)S(1)} %get-tuple-element.27), channel_id=1, source_target_pairs={{0,32},{32,64},{64,96},{96,128},{128,160},{160,192},{192,224},{224... | collective-permute-start | bytes 786440 | tf_op jit(solution)/shard_map/ppermute | solution.py:370
  133.3 33.4 %collective-permute-start.9 = (f32[2,256,256]{2,1,0:T(8,128)S(1)}, f32[2,256,256]{2,1,0:T(8,128)S(1)}, u32[]{:S(2)}, u32[]{:S(2)}) collective-permute-start(f32[2,256,256]{2,1,0:T(8,128)S(1)} %bitcast.6), channel_id=1, source_target_pairs={{0,1},{1,0},{2,3},{3,2},{4,5},{5,4},{6,7},{7,6},{8,9},{9,8},{10,11... | collective-permute-start | bytes 1572872 | tf_op jit(solution)/shard_map/ppermute | solution.py:378
  154.0 11.2 %collective-permute-start.7 = (f32[2,384,128]{2,1,0:T(8,128)S(1)}, f32[2,384,128]{2,1,0:T(8,128)S(1)}, u32[]{:S(2)}, u32[]{:S(2)}) collective-permute-start(f32[2,384,128]{2,1,0:T(8,128)S(1)} %shard_map.119), channel_id=1, source_target_pairs={{0,1},{1,2},{2,3},{3,4},{4,5},{5,6},{6,7},{7,8},{8,9},{9,10},{10,1... | collective-permute-start | bytes 1179656 | tf_op jit(solution)/shard_map/ppermute | solution.py:370
  165.2 1.6 copy-start.1

commit v8 on v7

--- a/solution.py
+++ b/solution.py
@@ -144,7 +144,14 @@
     lax.fori_loop(0, 2, inward, 0)
 
 
-def before_kernel(probe_hbm, amp_hbm, amp_out, step_out, probe, amp, ordered, sems):
+def before_kernel_of(rows_of_share):
+    def kernel(*refs):
+        before_kernel(rows_of_share, *refs)
+
+    return kernel
+
+
+def before_kernel(size, info, probe_hbm, amp_hbm, amp_out, step_out, share, probe, amp, ordered, sems):
     amp_copy = pltpu.make_async_copy(amp_hbm, amp, sems.at[0])
     probe_copy = pltpu.make_async_copy(probe_hbm, probe, sems.at[1])
     out_copy = lambda b: pltpu.make_async_copy(ordered.at[b], amp_out.at[b], sems.at[2 + b])
@@ -166,6 +173,9 @@
             square = probe[m, k] * probe[m, k]
             square = jnp.sum(square.reshape(WIN // 8, 8, WIN), axis=0)
             total = total + square[:, :HALF] + square[:, HALF:]
+    per_part = WIN // size
+    start = pl.multiple_of(lax.rem(info[2], per_part) * size, size)
+    share[...] = probe[info[1], info[2] // per_part, pl.ds(start, size), :]
     power = jnp.sum(total) / (WIN * WIN)
     step_out[...] = jnp.full((8, HALF), 1.0, jnp.float32) / (power + 1e-06)
     for b in range(BATCHES):
@@ -316,19 +326,24 @@
         new_spill[k, HALO:] = own_grad[k, :, WIN:]
 
 
-def object_kernel(above, whole, own_grad, from_above, from_left, out):
+def last_kernel(above, info, whole, own_grad, from_above, from_left, own, other, object_hbm, probe_hbm, out, sems):
+    core = info[1]
+    own_copy = pltpu.make_async_copy(own, probe_hbm.at[core], sems.at[0])
+    other_copy = pltpu.make_async_copy(other, probe_hbm.at[1 - core], sems.at[1])
+    object_copy = lambda k: pltpu.make_async_copy(out.at[k], object_hbm.at[k], sems.at[2 + k])
+    own_copy.start()
+    other_copy.start()
     for k in range(2):
         fell = jnp.where(lanes() >= above[1, 1], from_above[k, :, :HALO], 0.0)
         out[k, :LAST, :HALO] = whole[k, :LAST, :HALO] + fell + from_left[k, :LAST]
         out[k, :LAST, HALO:] = whole[k, :LAST, HALO:] + from_above[k, :, HALO:]
         out[k, LAST:, :HALO] = whole[k, LAST:, :HALO] + own_grad[k, :, :HALO] + from_left[k, LAST:]
         out[k, LAST:, HALO:] = whole[k, LAST:, HALO:] + own_grad[k, :, HALO:WIN]
-
-
-def probe_kernel(info, probe, own, other, out):
-    core = info[1]
-    out[core] = probe[core] + own[...]
-    out[1 - core] = probe[1 - core] + other[...]
+        object_copy(k).start()
+    own_copy.wait()
+    other_copy.wait()
+    for k in range(2):
+        object_copy(k).wait()
 
 
 HBM = object()
@@ -378,7 +393,7 @@
     return lax.ppermute(block, CORE, [(0, 1), (1, 0)])
 
 
-def summed_everywhere(keep, send, divisor):
+def new_modes(keep, send, old_share, divisor):
     plane = lax.axis_size(PLANE)
     mode = keep + swapped(send)
     parts = exchanged(mode.reshape(plane, -1, WIN), PLANE)
@@ -386,7 +401,7 @@
     for axis in ("col_0", "row_1"):
         parts = exchanged(jnp.broadcast_to(share, (lax.axis_size(axis), *share.shape)), axis)
         share = jnp.sum(parts, axis=0)
-    share = share / divisor
+    share = old_share + share / divisor
     mode = exchanged(jnp.broadcast_to(share, (plane, *share.shape)), PLANE).reshape(2, WIN, WIN)
     return mode, swapped(mode)
 
@@ -403,11 +418,12 @@
 
     halo = passed_along(object_field[:, :, :HALO], COL, -1)
     above = passed_along(positions, ROW, 1)
-    info = jnp.stack([has_right, lax.axis_index(CORE)])
-    amp, step = call(
-        before_kernel, [((BATCHES, WIN, WIN), HBM), (8, HALF)],
+    info = jnp.stack([has_right, lax.axis_index(CORE), lax.axis_index(PLANE)])
+    rows = 2 * WIN // lax.axis_size(PLANE)
+    amp, step, old_share = call(
+        before_kernel_of(rows), [((BATCHES, WIN, WIN), HBM), (8, HALF), (rows, WIN)],
         [probe_shape, pltpu.VMEM((BATCHES, WIN, WIN), jnp.bfloat16), (BATCHES, WIN, WIN)],
-        [], [(probe_modes, HBM), (amplitudes[0, 0], HBM)], copies=4)
+        [info], [(probe_modes, HBM), (amplitudes[0, 0], HBM)], copies=4)
     obj, spill, edge, middle, probe_sum = call(
         first_kernel, [tile, side, (2, TILE_R - LOW + HALO, HALO), block, (probe_shape, HBM)], fit_scratch, [positions],
         [object_field, halo, probe_modes, (amp, HBM), step, *tables], copies=5, in_place={1: 0, 2: 1})
@@ -424,13 +440,13 @@
         [source, below_mid, below_rest, (probe_modes, HBM), (amp, HBM), (probe_sum, HBM), *tables], copies=5)
     grad, downward = call(
         place_kernel, [(2, WIN, WIDE), (2, HALO, WIN)], [(2, TILE_R + 8, WIN)], [positions], [grad, step])
-    own, other = summed_everywhere(keep, send, divisor)
+    own, other = new_modes(keep, send, old_share, divisor)
     from_above = passed_along(downward, ROW, 1)
     (spill,) = call(spill_kernel, [side], [], [above], [grad, from_above])
     from_left = passed_along(spill, COL, 1)
-    (object_out,) = call(
-        object_kernel, [(tile, AUTO)], [], [above], [(whole, AUTO), (grad, AUTO), (from_above, AUTO), (from_left, AUTO)])
-    (probe_out,) = call(probe_kernel, [(probe_shape, AUTO)], [], [info], [(probe_modes, AUTO), own, other])
+    object_out, probe_out = call(
+        last_kernel, [(tile, HBM), (probe_shape, HBM)], [tile], [above, info],
+        [(whole, AUTO), grad, from_above, from_left, own, other], copies=4)
     return (object_out, probe_out)
 
 

time: 169 us -> 168 us (level)
    pallas_call x9 -> x8, Pallas kernels: 20 us -> 19.1 us  [call(): pl.pallas_call(kernel, out_shape=shapes, in_specs=[smem] * len(scalars) +...]
where the time goes in v8:
time: 168 us; the launch traced here: 167 us
  starting transfers between devices  48.9 us (29%)
  waiting for transfers between devices  48.7 us (29%)
  blocking collectives  46.5 us (28%)
  Pallas kernels  19.1 us (11%)
  local copies, waits for them, and re-layouts  2.69 us (2%)
    all_to_all x3, blocking collectives, exchanged(): return lax.all_to_all(parts, axes, 0, 0, tiled=False)  46.5 us
    ppermute x8, waiting for transfers between devices, passed_along(): return lax.ppermute(block, axis, route)  43.3 us
    ppermute x8, starting transfers between devices, passed_along(): return lax.ppermute(block, axis, route)  39 us
    pallas_call x8, Pallas kernels, call(): pl.pallas_call(kernel, out_shape=shapes, in_specs=[smem] * len(scalars) +...  19.1 us
    all_to_all x1, starting transfers between devices, exchanged(): return lax.all_to_all(parts, axes, 0, 0, tiled=False)  6.09 us
    ppermute x2, starting transfers between devices, swapped(): return lax.ppermute(block, CORE, [(0, 1), (1, 0)])  3.83 us
    all_to_all x1, waiting for transfers between devices, exchanged(): return lax.all_to_all(parts, axes, 0, 0, tiled=False)  3.48 us
  transfers between devices with their start and end apart: 11, of which 7 were waited for; matrix products, arithmetic and copies ran while one was open for 0% of the time, Pallas kernels for 4%

profile of v8, /device:TPU:48, one launch (start us, length us, event | category | flops | bytes accessed | tf_op | source)
XLA Modules:
  0.0 167.1 jit_solution(5302406521772377452)
XLA Ops:
  0.6 1.1 copy.17.obj
  1.8 0.0 copy-start
  1.8 3.8 %collective-permute-start.1 = (f32[2,384,128]{2,1,0:T(8,128)S(1)}, f32[2,384,128]{2,1,0:T(8,128)S(1)}, u32[]{:S(2)}, u32[]{:S(2)}) collective-permute-start(f32[2,384,128]{2,1,0:T(8,128)S(1)} %slice.3), channel_id=1, source_target_pairs={{1,0},{2,1},{3,2},{4,3},{5,4},{6,5},{7,6},{8,7},{9,8},{10,9},{11,1... | collective-permute-start | bytes 1179656 | tf_op jit(solution)/shard_map/ppermute | solution.py:385
  5.6 0.1 pad_add_fusion.refs_0_.info
  5.7 0.0 copy-start.2
  5.7 0.0 copy-start.3
  5.7 0.0 copy-start.4
  5.7 0.0 copy-start.5
  5.7 0.0 copy-start.6
  5.7 0.0 copy-start.7
  5.7 2.7 %shard_map.113 = (f32[2,256,256]{2,1,0:T(8,128)}, f32[8,128]{1,0:T(8,128)S(1)}, f32[32,256]{1,0:T(8,128)S(1)}) custom-call(s32[3]{0:T(128)S(1)} %pad_add_fusion.refs_0_.info, f32[2,2,256,256]{3,2,1,0:T(8,128)} %probe_hbm.1, bf16[2,256,256]{2,1,0:T(8,128)(2,1)} %bitcast.14), custom_call_target="tpu_custom_call" | custom-call | tf_op jit(solution)/shard_map/pallas_call | solution.py:369
  8.4 2.5 %collective-permute-done.1.halo = f32[2,384,128]{2,1,0:T(8,128)S(1)} collective-permute-done((f32[2,384,128]{2,1,0:T(8,128)S(1)}, f32[2,384,128]{2,1,0:T(8,128)S(1)}, u32[]{:S(2)}, u32[]{:S(2)}) %collective-permute-start.1) | collective-permute-done | bytes 393248 | tf_op jit(solution)/shard_map/ppermute | solution.py:385
  10.9 0.0 copy-start.8
  10.9 0.0 copy-done
  10.9 0.0 copy-done.2
  10.9 0.0 copy-done.3
  10.9 0.0 copy-done.4
  10.9 0.0 copy-done.5
  10.9 0.0 copy-done.6
  10.9 0.0 copy-done.7
  10.9 0.6 copy-done.8
  11.5 5.5 %shard_map.114 = (f32[2,384,256]{2,1,0:T(8,128)S(1)}, f32[2,384,128]{2,1,0:T(8,128)S(1)}, f32[2,320,128]{2,1,0:T(8,128)S(1)}, f32[2,128,128]{2,1,0:T(8,128)S(1)}, f32[2,2,256,256]{3,2,1,0:T(8,128)}) custom-call(s32[2,2]{1,0:T(2,128)S(1)} %bitcast.9, f32[2,384,256]{2,1,0:T(8,128)S(1)} %copy.17.obj, ...), custom_call_target="tpu_custom_call", output_to_operand_aliasing={{0}: (1, {}), {1}: (2, {})} | custom-call | tf_op jit(solution)/shard_map/pallas_call | solution.py:369
  17.0 2.0 %collective-permute-start.2 = (f32[2,384,128]{2,1,0:T(8,128)S(1)}, f32[2,384,128]{2,1,0:T(8,128)S(1)}, u32[]{:S(2)}, u32[]{:S(2)}) collective-permute-start(f32[2,384,128]{2,1,0:T(8,128)S(1)} %get-tuple-element.20.spill), channel_id=1, source_target_pairs={{0,1},{1,2},{2,3},{3,4},{4,5},{5,6},{6,7},{7,8},{8,9},{9,10},{10,1... | collective-permute-start | bytes 1179656 | tf_op jit(solution)/shard_map/ppermute | solution.py:385
  19.0 5.9 %collective-permute-start.3 = (f32[2,320,128]{2,1,0:T(8,128)S(1)}, f32[2,320,128]{2,1,0:T(8,128)S(1)}, u32[]{:S(2)}, u32[]{:S(2)}) collective-permute-start(f32[2,320,128]{2,1,0:T(8,128)S(1)} %get-tuple-element.21.edge), channel_id=1, source_target_pairs={{1,0},{2,1},{3,2},{4,3},{5,4},{6,5},{7,6},{8,7},{9,8},{10,9},{11,1... | collective-permute-start | bytes 983048 | tf_op jit(solution)/shard_map/ppermute | solution.py:385
  24.9 9.1 %collective-permute-start = (s32[2,2]{1,0:T(2,128)S(1)}, s32[2,2]{1,0:T(2,128)S(1)}, u32[]{:S(2)}, u32[]{:S(2)}) collective-permute-start(s32[2,2]{1,0:T(2,128)S(1)} %bitcast.10), channel_id=1, source_target_pairs={{0,32},{32,64},{64,96},{96,128},{128,160},{160,192},{192,224},{224... | collective-permute-start | bytes 56 | tf_op jit(solution)/shard_map/ppermute | solution.py:385
  34.0 5.4 %collective-permute-start.4 = (f32[2,128,128]{2,1,0:T(8,128)S(1)}, f32[2,128,128]{2,1,0:T(8,128)S(1)}, u32[]{:S(2)}, u32[]{:S(2)}) collective-permute-start(f32[2,128,128]{2,1,0:T(8,128)S(1)} %get-tuple-element.24), channel_id=1, source_target_pairs={{32,0},{64,32},{96,64},{128,96},{160,128},{192,160},{224,192},{256... | collective-permute-start | bytes 393224 | tf_op jit(solution)/shard_map/ppermute | solution.py:385
  39.4 0.0 collective-permute-done.above
  39.4 0.0 collective-permute-done.3.from_right
  39.4 0.0 collective-permute-done.2.from_left
  39.5 0.6 shard_map.116
  40.1 7.8 %collective-permute-start.5 = (f32[2,128,128]{2,1,0:T(8,128)S(1)}, f32[2,128,128]{2,1,0:T(8,128)S(1)}, u32[]{:S(2)}, u32[]{:S(2)}) collective-permute-start(f32[2,128,128]{2,1,0:T(8,128)S(1)} %shard_map.116), channel_id=1, source_target_pairs={{32,0},{64,32},{96,64},{128,96},{160,128},{192,160},{224,192},{256... | collective-permute-start | bytes 393224 | tf_op jit(solution)/shard_map/ppermute | solution.py:385
  47.9 1.5 shard_map.115
  49.4 7.9 %collective-permute-done.4.below_mid = f32[2,128,128]{2,1,0:T(8,128)S(1)} collective-permute-done((f32[2,128,128]{2,1,0:T(8,128)S(1)}, f32[2,128,128]{2,1,0:T(8,128)S(1)}, u32[]{:S(2)}, u32[]{:S(2)}) %collective-permute-start.4) | collective-permute-done | bytes 131104 | tf_op jit(solution)/shard_map/ppermute | solution.py:385
  57.2 5.5 %collective-permute-done.5.below_rest = f32[2,128,128]{2,1,0:T(8,128)S(1)} collective-permute-done((f32[2,128,128]{2,1,0:T(8,128)S(1)}, f32[2,128,128]{2,1,0:T(8,128)S(1)}, u32[]{:S(2)}, u32[]{:S(2)}) %collective-permute-start.5) | collective-permute-done | bytes 131104 | tf_op jit(solution)/shard_map/ppermute | solution.py:385
  62.8 5.6 %shard_map.117 = (f32[2,256,256]{2,1,0:T(8,128)S(1)}, f32[2,256,256]{2,1,0:T(8,128)S(1)}, f32[2,256,256]{2,1,0:T(8,128)S(1)}) custom-call(s32[2,2]{1,0:T(2,128)S(1)} %bitcast.11, s32[3]{0:T(128)S(1)} %pad_add_fusion.refs_0_.info, f32[2,256,384]{2,1,0:T(8,128)S(1)} %get-tuple-element.23.source, f32[2,128,128]{2,1,0:T(8,128)S(1)} %collective-permute-done.4.below_mid, ...), custom_call_target="tpu_custom_call" | custom-call | tf_op jit(solution)/shard_map/pallas_call | solution.py:369
  68.4 1.9 %collective-permute-start.8 = (f32[2,256,256]{2,1,0:T(8,128)S(1)}, f32[2,256,256]{2,1,0:T(8,128)S(1)}, u32[]{:S(2)}, u32[]{:S(2)}) collective-permute-start(f32[2,256,256]{2,1,0:T(8,128)S(1)} %get-tuple-element.31), channel_id=1, source_target_pairs={{0,1},{1,0},{2,3},{3,2},{4,5},{5,4},{6,7},{7,6},{8,9},{9,8},{10,11... | collective-permute-start | bytes 1572872 | tf_op jit(solution)/shard_map/ppermute | solution.py:393
  70.3 1.9 %collective-permute-done.8 = f32[2,256,256]{2,1,0:T(8,128)S(1)} collective-permute-done((f32[2,256,256]{2,1,0:T(8,128)S(1)}, f32[2,256,256]{2,1,0:T(8,128)S(1)}, u32[]{:S(2)}, u32[]{:S(2)}) %collective-permute-start.8) | collective-permute-done | bytes 524320 | tf_op jit(solution)/shard_map/ppermute | solution.py:393
  72.2 0.1 add.18
  72.3 13.9 %all_to_all.20 = f32[16,32,256]{2,1,0:T(8,128)S(1)} all-to-all(f32[16,32,256]{2,1,0:T(8,128)S(1)} %bitcast.13), channel_id=1, replica_groups=mesh['row_0'=4,'row_1'=4,'col_0'=4,'col_1'=4,'col_2'=2] {'row_0','col_1'}, dimensions={0} | all-to-all | bytes 1048576 | tf_op jit(solution)/shard_map/all_to_all | solution.py:389
  86.2 10.7 %all_to_all.21 = f32[4,32,256]{2,1,0:T(8,128)S(1)} all-to-all(f32[4,32,256]{2,1,0:T(8,128)S(1)} %broadcast_in_dim.9), channel_id=1, replica_groups=mesh['row_0'=4,'row_1'=4,'col_0'=4,'col_1'=4,'col_2'=2] {'col_0'}, dimensions={0} | all-to-all | bytes 262144 | tf_op jit(solution)/shard_map/all_to_all | solution.py:389
  97.0 22.0 %all_to_all.22 = f32[4,32,256]{2,1,0:T(8,128)S(1)} all-to-all(f32[4,32,256]{2,1,0:T(8,128)S(1)} %broadcast_in_dim.10), channel_id=1, replica_groups=mesh['row_0'=4,'row_1'=4,'col_0'=4,'col_1'=4,'col_2'=2] {'row_1'}, dimensions={0} | all-to-all | bytes 262144 | tf_op jit(solution)/shard_map/all_to_all | solution.py:389
  118.9 0.8 broadcast_in_dim.11
  119.8 6.1 %all-to-all-start.3 = ((f32[16,32,256]{2,1,0:T(8,128)}), f32[16,32,256]{2,1,0:T(8,128)S(1)}, u32[]{:S(2)}, u32[]{:S(2)}) async-start(f32[16,32,256]{2,1,0:T(8,128)} %broadcast_in_dim.11), calls=%async_computation.3 | async-start | bytes 1048576 | tf_op jit(solution)/shard_map/all_to_all | solution.py:389
  125.9 0.9 shard_map.118
  126.8 0.0 copy-start.1
  126.8 3.1 %collective-permute-start.6 = (f32[2,128,256]{2,1,0:T(8,128)S(1)}, f32[2,128,256]{2,1,0:T(8,128)S(1)}, u32[]{:S(2)}, u32[]{:S(2)}) collective-permute-start(f32[2,128,256]{2,1,0:T(8,128)S(1)} %get-tuple-element.28), channel_id=1, source_target_pairs={{0,32},{32,64},{64,96},{96,128},{128,160},{160,192},{192,224},{224... | collective-permute-start | bytes 786440 | tf_op jit(solution)/shard_map/ppermute | solution.py:385
  129.9 3.5 %all-to-all-done.3 = f32[16,32,256]{2,1,0:T(8,128)S(1)} async-done(((f32[16,32,256]{2,1,0:T(8,128)}), f32[16,32,256]{2,1,0:T(8,128)S(1)}, u32[]{:S(2)}, u32[]{:S(2)}) %all-to-all-start.3) | async-done | bytes 524320 | tf_op jit(solution)/shard_map/all_to_all | solution.py:389
  133.4 1.9 %collective-permute-start.9 = (f32[2,256,256]{2,1,0:T(8,128)S(1)}, f32[2,256,256]{2,1,0:T(8,128)S(1)}, u32[]{:S(2)}, u32[]{:S(2)}) collective-permute-start(f32[2,256,256]{2,1,0:T(8,128)S(1)} %bitcast.7), channel_id=1, source_target_pairs={{0,1},{1,0},{2,3},{3,2},{4,5},{5,4},{6,7},{7,6},{8,9},{9,8},{10,11... | collective-permute-start | bytes 1572872 | tf_op jit(solution)/shard_map/ppermute | solution.py:393
  135.3 18.1 %collective-permute-done.6.from_above = f32[2,128,256]{2,1,0:T(8,128)S(1)} collective-permute-done((f32[2,128,256]{2,1,0:T(8,128)S(1)}, f32[2,128,256]{2,1,0:T(8,128)S(1)}, u32[]{:S(2)}, u32[]{:S(2)}) %collective-permute-start.6) | collective-permute-done | bytes 262176 | tf_op jit(solution)/shard_map/ppermute | solution.py:385
  153.5 0.6 shard_map.119
  154.1 1.9 %collective-permute-start.7 = (f32[2,384,128]{2,1,0:T(8,128)S(1)}, f32[2,384,128]{2,1,0:T(8,128)S(1)}, u32[]{:S(2)}, u32[]{:S(2)}) collective-permute-start(f32[2,384,128]{2,1,0:T(8,128)S(1)} %shard_map.119), channel_id=1, source_target_pairs={{0,1},{1,2},{2,3},{3,4},{4,5},{5,6},{6,7},{7,8},{8,9},{9,10},{10,1... | collective-permute-start | bytes 1179656 | tf_op jit(solution)/shard_map/ppermute | solution.py:385
  156.0 9.3 %collective-permute-done.7.from_left = f32[2,384,128]{2,1,0:T(8,128)S(1)} collective-permute-done((f32[2,384,128]{2,1,0:T(8,128)S(1)}, f32[2,384,128]{2,1,0:T(8,128)S(1)}, u32[]{:S(2)}, u32[]{:S(2)}) %collective-permute-start.7) | collective-permute-done | bytes 393248 | tf_op jit(solution)/shard_map/ppermute | solution.py:385
  165.3 0.0 collective-permute-done.9.other
  165.3 0.0 copy-done.1
  165.3 1.8 %shard_map.120 = (f32[2,384,256]{2,1,0:T(8,128)}, f32[2,2,256,256]{3,2,1,0:T(8,128)}) custom-call(s32[2,2]{1,0:T(2,128)S(1)} %collective-permute-done.above, s32[3]{0:T(128)S(1)} %pad_add_fusion.refs_0_.info, f32[2,384,256]{2,1,0:T(8,128)S(1)} %copy-done.1, f32[2,256,384]{2,1,0:T(8,128)S(1)} %get-tuple-element.27.own_grad, ...), custom_call_target="tpu_custom_call" | custom-call | tf_op jit(solution)/shard_map/pallas_call | solution.py:369
  (7 shorter events, 0.1 us)
Async XLA Ops:
  1.8 9.1 %copy-start = (f32[2,2,256,256]{3,2,1,0:T(8,128)S(1)}, f32[2,2,256,256]{3,2,1,0:T(8,128)}, u32[]{:S(2)}) copy-start(f32[2,2,256,256]{3,2,1,0:T(8,128)} %probe_hbm.1) | copy-start | bytes 3145732
  1.8 9.1 %collective-permute-start.1 = (f32[2,384,128]{2,1,0:T(8,128)S(1)}, f32[2,384,128]{2,1,0:T(8,128)S(1)}, u32[]{:S(2)}, u32[]{:S(2)}) collective-permute-start(f32[2,384,128]{2,1,0:T(8,128)S(1)} %slice.3), channel_id=1, source_target_pairs={{1,0},{2,1},{3,2},{4,3},{5,4},{6,5},{7,6},{8,7},{9,8},{10,9},{11,1... | collective-permute-start | bytes 1179656 | tf_op jit(solution)/shard_map/ppermute | solution.py:385
  5.7 5.2 %copy-start.2 = (f32[2,128,128]{2,1,0:T(8,128)S(1)}, f32[2,128,128]{2,1,0:T(8,128)}, u32[]{:S(2)}) copy-start(f32[2,128,128]{2,1,0:T(8,128)} %constant.44.clone.rows) | copy-start | bytes 393220
  5.7 5.2 %copy-start.3 = (bf16[256,256]{1,0:T(8,128)(2,1)S(1)}, bf16[256,256]{1,0:T(8,128)(2,1)}, u32[]{:S(2)}) copy-start(bf16[256,256]{1,0:T(8,128)(2,1)} %constant.43.clone.low_t) | copy-start | bytes 393220
  5.7 5.2 %copy-start.4 = (bf16[256,256]{1,0:T(8,128)(2,1)S(1)}, bf16[256,256]{1,0:T(8,128)(2,1)}, u32[]{:S(2)}) copy-start(bf16[256,256]{1,0:T(8,128)(2,1)} %constant.42.clone.high_t) | copy-start | bytes 393220
  5.7 5.2 %copy-start.5 = (bf16[256,256]{1,0:T(8,128)(2,1)S(1)}, bf16[256,256]{1,0:T(8,128)(2,1)}, u32[]{:S(2)}) copy-start(bf16[256,256]{1,0:T(8,128)(2,1)} %constant.41.clone.low) | copy-start | bytes 393220
  5.7 5.2 %copy-start.6 = (bf16[256,256]{1,0:T(8,128)(2,1)S(1)}, bf16[256,256]{1,0:T(8,128)(2,1)}, u32[]{:S(2)}) copy-start(bf16[256,256]{1,0:T(8,128)(2,1)} %constant.40.clone.high) | copy-start | bytes 393220
  5.7 5.2 %copy-start.7 = (f32[2,8,128]{2,1,0:T(8,128)S(1)}, f32[2,8,128]{2,1,0:T(8,128)}, u32[]{:S(2)}) copy-start(f32[2,8,128]{2,1,0:T(8,128)} %constant.45.clone.cols) | copy-start | bytes 24580
  10.9 0.7 copy-start.8
  17.0 22.4 %collective-permute-start.2 = (f32[2,384,128]{2,1,0:T(8,128)S(1)}, f32[2,384,128]{2,1,0:T(8,128)S(1)}, u32[]{:S(2)}, u32[]{:S(2)}) collective-permute-start(f32[2,384,128]{2,1,0:T(8,128)S(1)} %get-tuple-element.20.spill), channel_id=1, source_target_pairs={{0,1},{1,2},{2,3},{3,4},{4,5},{5,6},{6,7},{7,8},{8,9},{9,10},{10,1... | collective-permute-start | bytes 1179656 | tf_op jit(solution)/shard_map/ppermute | solution.py:385
  19.0 20.5 %collective-permute-start.3 = (f32[2,320,128]{2,1,0:T(8,128)S(1)}, f32[2,320,128]{2,1,0:T(8,128)S(1)}, u32[]{:S(2)}, u32[]{:S(2)}) collective-permute-start(f32[2,320,128]{2,1,0:T(8,128)S(1)} %get-tuple-element.21.edge), channel_id=1, source_target_pairs={{1,0},{2,1},{3,2},{4,3},{5,4},{6,5},{7,6},{8,7},{9,8},{10,9},{11,1... | collective-permute-start | bytes 983048 | tf_op jit(solution)/shard_map/ppermute | solution.py:385
  24.9 14.6 %collective-permute-start = (s32[2,2]{1,0:T(2,128)S(1)}, s32[2,2]{1,0:T(2,128)S(1)}, u32[]{:S(2)}, u32[]{:S(2)}) collective-permute-start(s32[2,2]{1,0:T(2,128)S(1)} %bitcast.10), channel_id=1, source_target_pairs={{0,32},{32,64},{64,96},{96,128},{128,160},{160,192},{192,224},{224... | collective-permute-start | bytes 56 | tf_op jit(solution)/shard_map/ppermute | solution.py:385
  34.0 23.3 %collective-permute-start.4 = (f32[2,128,128]{2,1,0:T(8,128)S(1)}, f32[2,128,128]{2,1,0:T(8,128)S(1)}, u32[]{:S(2)}, u32[]{:S(2)}) collective-permute-start(f32[2,128,128]{2,1,0:T(8,128)S(1)} %get-tuple-element.24), channel_id=1, source_target_pairs={{32,0},{64,32},{96,64},{128,96},{160,128},{192,160},{224,192},{256... | collective-permute-start | bytes 393224 | tf_op jit(solution)/shard_map/ppermute | solution.py:385
  40.1 22.7 %collective-permute-start.5 = (f32[2,128,128]{2,1,0:T(8,128)S(1)}, f32[2,128,128]{2,1,0:T(8,128)S(1)}, u32[]{:S(2)}, u32[]{:S(2)}) collective-permute-start(f32[2,128,128]{2,1,0:T(8,128)S(1)} %shard_map.116), channel_id=1, source_target_pairs={{32,0},{64,32},{96,64},{128,96},{160,128},{192,160},{224,192},{256... | collective-permute-start | bytes 393224 | tf_op jit(solution)/shard_map/ppermute | solution.py:385
  68.4 3.8 %collective-permute-start.8 = (f32[2,256,256]{2,1,0:T(8,128)S(1)}, f32[2,256,256]{2,1,0:T(8,128)S(1)}, u32[]{:S(2)}, u32[]{:S(2)}) collective-permute-start(f32[2,256,256]{2,1,0:T(8,128)S(1)} %get-tuple-element.31), channel_id=1, source_target_pairs={{0,1},{1,0},{2,3},{3,2},{4,5},{5,4},{6,7},{7,6},{8,9},{9,8},{10,11... | collective-permute-start | bytes 1572872 | tf_op jit(solution)/shard_map/ppermute | solution.py:393
  119.8 13.6 %all-to-all-start.3 = ((f32[16,32,256]{2,1,0:T(8,128)}), f32[16,32,256]{2,1,0:T(8,128)S(1)}, u32[]{:S(2)}, u32[]{:S(2)}) async-start(f32[16,32,256]{2,1,0:T(8,128)} %broadcast_in_dim.11), calls=%async_computation.3 | async-start | bytes 1048576 | tf_op jit(solution)/shard_map/all_to_all | solution.py:389
  126.8 38.5 %copy-start.1 = (f32[2,384,256]{2,1,0:T(8,128)S(1)}, f32[2,384,256]{2,1,0:T(8,128)}, u32[]{:S(2)}) copy-start(f32[2,384,256]{2,1,0:T(8,128)} %get-tuple-element.22.whole) | copy-start | bytes 2359300
  126.8 26.7 %collective-permute-start.6 = (f32[2,128,256]{2,1,0:T(8,128)S(1)}, f32[2,128,256]{2,1,0:T(8,128)S(1)}, u32[]{:S(2)}, u32[]{:S(2)}) collective-permute-start(f32[2,128,256]{2,1,0:T(8,128)S(1)} %get-tuple-element.28), channel_id=1, source_target_pairs={{0,32},{32,64},{64,96},{96,128},{128,160},{160,192},{192,224},{224... | collective-permute-start | bytes 786440 | tf_op jit(solution)/shard_map/ppermute | solution.py:385
  133.4 31.9 %collective-permute-start.9 = (f32[2,256,256]{2,1,0:T(8,128)S(1)}, f32[2,256,256]{2,1,0:T(8,128)S(1)}, u32[]{:S(2)}, u32[]{:S(2)}) collective-permute-start(f32[2,256,256]{2,1,0:T(8,128)S(1)} %bitcast.7), channel_id=1, source_target_pairs={{0,1},{1,0},{2,3},{3,2},{4,5},{5,4},{6,7},{7,6},{8,9},{9,8},{10,11... | collective-permute-start | bytes 1572872 | tf_op jit(solution)/shard_map/ppermute | solution.py:393
  154.1 11.2 %collective-permute-start.7 = (f32[2,384,128]{2,1,0:T(8,128)S(1)}, f32[2,384,128]{2,1,0:T(8,128)S(1)}, u32[]{:S(2)}, u32[]{:S(2)}) collective-permute-start(f32[2,384,128]{2,1,0:T(8,128)S(1)} %shard_map.119), channel_id=1, source_target_pairs={{0,1},{1,2},{2,3},{3,4},{4,5},{5,6},{6,7},{7,8},{8,9},{9,10},{10,1... | collective-permute-start | bytes 1179656 | tf_op jit(solution)/shard_map/ppermute | solution.py:385

commit v9 on v8

--- a/solution.py
+++ b/solution.py
@@ -326,24 +326,23 @@
         new_spill[k, HALO:] = own_grad[k, :, WIN:]
 
 
-def last_kernel(above, info, whole, own_grad, from_above, from_left, own, other, object_hbm, probe_hbm, out, sems):
-    core = info[1]
-    own_copy = pltpu.make_async_copy(own, probe_hbm.at[core], sems.at[0])
-    other_copy = pltpu.make_async_copy(other, probe_hbm.at[1 - core], sems.at[1])
-    object_copy = lambda k: pltpu.make_async_copy(out.at[k], object_hbm.at[k], sems.at[2 + k])
-    own_copy.start()
-    other_copy.start()
+def object_kernel(above, whole, own_grad, from_above, from_left, out):
     for k in range(2):
         fell = jnp.where(lanes() >= above[1, 1], from_above[k, :, :HALO], 0.0)
         out[k, :LAST, :HALO] = whole[k, :LAST, :HALO] + fell + from_left[k, :LAST]
         out[k, :LAST, HALO:] = whole[k, :LAST, HALO:] + from_above[k, :, HALO:]
         out[k, LAST:, :HALO] = whole[k, LAST:, :HALO] + own_grad[k, :, :HALO] + from_left[k, LAST:]
         out[k, LAST:, HALO:] = whole[k, LAST:, HALO:] + own_grad[k, :, HALO:WIN]
-        object_copy(k).start()
+
+
+def last_kernel(info, own, other, probe_hbm, sems):
+    core = info[1]
+    own_copy = pltpu.make_async_copy(own, probe_hbm.at[core], sems.at[0])
+    other_copy = pltpu.make_async_copy(other, probe_hbm.at[1 - core], sems.at[1])
+    own_copy.start()
+    other_copy.start()
     own_copy.wait()
     other_copy.wait()
-    for k in range(2):
-        object_copy(k).wait()
 
 
 HBM = object()
@@ -444,9 +443,9 @@
     from_above = passed_along(downward, ROW, 1)
     (spill,) = call(spill_kernel, [side], [], [above], [grad, from_above])
     from_left = passed_along(spill, COL, 1)
-    object_out, probe_out = call(
-        last_kernel, [(tile, HBM), (probe_shape, HBM)], [tile], [above, info],
-        [(whole, AUTO), grad, from_above, from_left, own, other], copies=4)
+    (object_out,) = call(
+        object_kernel, [(tile, AUTO)], [], [above], [(whole, AUTO), (grad, AUTO), (from_above, AUTO), (from_left, AUTO)])
+    (probe_out,) = call(last_kernel, [(probe_shape, HBM)], [], [info], [own, other], copies=2)
     return (object_out, probe_out)
 
 

time: 168 us -> 169 us (level)
    pallas_call x8 -> x9, Pallas kernels: 19.1 us -> 20.4 us  [call(): pl.pallas_call(kernel, out_shape=shapes, in_specs=[smem] * len(scalars) +...]
  transfers between devices with their start and end apart: 11 -> 11, of which waited for: 7 -> 7; matrix products, arithmetic and copies ran while one was open for 0% -> 0% of each run, Pallas kernels for 4% -> 5%
where the time goes in v9:
time: 169 us; the launch traced here: 168 us
  starting transfers between devices  48.9 us (29%)
  waiting for transfers between devices  48.7 us (29%)
  blocking collectives  46.5 us (28%)
  Pallas kernels  20.4 us (12%)
  local copies, waits for them, and re-layouts  2.69 us (2%)
    all_to_all x3, blocking collectives, exchanged(): return lax.all_to_all(parts, axes, 0, 0, tiled=False)  46.5 us
    ppermute x8, waiting for transfers between devices, passed_along(): return lax.ppermute(block, axis, route)  43.3 us
    ppermute x8, starting transfers between devices, passed_along(): return lax.ppermute(block, axis, route)  39 us
    pallas_call x9, Pallas kernels, call(): pl.pallas_call(kernel, out_shape=shapes, in_specs=[smem] * len(scalars) +...  20.4 us
    all_to_all x1, starting transfers between devices, exchanged(): return lax.all_to_all(parts, axes, 0, 0, tiled=False)  6.09 us
    ppermute x2, starting transfers between devices, swapped(): return lax.ppermute(block, CORE, [(0, 1), (1, 0)])  3.83 us
    all_to_all x1, waiting for transfers between devices, exchanged(): return lax.all_to_all(parts, axes, 0, 0, tiled=False)  3.48 us
  transfers between devices with their start and end apart: 11, of which 7 were waited for; matrix products, arithmetic and copies ran while one was open for 0% of the time, Pallas kernels for 5%

profile of v9, /device:TPU:48, one launch (start us, length us, event | category | flops | bytes accessed | tf_op | source)
XLA Modules:
  0.0 168.4 jit_solution(11820942131792077023)
XLA Ops:
  0.6 1.1 copy.17.obj
  1.8 0.0 copy-start
  1.8 3.8 %collective-permute-start.1 = (f32[2,384,128]{2,1,0:T(8,128)S(1)}, f32[2,384,128]{2,1,0:T(8,128)S(1)}, u32[]{:S(2)}, u32[]{:S(2)}) collective-permute-start(f32[2,384,128]{2,1,0:T(8,128)S(1)} %slice.3), channel_id=1, source_target_pairs={{1,0},{2,1},{3,2},{4,3},{5,4},{6,5},{7,6},{8,7},{9,8},{10,9},{11,1... | collective-permute-start | bytes 1179656 | tf_op jit(solution)/shard_map/ppermute | solution.py:384
  5.6 0.1 pad_add_fusion.refs_0_.info
  5.7 0.0 copy-start.2
  5.7 0.0 copy-start.3
  5.7 0.0 copy-start.4
  5.7 0.0 copy-start.5
  5.7 0.0 copy-start.6
  5.7 0.0 copy-start.7
  5.7 2.7 %shard_map.113 = (f32[2,256,256]{2,1,0:T(8,128)}, f32[8,128]{1,0:T(8,128)S(1)}, f32[32,256]{1,0:T(8,128)S(1)}) custom-call(s32[3]{0:T(128)S(1)} %pad_add_fusion.refs_0_.info, f32[2,2,256,256]{3,2,1,0:T(8,128)} %probe_hbm.1, bf16[2,256,256]{2,1,0:T(8,128)(2,1)} %bitcast.14), custom_call_target="tpu_custom_call" | custom-call | tf_op jit(solution)/shard_map/pallas_call | solution.py:368
  8.4 2.5 %collective-permute-done.1.halo = f32[2,384,128]{2,1,0:T(8,128)S(1)} collective-permute-done((f32[2,384,128]{2,1,0:T(8,128)S(1)}, f32[2,384,128]{2,1,0:T(8,128)S(1)}, u32[]{:S(2)}, u32[]{:S(2)}) %collective-permute-start.1) | collective-permute-done | bytes 393248 | tf_op jit(solution)/shard_map/ppermute | solution.py:384
  10.9 0.0 copy-start.8
  10.9 0.0 copy-done
  10.9 0.0 copy-done.2
  10.9 0.0 copy-done.3
  10.9 0.0 copy-done.4
  10.9 0.0 copy-done.5
  10.9 0.0 copy-done.6
  10.9 0.0 copy-done.7
  10.9 0.6 copy-done.8
  11.5 5.5 %shard_map.114 = (f32[2,384,256]{2,1,0:T(8,128)S(1)}, f32[2,384,128]{2,1,0:T(8,128)S(1)}, f32[2,320,128]{2,1,0:T(8,128)S(1)}, f32[2,128,128]{2,1,0:T(8,128)S(1)}, f32[2,2,256,256]{3,2,1,0:T(8,128)}) custom-call(s32[2,2]{1,0:T(2,128)S(1)} %bitcast.9, f32[2,384,256]{2,1,0:T(8,128)S(1)} %copy.17.obj, ...), custom_call_target="tpu_custom_call", output_to_operand_aliasing={{0}: (1, {}), {1}: (2, {})} | custom-call | tf_op jit(solution)/shard_map/pallas_call | solution.py:368
  17.0 2.0 %collective-permute-start.2 = (f32[2,384,128]{2,1,0:T(8,128)S(1)}, f32[2,384,128]{2,1,0:T(8,128)S(1)}, u32[]{:S(2)}, u32[]{:S(2)}) collective-permute-start(f32[2,384,128]{2,1,0:T(8,128)S(1)} %get-tuple-element.20.spill), channel_id=1, source_target_pairs={{0,1},{1,2},{2,3},{3,4},{4,5},{5,6},{6,7},{7,8},{8,9},{9,10},{10,1... | collective-permute-start | bytes 1179656 | tf_op jit(solution)/shard_map/ppermute | solution.py:384
  19.0 5.9 %collective-permute-start.3 = (f32[2,320,128]{2,1,0:T(8,128)S(1)}, f32[2,320,128]{2,1,0:T(8,128)S(1)}, u32[]{:S(2)}, u32[]{:S(2)}) collective-permute-start(f32[2,320,128]{2,1,0:T(8,128)S(1)} %get-tuple-element.21.edge), channel_id=1, source_target_pairs={{1,0},{2,1},{3,2},{4,3},{5,4},{6,5},{7,6},{8,7},{9,8},{10,9},{11,1... | collective-permute-start | bytes 983048 | tf_op jit(solution)/shard_map/ppermute | solution.py:384
  24.9 9.1 %collective-permute-start = (s32[2,2]{1,0:T(2,128)S(1)}, s32[2,2]{1,0:T(2,128)S(1)}, u32[]{:S(2)}, u32[]{:S(2)}) collective-permute-start(s32[2,2]{1,0:T(2,128)S(1)} %bitcast.10), channel_id=1, source_target_pairs={{0,32},{32,64},{64,96},{96,128},{128,160},{160,192},{192,224},{224... | collective-permute-start | bytes 56 | tf_op jit(solution)/shard_map/ppermute | solution.py:384
  34.0 5.4 %collective-permute-start.4 = (f32[2,128,128]{2,1,0:T(8,128)S(1)}, f32[2,128,128]{2,1,0:T(8,128)S(1)}, u32[]{:S(2)}, u32[]{:S(2)}) collective-permute-start(f32[2,128,128]{2,1,0:T(8,128)S(1)} %get-tuple-element.24), channel_id=1, source_target_pairs={{32,0},{64,32},{96,64},{128,96},{160,128},{192,160},{224,192},{256... | collective-permute-start | bytes 393224 | tf_op jit(solution)/shard_map/ppermute | solution.py:384
  39.4 0.0 collective-permute-done.above
  39.4 0.0 collective-permute-done.3.from_right
  39.4 0.0 collective-permute-done.2.from_left
  39.5 0.6 shard_map.116
  40.1 7.8 %collective-permute-start.5 = (f32[2,128,128]{2,1,0:T(8,128)S(1)}, f32[2,128,128]{2,1,0:T(8,128)S(1)}, u32[]{:S(2)}, u32[]{:S(2)}) collective-permute-start(f32[2,128,128]{2,1,0:T(8,128)S(1)} %shard_map.116), channel_id=1, source_target_pairs={{32,0},{64,32},{96,64},{128,96},{160,128},{192,160},{224,192},{256... | collective-permute-start | bytes 393224 | tf_op jit(solution)/shard_map/ppermute | solution.py:384
  47.9 1.5 shard_map.115
  49.4 7.9 %collective-permute-done.4.below_mid = f32[2,128,128]{2,1,0:T(8,128)S(1)} collective-permute-done((f32[2,128,128]{2,1,0:T(8,128)S(1)}, f32[2,128,128]{2,1,0:T(8,128)S(1)}, u32[]{:S(2)}, u32[]{:S(2)}) %collective-permute-start.4) | collective-permute-done | bytes 131104 | tf_op jit(solution)/shard_map/ppermute | solution.py:384
  57.2 5.5 %collective-permute-done.5.below_rest = f32[2,128,128]{2,1,0:T(8,128)S(1)} collective-permute-done((f32[2,128,128]{2,1,0:T(8,128)S(1)}, f32[2,128,128]{2,1,0:T(8,128)S(1)}, u32[]{:S(2)}, u32[]{:S(2)}) %collective-permute-start.5) | collective-permute-done | bytes 131104 | tf_op jit(solution)/shard_map/ppermute | solution.py:384
  62.8 5.6 %shard_map.117 = (f32[2,256,256]{2,1,0:T(8,128)S(1)}, f32[2,256,256]{2,1,0:T(8,128)S(1)}, f32[2,256,256]{2,1,0:T(8,128)S(1)}) custom-call(s32[2,2]{1,0:T(2,128)S(1)} %bitcast.11, s32[3]{0:T(128)S(1)} %pad_add_fusion.refs_0_.info, f32[2,256,384]{2,1,0:T(8,128)S(1)} %get-tuple-element.23.source, f32[2,128,128]{2,1,0:T(8,128)S(1)} %collective-permute-done.4.below_mid, ...), custom_call_target="tpu_custom_call" | custom-call | tf_op jit(solution)/shard_map/pallas_call | solution.py:368
  68.4 1.9 %collective-permute-start.8 = (f32[2,256,256]{2,1,0:T(8,128)S(1)}, f32[2,256,256]{2,1,0:T(8,128)S(1)}, u32[]{:S(2)}, u32[]{:S(2)}) collective-permute-start(f32[2,256,256]{2,1,0:T(8,128)S(1)} %get-tuple-element.31), channel_id=1, source_target_pairs={{0,1},{1,0},{2,3},{3,2},{4,5},{5,4},{6,7},{7,6},{8,9},{9,8},{10,11... | collective-permute-start | bytes 1572872 | tf_op jit(solution)/shard_map/ppermute | solution.py:392
  70.3 1.9 %collective-permute-done.8 = f32[2,256,256]{2,1,0:T(8,128)S(1)} collective-permute-done((f32[2,256,256]{2,1,0:T(8,128)S(1)}, f32[2,256,256]{2,1,0:T(8,128)S(1)}, u32[]{:S(2)}, u32[]{:S(2)}) %collective-permute-start.8) | collective-permute-done | bytes 524320 | tf_op jit(solution)/shard_map/ppermute | solution.py:392
  72.2 0.1 add.18
  72.3 13.9 %all_to_all.20 = f32[16,32,256]{2,1,0:T(8,128)S(1)} all-to-all(f32[16,32,256]{2,1,0:T(8,128)S(1)} %bitcast.13), channel_id=1, replica_groups=mesh['row_0'=4,'row_1'=4,'col_0'=4,'col_1'=4,'col_2'=2] {'row_0','col_1'}, dimensions={0} | all-to-all | bytes 1048576 | tf_op jit(solution)/shard_map/all_to_all | solution.py:388
  86.2 10.7 %all_to_all.21 = f32[4,32,256]{2,1,0:T(8,128)S(1)} all-to-all(f32[4,32,256]{2,1,0:T(8,128)S(1)} %broadcast_in_dim.9), channel_id=1, replica_groups=mesh['row_0'=4,'row_1'=4,'col_0'=4,'col_1'=4,'col_2'=2] {'col_0'}, dimensions={0} | all-to-all | bytes 262144 | tf_op jit(solution)/shard_map/all_to_all | solution.py:388
  97.0 22.0 %all_to_all.22 = f32[4,32,256]{2,1,0:T(8,128)S(1)} all-to-all(f32[4,32,256]{2,1,0:T(8,128)S(1)} %broadcast_in_dim.10), channel_id=1, replica_groups=mesh['row_0'=4,'row_1'=4,'col_0'=4,'col_1'=4,'col_2'=2] {'row_1'}, dimensions={0} | all-to-all | bytes 262144 | tf_op jit(solution)/shard_map/all_to_all | solution.py:388
  118.9 0.8 broadcast_in_dim.11
  119.8 6.1 %all-to-all-start.3 = ((f32[16,32,256]{2,1,0:T(8,128)}), f32[16,32,256]{2,1,0:T(8,128)S(1)}, u32[]{:S(2)}, u32[]{:S(2)}) async-start(f32[16,32,256]{2,1,0:T(8,128)} %broadcast_in_dim.11), calls=%async_computation.3 | async-start | bytes 1048576 | tf_op jit(solution)/shard_map/all_to_all | solution.py:388
  125.9 0.9 shard_map.118
  126.8 0.0 copy-start.1
  126.8 3.1 %collective-permute-start.6 = (f32[2,128,256]{2,1,0:T(8,128)S(1)}, f32[2,128,256]{2,1,0:T(8,128)S(1)}, u32[]{:S(2)}, u32[]{:S(2)}) collective-permute-start(f32[2,128,256]{2,1,0:T(8,128)S(1)} %get-tuple-element.28), channel_id=1, source_target_pairs={{0,32},{32,64},{64,96},{96,128},{128,160},{160,192},{192,224},{224... | collective-permute-start | bytes 786440 | tf_op jit(solution)/shard_map/ppermute | solution.py:384
  129.9 3.5 %all-to-all-done.3 = f32[16,32,256]{2,1,0:T(8,128)S(1)} async-done(((f32[16,32,256]{2,1,0:T(8,128)}), f32[16,32,256]{2,1,0:T(8,128)S(1)}, u32[]{:S(2)}, u32[]{:S(2)}) %all-to-all-start.3) | async-done | bytes 524320 | tf_op jit(solution)/shard_map/all_to_all | solution.py:388
  133.4 1.9 %collective-permute-start.9 = (f32[2,256,256]{2,1,0:T(8,128)S(1)}, f32[2,256,256]{2,1,0:T(8,128)S(1)}, u32[]{:S(2)}, u32[]{:S(2)}) collective-permute-start(f32[2,256,256]{2,1,0:T(8,128)S(1)} %bitcast.7), channel_id=1, source_target_pairs={{0,1},{1,0},{2,3},{3,2},{4,5},{5,4},{6,7},{7,6},{8,9},{9,8},{10,11... | collective-permute-start | bytes 1572872 | tf_op jit(solution)/shard_map/ppermute | solution.py:392
  135.3 18.1 %collective-permute-done.6.from_above = f32[2,128,256]{2,1,0:T(8,128)S(1)} collective-permute-done((f32[2,128,256]{2,1,0:T(8,128)S(1)}, f32[2,128,256]{2,1,0:T(8,128)S(1)}, u32[]{:S(2)}, u32[]{:S(2)}) %collective-permute-start.6) | collective-permute-done | bytes 262176 | tf_op jit(solution)/shard_map/ppermute | solution.py:384
  153.5 0.6 shard_map.119
  154.1 1.9 %collective-permute-start.7 = (f32[2,384,128]{2,1,0:T(8,128)S(1)}, f32[2,384,128]{2,1,0:T(8,128)S(1)}, u32[]{:S(2)}, u32[]{:S(2)}) collective-permute-start(f32[2,384,128]{2,1,0:T(8,128)S(1)} %shard_map.119), channel_id=1, source_target_pairs={{0,1},{1,2},{2,3},{3,4},{4,5},{5,6},{6,7},{7,8},{8,9},{9,10},{10,1... | collective-permute-start | bytes 1179656 | tf_op jit(solution)/shard_map/ppermute | solution.py:384
  156.0 9.3 %collective-permute-done.7.from_left = f32[2,384,128]{2,1,0:T(8,128)S(1)} collective-permute-done((f32[2,384,128]{2,1,0:T(8,128)S(1)}, f32[2,384,128]{2,1,0:T(8,128)S(1)}, u32[]{:S(2)}, u32[]{:S(2)}) %collective-permute-start.7) | collective-permute-done | bytes 393248 | tf_op jit(solution)/shard_map/ppermute | solution.py:384
  165.3 0.0 copy-done.1
  165.3 1.5 shard_map.120
  166.8 0.0 collective-permute-done.9.other
  166.8 1.5 shard_map.121
  (7 shorter events, 0.1 us)
Async XLA Ops:
  1.8 9.1 %copy-start = (f32[2,2,256,256]{3,2,1,0:T(8,128)S(1)}, f32[2,2,256,256]{3,2,1,0:T(8,128)}, u32[]{:S(2)}) copy-start(f32[2,2,256,256]{3,2,1,0:T(8,128)} %probe_hbm.1) | copy-start | bytes 3145732
  1.8 9.1 %collective-permute-start.1 = (f32[2,384,128]{2,1,0:T(8,128)S(1)}, f32[2,384,128]{2,1,0:T(8,128)S(1)}, u32[]{:S(2)}, u32[]{:S(2)}) collective-permute-start(f32[2,384,128]{2,1,0:T(8,128)S(1)} %slice.3), channel_id=1, source_target_pairs={{1,0},{2,1},{3,2},{4,3},{5,4},{6,5},{7,6},{8,7},{9,8},{10,9},{11,1... | collective-permute-start | bytes 1179656 | tf_op jit(solution)/shard_map/ppermute | solution.py:384
  5.7 5.2 %copy-start.2 = (f32[2,128,128]{2,1,0:T(8,128)S(1)}, f32[2,128,128]{2,1,0:T(8,128)}, u32[]{:S(2)}) copy-start(f32[2,128,128]{2,1,0:T(8,128)} %constant.44.clone.rows) | copy-start | bytes 393220
  5.7 5.2 %copy-start.3 = (bf16[256,256]{1,0:T(8,128)(2,1)S(1)}, bf16[256,256]{1,0:T(8,128)(2,1)}, u32[]{:S(2)}) copy-start(bf16[256,256]{1,0:T(8,128)(2,1)} %constant.43.clone.low_t) | copy-start | bytes 393220
  5.7 5.2 %copy-start.4 = (bf16[256,256]{1,0:T(8,128)(2,1)S(1)}, bf16[256,256]{1,0:T(8,128)(2,1)}, u32[]{:S(2)}) copy-start(bf16[256,256]{1,0:T(8,128)(2,1)} %constant.42.clone.high_t) | copy-start | bytes 393220
  5.7 5.2 %copy-start.5 = (bf16[256,256]{1,0:T(8,128)(2,1)S(1)}, bf16[256,256]{1,0:T(8,128)(2,1)}, u32[]{:S(2)}) copy-start(bf16[256,256]{1,0:T(8,128)(2,1)} %constant.41.clone.low) | copy-start | bytes 393220
  5.7 5.2 %copy-start.6 = (bf16[256,256]{1,0:T(8,128)(2,1)S(1)}, bf16[256,256]{1,0:T(8,128)(2,1)}, u32[]{:S(2)}) copy-start(bf16[256,256]{1,0:T(8,128)(2,1)} %constant.40.clone.high) | copy-start | bytes 393220
  5.7 5.2 %copy-start.7 = (f32[2,8,128]{2,1,0:T(8,128)S(1)}, f32[2,8,128]{2,1,0:T(8,128)}, u32[]{:S(2)}) copy-start(f32[2,8,128]{2,1,0:T(8,128)} %constant.45.clone.cols) | copy-start | bytes 24580
  10.9 0.7 copy-start.8
  17.0 22.4 %collective-permute-start.2 = (f32[2,384,128]{2,1,0:T(8,128)S(1)}, f32[2,384,128]{2,1,0:T(8,128)S(1)}, u32[]{:S(2)}, u32[]{:S(2)}) collective-permute-start(f32[2,384,128]{2,1,0:T(8,128)S(1)} %get-tuple-element.20.spill), channel_id=1, source_target_pairs={{0,1},{1,2},{2,3},{3,4},{4,5},{5,6},{6,7},{7,8},{8,9},{9,10},{10,1... | collective-permute-start | bytes 1179656 | tf_op jit(solution)/shard_map/ppermute | solution.py:384
  19.0 20.5 %collective-permute-start.3 = (f32[2,320,128]{2,1,0:T(8,128)S(1)}, f32[2,320,128]{2,1,0:T(8,128)S(1)}, u32[]{:S(2)}, u32[]{:S(2)}) collective-permute-start(f32[2,320,128]{2,1,0:T(8,128)S(1)} %get-tuple-element.21.edge), channel_id=1, source_target_pairs={{1,0},{2,1},{3,2},{4,3},{5,4},{6,5},{7,6},{8,7},{9,8},{10,9},{11,1... | collective-permute-start | bytes 983048 | tf_op jit(solution)/shard_map/ppermute | solution.py:384
  24.9 14.6 %collective-permute-start = (s32[2,2]{1,0:T(2,128)S(1)}, s32[2,2]{1,0:T(2,128)S(1)}, u32[]{:S(2)}, u32[]{:S(2)}) collective-permute-start(s32[2,2]{1,0:T(2,128)S(1)} %bitcast.10), channel_id=1, source_target_pairs={{0,32},{32,64},{64,96},{96,128},{128,160},{160,192},{192,224},{224... | collective-permute-start | bytes 56 | tf_op jit(solution)/shard_map/ppermute | solution.py:384
  34.0 23.3 %collective-permute-start.4 = (f32[2,128,128]{2,1,0:T(8,128)S(1)}, f32[2,128,128]{2,1,0:T(8,128)S(1)}, u32[]{:S(2)}, u32[]{:S(2)}) collective-permute-start(f32[2,128,128]{2,1,0:T(8,128)S(1)} %get-tuple-element.24), channel_id=1, source_target_pairs={{32,0},{64,32},{96,64},{128,96},{160,128},{192,160},{224,192},{256... | collective-permute-start | bytes 393224 | tf_op jit(solution)/shard_map/ppermute | solution.py:384
  40.1 22.7 %collective-permute-start.5 = (f32[2,128,128]{2,1,0:T(8,128)S(1)}, f32[2,128,128]{2,1,0:T(8,128)S(1)}, u32[]{:S(2)}, u32[]{:S(2)}) collective-permute-start(f32[2,128,128]{2,1,0:T(8,128)S(1)} %shard_map.116), channel_id=1, source_target_pairs={{32,0},{64,32},{96,64},{128,96},{160,128},{192,160},{224,192},{256... | collective-permute-start | bytes 393224 | tf_op jit(solution)/shard_map/ppermute | solution.py:384
  68.4 3.8 %collective-permute-start.8 = (f32[2,256,256]{2,1,0:T(8,128)S(1)}, f32[2,256,256]{2,1,0:T(8,128)S(1)}, u32[]{:S(2)}, u32[]{:S(2)}) collective-permute-start(f32[2,256,256]{2,1,0:T(8,128)S(1)} %get-tuple-element.31), channel_id=1, source_target_pairs={{0,1},{1,0},{2,3},{3,2},{4,5},{5,4},{6,7},{7,6},{8,9},{9,8},{10,11... | collective-permute-start | bytes 1572872 | tf_op jit(solution)/shard_map/ppermute | solution.py:392
  119.8 13.6 %all-to-all-start.3 = ((f32[16,32,256]{2,1,0:T(8,128)}), f32[16,32,256]{2,1,0:T(8,128)S(1)}, u32[]{:S(2)}, u32[]{:S(2)}) async-start(f32[16,32,256]{2,1,0:T(8,128)} %broadcast_in_dim.11), calls=%async_computation.3 | async-start | bytes 1048576 | tf_op jit(solution)/shard_map/all_to_all | solution.py:388
  126.8 38.5 %copy-start.1 = (f32[2,384,256]{2,1,0:T(8,128)S(1)}, f32[2,384,256]{2,1,0:T(8,128)}, u32[]{:S(2)}) copy-start(f32[2,384,256]{2,1,0:T(8,128)} %get-tuple-element.22.whole) | copy-start | bytes 2359300
  126.8 26.7 %collective-permute-start.6 = (f32[2,128,256]{2,1,0:T(8,128)S(1)}, f32[2,128,256]{2,1,0:T(8,128)S(1)}, u32[]{:S(2)}, u32[]{:S(2)}) collective-permute-start(f32[2,128,256]{2,1,0:T(8,128)S(1)} %get-tuple-element.28), channel_id=1, source_target_pairs={{0,32},{32,64},{64,96},{96,128},{128,160},{160,192},{192,224},{224... | collective-permute-start | bytes 786440 | tf_op jit(solution)/shard_map/ppermute | solution.py:384
  133.4 33.4 %collective-permute-start.9 = (f32[2,256,256]{2,1,0:T(8,128)S(1)}, f32[2,256,256]{2,1,0:T(8,128)S(1)}, u32[]{:S(2)}, u32[]{:S(2)}) collective-permute-start(f32[2,256,256]{2,1,0:T(8,128)S(1)} %bitcast.7), channel_id=1, source_target_pairs={{0,1},{1,0},{2,3},{3,2},{4,5},{5,4},{6,7},{7,6},{8,9},{9,8},{10,11... | collective-permute-start | bytes 1572872 | tf_op jit(solution)/shard_map/ppermute | solution.py:392
  154.1 11.2 %collective-permute-start.7 = (f32[2,384,128]{2,1,0:T(8,128)S(1)}, f32[2,384,128]{2,1,0:T(8,128)S(1)}, u32[]{:S(2)}, u32[]{:S(2)}) collective-permute-start(f32[2,384,128]{2,1,0:T(8,128)S(1)} %shard_map.119), channel_id=1, source_target_pairs={{0,1},{1,2},{2,3},{3,4},{4,5},{5,6},{6,7},{7,8},{8,9},{9,10},{10,1... | collective-permute-start | bytes 1179656 | tf_op jit(solution)/shard_map/ppermute | solution.py:384
